TPU v7x, 32 devices: a whole 2x2x4 slice. The times are simulated.
32 devices in a mesh: dp: 32 (over z, y, x, core).
Axes of the slice: x: 2, y: 2, z: 4, core: 2. Of those that a mesh axis runs over, the one named last changes fastest.
Arguments:
- block_in: bfloat16 [4096, 1024], P('dp'), may hold values from -6 to 6
- grad_out: bfloat16 [4096, 1024], P('dp'), may hold values from -6 to 6
- w_qkv: bfloat16 [1024, 3072], P('dp')
- b_qkv: bfloat16 [3072], P('dp'), may hold values from -3 to 3
- w_o: bfloat16 [1024, 1024], P('dp'), may hold values from -1 to 1
- b_o: bfloat16 [1024], P('dp'), may hold values from -2 to 2
- w_in: bfloat16 [1024, 4096], P('dp'), may hold values from -0.1875 to 0.1875
- b_in: bfloat16 [4096], P('dp'), may hold values from -3 to 3
- w_out: bfloat16 [4096, 1024], P('dp'), may hold values from -0.09375 to 0.09375
- b_out: bfloat16 [1024], P('dp'), may hold values from -2 to 2
- ln1_gain: bfloat16 [1024], P('dp'), may hold values from 0.25 to 1.75
- ln1_shift: bfloat16 [1024], P('dp'), may hold values from -2 to 2
- ln2_gain: bfloat16 [1024], P('dp'), may hold values from 0.25 to 1.75
- ln2_shift: bfloat16 [1024], P('dp'), may hold values from -2 to 2
- seq_lens: int32 [96], replicated, may hold values from 0 to 128, as said below
- seq_device: int32 [96], replicated, may hold values from 0 to 31, as said below
- seq_offset: int32 [96], replicated, may hold values from 0 to 128, as said below
Outputs:
- block_out: bfloat16 [4096, 1024], P('dp')
- grad_input: bfloat16 [4096, 1024], P('dp')
- grad_w_qkv: float32 [1024, 3072], P('dp')
- grad_b_qkv: float32 [3072], P('dp')
- grad_w_o: float32 [1024, 1024], P('dp')
- grad_b_o: float32 [1024], P('dp')
- grad_w_in: float32 [1024, 4096], P('dp')
- grad_b_in: float32 [4096], P('dp')
- grad_w_out: float32 [4096, 1024], P('dp')
- grad_b_out: float32 [1024], P('dp')
- grad_ln1_gain: float32 [1024], P('dp')
- grad_ln1_shift: float32 [1024], P('dp')
- grad_ln2_gain: float32 [1024], P('dp')
- grad_ln2_shift: float32 [1024], P('dp')
Inputs may be any that keep to these rules, and one draw needn't show every extreme that they name: `seq_lens`: the entries of one device have lengths summing to at most 128; some device holds one entry of exactly 128 tokens; a length of 0 marks an unused entry. `seq_device`: every device holds exactly 3 entries. `seq_offset`: the entries of one device take disjoint runs of slots that start at slot 0 and follow one another without gaps.
All inputs are finite; a program needn't handle non-finite values.
Results may differ from a plain program's by a relative error of at most 0.0087.
Values may be sent and summed in bfloat16 or wider, within the bound.
No kernel may reach another device: no remote copies, remote signals or barrier semaphores. Data moves between devices by JAX's collectives and lax.ppermute only.
A program may use at most 192 MiB of HBM per device.

v0:
```python
import math

import jax
import jax.numpy as jnp
from jax import lax
from jax.experimental import pallas as pl
from jax.experimental.pallas import tpu as pltpu
from jax.sharding import PartitionSpec as P


D = 1024
HEAD = 64
ROT = 16
NB = 4
QB = D // NB
NEG = -1e30

F32 = jnp.float32
BF = jnp.bfloat16
I32 = jnp.int32


def dot_nn(left, right):
    return jnp.dot(left, right, preferred_element_type=F32)


def dot_nt(left, right):
    return lax.dot_general(left, right, (((1,), (1,)), ((), ())), preferred_element_type=F32)


def iota(shape, axis):
    return lax.broadcasted_iota(I32, shape, axis)


def call(body, ins, outs, scratch=(), flops=0, extra=4 << 20, hbm=()):
    spaces = {"v": pltpu.VMEM, "s": pltpu.SMEM, "a": pl.ANY}
    arrays = [a for _, a in ins]
    nbytes = sum(a.size * a.dtype.itemsize for a in arrays) + sum(math.prod(o.shape) * o.dtype.itemsize for o in outs)
    room = sum(math.prod(t.shape) * jnp.dtype(t.dtype).itemsize for t in scratch if t.memory_space == pltpu.VMEM)
    room += sum(a.size * a.dtype.itemsize for s, a in ins if s == "v") + sum(math.prod(o.shape) * o.dtype.itemsize for i, o in enumerate(outs) if i not in hbm)
    return pl.pallas_call(
        body,
        out_shape=tuple(outs),
        in_specs=[pl.BlockSpec(memory_space=spaces[s]) for s, _ in ins],
        out_specs=tuple(pl.BlockSpec(memory_space=pltpu.HBM if i in hbm else pltpu.VMEM) for i in range(len(outs))),
        scratch_shapes=list(scratch),
        compiler_params=pltpu.CompilerParams(vmem_limit_bytes=int(room * 1.02) + extra),
        cost_estimate=pl.CostEstimate(flops=int(flops), bytes_accessed=int(nbytes), transcendentals=0),
    )(*arrays)


def sds(shape, dtype):
    return jax.ShapeDtypeStruct(shape, dtype)


def by_rows(count, chunk, fn):
    def step(i, carry):
        fn(pl.ds(pl.multiple_of(i * chunk, chunk), chunk))
        return carry

    lax.fori_loop(0, count // chunk, step, 0)


def lanes(i, width):
    return pl.ds(pl.multiple_of(i * width, width), width)


def partner(v):
    low = iota(v.shape, 1) % HEAD < ROT // 2
    return jnp.where(low, pltpu.roll(v, v.shape[1] - ROT // 2, 1), pltpu.roll(v, ROT // 2, 1))


def split_heads(v):
    first = iota(v.shape, 1) < HEAD
    zero = jnp.zeros_like(v)
    return jnp.concatenate([jnp.where(first, v, zero), jnp.where(first, zero, v)], axis=0)


def stats(x):
    centre = jnp.mean(x, axis=-1, keepdims=True)
    centered = x - centre
    spread = jnp.mean(centered * centered, axis=-1, keepdims=True)
    return centered, lax.rsqrt(spread + 1e-05)


def make(n):
    R = n // NB
    assert R * NB == n and R & (R - 1) == 0

    def shift(v, k):
        k = k % NB
        return lax.ppermute(v, "dp", [(b * R + r, (b + k) % NB * R + r) for b in range(NB) for r in range(R)])

    def swap(v, mask):
        return lax.ppermute(v, "dp", [(d, d ^ mask) for d in range(n)])

    def gather_r(own):
        got = {0: own}
        for m in range(2, R, 2):
            got[m] = swap(own, m)
        for m in range(0, R, 2):
            got[m + 1] = swap(got[m], 1)
        return [got[m] for m in range(R)]

    def on_device(
        block_in, grad_out, w_qkv, b_qkv, w_o, b_o, w_in, b_in, w_out, b_out,
        ln1_gain, ln1_shift, ln2_gain, ln2_shift, seq_lens, seq_device, seq_offset,
    ):
        T = block_in.shape[0]
        NT = NB * T
        rows = w_qkv.shape[0]
        ff_dev = w_out.shape[0]
        FB = w_in.shape[1] // NB
        W1 = 3 * QB + FB
        J = R // 2
        MF = NB * rows + ff_dev
        MA = NB * rows
        idx = lax.axis_index("dp").astype(I32)
        b, r = idx // R, idx % R
        br = jnp.stack([b, r])

        slots1 = jnp.arange(T, dtype=I32)
        owners = [(b - k) % NB * R + r for k in range(NB)]
        device = jnp.concatenate([jnp.full((T,), o, I32) for o in owners])
        slots = jnp.tile(slots1, NB)
        count = seq_lens.shape[0]
        inside = (
            (seq_device[None, :] == device[:, None])
            & (slots[:, None] >= seq_offset[None, :])
            & (slots[:, None] < (seq_offset + seq_lens)[None, :])
        )
        number = jnp.arange(count, dtype=I32)
        present = jnp.any(inside, axis=1)
        segment = jnp.where(present, jnp.sum(jnp.where(inside, number[None, :], 0), axis=1), count + slots)
        position = jnp.sum(jnp.where(inside, slots[:, None] - seq_offset[None, :], 0), axis=1)
        live = present.astype(F32)[:, None]
        seg = segment.reshape(NB, T)
        allowed = (seg[:, :, None] == seg[:, None, :]) & (slots1[None, None, :] <= slots1[None, :, None])
        mask = jnp.where(allowed, 0.0, NEG).astype(F32)
        lane = jnp.arange(2 * HEAD, dtype=I32) % HEAD
        half = ROT // 2
        freqs = 10000.0 ** (-(lane % half).astype(F32) / half)
        angle = position.astype(F32)[:, None] * jnp.where(lane < ROT, freqs, 0.0)[None, :]
        cosine = jnp.cos(angle)
        sines = jnp.sin(angle) * jnp.where(lane < half, -1.0, 1.0)[None, :]

        small = [b_in, b_qkv, b_o, b_out, ln1_gain, ln1_shift, ln2_gain, ln2_shift]
        widths = [v.shape[0] for v in small]
        offsets = [sum(widths[:i]) for i in range(len(small))]
        WS = 1024

        def pack_body(br, qkv_ref, in_ref, o_ref, out_ref, *rest):
            vectors, outs = rest[: len(small)], rest[len(small) :]
            for k in range(NB):
                to = lax.rem(br[0] + k, NB)
                for s in range(3):
                    outs[k][:, s * QB : (s + 1) * QB] = qkv_ref[:, lanes(s * NB + to, QB)]
                outs[k][:, 3 * QB :] = in_ref[:, lanes(to, FB)]
            outs[NB][:ff_dev] = out_ref[...]
            outs[NB][ff_dev:] = o_ref[...]
            parts = [v[...].astype(F32) for v in vectors]
            if WS > sum(widths):
                parts.append(jnp.zeros((1, WS - sum(widths)), F32))
            every = jnp.concatenate(parts, axis=1)
            for i in range(8):
                outs[NB + 1][:, i] = jnp.broadcast_to(every[:, i * 128 : (i + 1) * 128], (n, 128)).astype(BF)

        packed = call(
            pack_body,
            [("s", br), ("v", w_qkv), ("v", w_in), ("v", w_o), ("v", w_out)] + [("v", v.reshape(1, -1)) for v in small],
            [sds((rows, W1), BF)] * NB + [sds((ff_dev + rows, D), BF), sds((n, 8, 128), BF)], extra=56 << 20,
        )
        columns, own_two, small_out = packed[:NB], packed[NB], packed[NB + 1]

        mine = jnp.concatenate([columns[0]] + [shift(columns[k], k) for k in range(1, NB)]).reshape(NB, rows, W1)
        two = gather_r(own_two)
        one = gather_r(mine)
        after, _ = lax.optimization_barrier((block_in, mine))
        tokens = [block_in] + [shift(after, k) for k in range(1, NB)]
        small_in = lax.all_to_all(small_out, "dp", 0, 0, tiled=True)
        after, _ = lax.optimization_barrier((grad_out, tokens))
        grads_in = [grad_out] + [shift(after, k) for k in range(1, NB)]

        def pick(width_mod, off, base, width):
            return (iota((width, width_mod.shape[1]), 0) + base == off + width_mod).astype(BF)

        def window(off, width):
            base = off // 128 * 128
            return base, -(-(off + width) // 128) * 128 - base

        def dec_body(br, got, bq, bi, g1, s1, g2, s2, bo):
            def expand(which, col):
                width, off = widths[which], offsets[which]
                base, span = window(off, width)
                total = col.shape[1]
                sel = pick(lax.rem(col, width), off, base, span)
                every = dot_nn(jnp.concatenate([got[:, i] for i in range(base // 128, (base + span) // 128)], axis=1), sel)
                return jnp.sum(jnp.where(iota((n, total), 0) == lax.div(col, width), every, 0.0), axis=0, keepdims=True)

            at = iota((1, 3 * QB), 1)
            bq[...] = expand(1, lax.div(at, QB) * D + br[0] * QB + lax.rem(at, QB))
            bi[...] = expand(0, iota((1, FB), 1) + br[0] * FB)
            whole = iota((1, D), 1)
            bo[...] = expand(2, whole) + expand(3, whole)
            for ref, which in ((g1, 4), (s1, 5), (g2, 6), (s2, 7)):
                ref[...] = expand(which, whole)

        row = sds((1, D), F32)
        bias_qkv, bias_in, gain_one, shift_one, gain_two, shift_two, bias_o = call(
            dec_body, [("s", br), ("v", small_in)], [sds((1, 3 * QB), F32), sds((1, FB), F32)] + [row] * 5
        )

        def load_one(br, pieces, w1, sems):
            copies = []
            for m in range(R):
                for k in range(NB):
                    copies.append(
                        pltpu.make_async_copy(
                            pieces[m].at[k], w1.at[lax.rem(br[0] + (NB - k), NB), br[1] ^ m], sems.at[m * NB + k]
                        )
                    )
            return copies

        def load_out(br, pieces, wout, sems):
            return [
                pltpu.make_async_copy(pieces[m].at[pl.ds(0, ff_dev)], wout.at[br[1] ^ m], sems.at[m]) for m in range(R)
            ]

        def load_o(br, pieces, wo, sems):
            return [
                pltpu.make_async_copy(pieces[m].at[pl.ds(ff_dev, rows)], wo.at[br[1] ^ m], sems.at[m]) for m in range(R)
            ]

        dma = pltpu.SemaphoreType.DMA
        PAIRS = QB // 128

        def fwd_body(br, x0, x1, x2, x3, cos, sin, mask_ref, bq, bi, g1, s1, g2, s2, *rest):
            one, two, rest = rest[:R], rest[R : 2 * R], rest[2 * R :]
            act1, act2, q, k, v, probs, mixed, hidden, dgelu, xhat_ref, w1, wo, wout, own, p1h, p2h, p3h = rest[:17]
            p1, p2, p3, sem1, semo, semout, semp = rest[17:]
            c1, co, cout = load_one(br, one, w1, sem1), load_o(br, two, wo, semo), load_out(br, two, wout, semout)
            for c in c1 + co + cout:
                c.start()
            for i, x in enumerate((x0, x1, x2, x3)):

                def norm(rws, i=i, x=x):
                    centered, rstd = stats(x[rws].astype(F32))
                    xhat = centered * rstd
                    to = pl.ds(pl.multiple_of(i * T + rws.start, T), T)
                    xhat_ref[to] = xhat
                    act1[to] = (xhat * g1[...] + s1[...]).astype(BF)
                    act2[to] = (xhat * g2[...] + s2[...]).astype(BF)

                by_rows(T, T, norm)
            for c in c1:
                c.wait()
            for s, ref in enumerate((q, k, v)):
                wt = w1[:, :, :, s * QB : (s + 1) * QB].reshape(D, QB)

                def project(rws, s=s, ref=ref, wt=wt):
                    y = dot_nn(act1[rws], wt) + bq[:, s * QB : (s + 1) * QB]
                    for p in range(PAIRS):
                        z = y[:, p * 128 : (p + 1) * 128]
                        if s < 2:
                            z = z * cos[rws] + partner(z) * sin[rws]
                        ref[rws, p * 128 : (p + 1) * 128] = z.astype(BF)

                by_rows(NT, 256, project)

            def attend(i, carry):
                rws = pl.ds(pl.multiple_of(i * T, T), T)
                m2 = mask_ref[i]
                m2 = jnp.concatenate([m2, m2], axis=0)
                for p in range(PAIRS):
                    cols = slice(p * 128, (p + 1) * 128)
                    s = dot_nt(split_heads(q[rws, cols]), k[rws, cols]) * (1.0 / math.sqrt(HEAD)) + m2
                    e = jnp.exp(s - jnp.max(s, axis=-1, keepdims=True))
                    pr = e / jnp.sum(e, axis=-1, keepdims=True)
                    probs[i * PAIRS + p] = pr
                    pb = pr.astype(BF)
                    pb = jnp.concatenate([pb[:T], pb[T:]], axis=1)
                    mixed[rws, cols] = dot_nn(pb, split_heads(v[rws, cols])).astype(BF)
                return carry

            lax.fori_loop(0, NB, attend, 0)

            def feed(t, carry):
                cols = lanes(t, 256)
                wt = w1[:, :, :, pl.ds(pl.multiple_of(3 * QB + t * 256, 256), 256)].reshape(D, 256)

                def act(rws):
                    h = dot_nn(act2[rws], wt) + bi[:, cols]
                    cdf = 0.5 * (1.0 + lax.erf(h * (1.0 / math.sqrt(2.0))))
                    hidden[rws, cols] = (h * cdf).astype(BF)
                    dgelu[rws, cols] = cdf + h * (jnp.exp(-0.5 * h * h) * (1.0 / math.sqrt(2.0 * math.pi)))

                by_rows(NT, 256, act)
                return carry

            lax.fori_loop(0, FB // 256, feed, 0)
            for c in co + cout:
                c.wait()

            def project_out(t, carry):
                cols = lanes(t, 256)
                y = dot_nn(mixed[...], wo[:, :, cols].reshape(QB, 256))
                y = y + dot_nn(hidden[...], wout[:, :, cols].reshape(FB, 256))
                own[:, cols] = y[:T]
                for i, ref in enumerate((p1, p2, p3)):
                    ref[:, cols] = y[(i + 1) * T : (i + 2) * T].astype(BF)
                return carry

            lax.fori_loop(0, D // 256, project_out, 0)
            sends = [pltpu.make_async_copy(a, z, semp.at[i]) for i, (a, z) in enumerate(((p1, p1h), (p2, p2h), (p3, p3h)))]
            for c in sends:
                c.start()
            for c in sends:
                c.wait()

        tab = sds((NT, D), BF)
        third = sds((NT, QB), BF)
        block = sds((T, D), BF)
        act1, act2, q, k, v, probs, mixed, hidden, dgelu, xhat, full_one, full_o, full_out, own_part, *parts = call(
            fwd_body,
            [("s", br)] + [("v", x) for x in tokens]
            + [("v", a) for a in (cosine, sines, mask, bias_qkv, bias_in, gain_one, shift_one, gain_two, shift_two)]
            + [("a", a) for a in one + two],
            [tab, tab, third, third, third, sds((NB * PAIRS, 2 * T, T), F32), third, sds((NT, FB), BF), sds((NT, FB), F32),
             sds((NT, D), F32), sds((NB, R, rows, W1), BF), sds((R, rows, D), BF), sds((R, ff_dev, D), BF),
             sds((T, D), F32), block, block, block],
            [pltpu.VMEM((T, D), BF)] * 3 + [dma((R * NB,)), dma((R,)), dma((R,)), dma((3,))], hbm=(14, 15, 16),
            flops=2 * NT * D * W1 + 2 * NT * D * (QB + FB) + 8 * NT * T * QB,
        )

        returned = [shift(parts[k - 1], -k) for k in range(1, NB)]

        def total_body(x, live_ref, bo, own, p1, p2, p3, out):
            def fn(rws):
                y = x[rws].astype(F32) + bo[...] + own[rws]
                for ref in (p1, p2, p3):
                    y = y + ref[rws].astype(F32)
                out[rws] = (y * live_ref[rws]).astype(BF)

            by_rows(T, 32, fn)

        (block_out,) = call(
            total_body,
            [("v", a) for a in (block_in, live[:T], bias_o, own_part, *returned)], [block],
        )

        def bwd1_body(br, live_ref, g0, g1, g2, g3, act2, hidden, dgelu, wout, *rest):
            grad, dhid, keep, send, sum_in, term, flip = rest
            for i, g in enumerate((g0, g1, g2, g3)):

                def masked(rws, i=i, g=g):
                    to = pl.ds(pl.multiple_of(i * T + rws.start, T), T)
                    grad[to] = (g[rws].astype(F32) * live_ref[to]).astype(BF)

                by_rows(T, T, masked)

            def term_out(t, carry):
                flip[...] = hidden[:, lanes(t, 256)].T
                y = dot_nn(flip[...], grad[...])
                per = 256 // ff_dev
                term[pl.ds(t * per, per)] = y.reshape(per, ff_dev, D)
                return carry

            lax.fori_loop(0, FB // 256, term_out, 0)

            def to_out(j, carry):
                keep[j, MA:] = term[br[1] ^ (2 * j)]
                send[j, MA:] = term[br[1] ^ (2 * j + 1)].astype(BF)
                return carry

            lax.fori_loop(0, J, to_out, 0)

            def d_hidden(t, carry):
                cols = lanes(t, 256)
                per = 256 // ff_dev
                wt = wout[pl.ds(t * per, per)].reshape(256, D)
                y = (dot_nt(grad[...], wt) * dgelu[:, cols]).astype(BF)
                dhid[:, cols] = y
                sum_in[:, cols] = jnp.sum(y.astype(F32), axis=0, keepdims=True)
                return carry

            lax.fori_loop(0, FB // 256, d_hidden, 0)

            term_r = term.reshape(R * ff_dev // rows, rows, D) if ff_dev != rows else term

            def term_in(t, carry):
                flip[...] = act2[:, lanes(t, 256)].T
                term_r[:R] = dot_nn(flip[...], dhid[...]).reshape(R, rows, D)
                at = pl.ds(pl.multiple_of(t * rows, rows), rows)

                def one_j(j, carry):
                    keep[j, at] = term_r[br[1] ^ (2 * j)]
                    send[j, at] = term_r[br[1] ^ (2 * j + 1)].astype(BF)
                    return carry

                return lax.fori_loop(0, J, one_j, carry)

            lax.fori_loop(0, NB, term_in, 0)

        grad_r, dhid, keep_f, send_f, sum_in = call(
            bwd1_body,
            [("s", br), ("v", live)] + [("v", g) for g in grads_in] + [("v", a) for a in (act2, hidden, dgelu, full_out)],
            [tab, sds((NT, FB), BF), sds((J, MF, D), F32), sds((J, MF, D), BF), sds((1, FB), F32)],
            [pltpu.VMEM((R, ff_dev, D), F32), pltpu.VMEM((256, NT), BF)],
            flops=6 * NT * D * FB,
        )

        def bwd2_body(br, grad, mixed, act1, q, k, v, probs, cos, sin, wo, *rest):
            dqkv, keep, send, sum_qkv, dmix, term, term_o, flip = rest
            flip[...] = mixed[...].T
            term_o[...] = dot_nn(flip[...], grad[...]).reshape(R, rows, D)

            def to_o(j, carry):
                for c in range(NB):
                    cols = slice(c * QB, (c + 1) * QB)
                    keep[j, c * rows : (c + 1) * rows, 3 * QB :] = term_o[br[1] ^ (2 * j), :, cols]
                    send[j, c * rows : (c + 1) * rows, 3 * QB :] = term_o[br[1] ^ (2 * j + 1), :, cols].astype(BF)
                return carry

            lax.fori_loop(0, J, to_o, 0)
            dmix[...] = dot_nt(grad[...], wo[...].reshape(QB, D)).astype(BF)

            def attend(i, carry):
                rws = pl.ds(pl.multiple_of(i * T, T), T)
                for p in range(PAIRS):
                    cols = slice(p * 128, (p + 1) * 128)
                    pr = probs[i * PAIRS + p]
                    pb = pr.astype(BF)
                    dm2 = split_heads(dmix[rws, cols])
                    dp = dot_nt(dm2, v[rws, cols])
                    ds = (pr * (dp - jnp.sum(dp * pr, axis=-1, keepdims=True))).astype(BF)
                    dq = dot_nn(jnp.concatenate([ds[:T], ds[T:]], axis=1), split_heads(k[rws, cols]))
                    dk = dot_nn(ds.T, split_heads(q[rws, cols]))
                    dv = dot_nn(pb.T, dm2)
                    for s, z in enumerate((dq, dk)):
                        z = z * (1.0 / math.sqrt(HEAD))
                        z = z * cos[rws] - partner(z) * sin[rws]
                        dqkv[rws, s * QB + p * 128 : s * QB + (p + 1) * 128] = z.astype(BF)
                    dqkv[rws, 2 * QB + p * 128 : 2 * QB + (p + 1) * 128] = dv.astype(BF)
                return carry

            lax.fori_loop(0, NB, attend, 0)
            sum_qkv[...] = jnp.sum(dqkv[...].astype(F32), axis=0, keepdims=True)

            def term_qkv(t, carry):
                flip[...] = act1[:, lanes(t, 256)].T
                term[...] = dot_nn(flip[...], dqkv[...]).reshape(R, rows, 3 * QB)
                at = pl.ds(pl.multiple_of(t * rows, rows), rows)

                def one_j(j, carry):
                    keep[j, at, : 3 * QB] = term[br[1] ^ (2 * j)]
                    send[j, at, : 3 * QB] = term[br[1] ^ (2 * j + 1)].astype(BF)
                    return carry

                return lax.fori_loop(0, J, one_j, carry)

            lax.fori_loop(0, NB, term_qkv, 0)

        dqkv, keep_a, send_a, sum_qkv = call(
            bwd2_body,
            [("s", br)] + [("v", a) for a in (grad_r, mixed, act1, q, k, v, probs, cosine, sines, full_o)],
            [sds((NT, 3 * QB), BF), sds((J, MA, D), F32), sds((J, MA, D), BF), sds((1, 3 * QB), F32)],
            [pltpu.VMEM((NT, QB), BF), pltpu.VMEM((R, rows, 3 * QB), F32), pltpu.VMEM((R, rows, D), F32),
             pltpu.VMEM((256, NT), BF)],
            flops=2 * NT * D * (3 * QB + 2 * QB) + 16 * NT * T * QB,
        )

        def merge_body(keep, got, *outs):
            size = keep.shape[1]
            for j in range(J):

                def fn(rws, j=j):
                    y = keep[j, rws] + got[j, rws].astype(F32)
                    outs[j][rws] = y if j == 0 else y.astype(BF)

                by_rows(size, 32, fn)

        def merge(keep, send):
            size = keep.shape[1]
            got = swap(send, 1)
            outs = call(merge_body, [("v", keep), ("v", got)], [sds((size, D), F32)] + [sds((size, D), BF)] * (J - 1))
            return [outs[0]] + [swap(outs[j], 2 * j) for j in range(1, J)]

        merged_f = merge(keep_f, send_f)
        merged_a = merge(keep_a, send_a)

        out_widths = [FB * NB // n, 3 * D // n] + [D // n] * 5
        out_offsets = [sum(out_widths[:i]) for i in range(len(out_widths))]
        WO = -(-sum(out_widths) // 128) * 128

        def bwd3_body(br, xhat, w1, dqkv, dhid, grad, sum_in, sum_qkv, g1, g2, *rest):
            own, p1h, p2h, p3h, small, p1, p2, p3, gs, sums, semp = rest
            gs[...] = jnp.sum(grad[:T].astype(F32), axis=0, keepdims=True)

            def back(t, carry):
                cols = lanes(t, QB)
                d1 = dot_nt(dqkv[...], w1[t, :, :, : 3 * QB].reshape(QB, 3 * QB))
                d2 = dot_nt(dhid[...], w1[t, :, :, 3 * QB :].reshape(QB, FB))
                xh = xhat[:, cols]
                y = d1 * g1[:, cols] + d2 * g2[:, cols]
                own[:, cols] = y[:T]
                for i, ref in enumerate((p1, p2, p3)):
                    ref[:, cols] = y[(i + 1) * T : (i + 2) * T].astype(BF)
                for i, z in enumerate((d1 * xh, d1, d2 * xh, d2)):
                    sums[i : i + 1, cols] = jnp.sum(z, axis=0, keepdims=True)
                return carry

            lax.fori_loop(0, D // QB, back, 0)
            sends = [pltpu.make_async_copy(a, z, semp.at[i]) for i, (a, z) in enumerate(((p1, p1h), (p2, p2h), (p3, p3h)))]
            for c in sends:
                c.start()

            total = jnp.zeros((n, WO), F32)

            def place(total, vec, col, which):
                size = vec.shape[1]
                width, off = out_widths[which], out_offsets[which]
                mine = jnp.where(iota((n, size), 0) == lax.div(col, width), vec, 0.0)
                base = off // 128 * 128
                span = -(-(off + width) // 128) * 128 - base
                sel = pick(lax.rem(col, width), off, base, span)
                high = mine.astype(BF)
                low = (mine - high.astype(F32)).astype(BF)
                placed = dot_nt(high, sel) + dot_nt(low, sel)
                parts = []
                if base:
                    parts.append(jnp.zeros((n, base), F32))
                parts.append(placed)
                if base + span < WO:
                    parts.append(jnp.zeros((n, WO - base - span), F32))
                return total + (jnp.concatenate(parts, axis=1) if len(parts) > 1 else placed)

            whole = iota((1, D), 1)
            at = iota((1, 3 * QB), 1)
            total = place(total, sum_in[...], iota((1, FB), 1) + br[0] * FB, 0)
            total = place(total, sum_qkv[...], lax.div(at, QB) * D + br[0] * QB + lax.rem(at, QB), 1)
            total = place(total, gs[...], whole, 2)
            for i in range(4):
                total = place(total, sums[i : i + 1], whole, 3 + i)
            for i in range(8):
                small[:, i] = total[:, i * 128 : (i + 1) * 128] if (i + 1) * 128 <= WO else jnp.zeros((n, 128), F32)
            for c in sends:
                c.wait()

        own_g, g_1, g_2, g_3, small_grads = call(
            bwd3_body,
            [("s", br)] + [("v", a) for a in (xhat, full_one, dqkv, dhid, grad_r, sum_in, sum_qkv, gain_one, gain_two)],
            [sds((T, D), F32), block, block, block, sds((n, 8, 128), F32)],
            [pltpu.VMEM((T, D), BF)] * 3 + [pltpu.VMEM((1, D), F32), pltpu.VMEM((8, D), F32), dma((3,))], hbm=(1, 2, 3),
            flops=2 * NT * D * W1,
        )
        g_back = [shift(g, -k) for k, g in ((1, g_1), (2, g_2), (3, g_3))]
        small_back = lax.all_to_all(small_grads, "dp", 0, 0, tiled=True)

        def input_body(x, grad, own, p1, p2, p3, out):
            def fn(rws):
                centered, rstd = stats(x[rws].astype(F32))
                xh = centered * rstd
                g = own[rws]
                for ref in (p1, p2, p3):
                    g = g + ref[rws].astype(F32)
                mean_g = jnp.mean(g, axis=-1, keepdims=True)
                mean_gx = jnp.mean(g * xh, axis=-1, keepdims=True)
                out[rws] = (grad[rws].astype(F32) + rstd * (g - mean_g - xh * mean_gx)).astype(BF)

            by_rows(T, 32, fn)

        (grad_input,) = call(input_body, [("v", a) for a in (block_in, grad_r[:T], own_g, *g_back)], [block])

        def plane_f_body(br, *rest):
            got, (w_out_ref, z0, z1, z2, z3) = rest[:J], rest[J:]

            def out_rows(rws):
                y = got[0][pl.ds(pl.multiple_of(MA + rws.start, 8), rws.size)]
                for ref in got[1:]:
                    y = y + ref[pl.ds(pl.multiple_of(MA + rws.start, 8), rws.size)].astype(F32)
                w_out_ref[rws] = y

            by_rows(ff_dev, min(32, ff_dev), out_rows)
            for k, ref in enumerate((z0, z1, z2, z3)):
                at = pl.ds(pl.multiple_of(lax.rem(br[0] + k, NB) * rows, rows), rows)
                y = got[0][at]
                for other in got[1:]:
                    y = y + other[at].astype(F32)
                ref[...] = y if k == 0 else y.astype(BF)

        grad_w_out, zf0, *zf = call(
            plane_f_body, [("s", br)] + [("v", a) for a in merged_f],
            [sds((ff_dev, D), F32), sds((rows, FB), F32)] + [sds((rows, FB), BF)] * 3,
        )

        def plane_a_body(br, *rest):
            got, (w_o_ref, z0, z1, z2, z3) = rest[:J], rest[J:]
            for c in range(NB):
                y = got[0][c * rows : (c + 1) * rows, 3 * QB :]
                for other in got[1:]:
                    y = y + other[c * rows : (c + 1) * rows, 3 * QB :].astype(F32)
                w_o_ref[:, c * QB : (c + 1) * QB] = y
            for k, ref in enumerate((z0, z1, z2, z3)):
                at = pl.ds(pl.multiple_of(lax.rem(br[0] + k, NB) * rows, rows), rows)
                y = got[0][at, : 3 * QB]
                for other in got[1:]:
                    y = y + other[at, : 3 * QB].astype(F32)
                ref[...] = y if k == 0 else y.astype(BF)

        grad_w_o, za0, *za = call(
            plane_a_body, [("s", br)] + [("v", a) for a in merged_a],
            [sds((rows, D), F32), sds((rows, 3 * QB), F32)] + [sds((rows, 3 * QB), BF)] * 3,
        )
        zf = [zf0] + [shift(z, k + 1) for k, z in enumerate(zf)]
        za = [za0] + [shift(z, k + 1) for k, z in enumerate(za)]

        def place_f_body(br, z0, z1, z2, z3, out):
            for k, ref in enumerate((z0, z1, z2, z3)):
                out[:, lanes(lax.rem(br[0] + (NB - k), NB), FB)] = ref[...].astype(F32)

        def place_a_body(br, z0, z1, z2, z3, out):
            for k, ref in enumerate((z0, z1, z2, z3)):
                at = lax.rem(br[0] + (NB - k), NB)
                for s in range(3):
                    out[:, lanes(s * NB + at, QB)] = ref[:, s * QB : (s + 1) * QB].astype(F32)

        (grad_w_in,) = call(place_f_body, [("s", br)] + [("v", z) for z in zf], [sds((rows, NB * FB), F32)])
        (grad_w_qkv,) = call(place_a_body, [("s", br)] + [("v", z) for z in za], [sds((rows, 3 * D), F32)])

        summed = jnp.sum(small_back, axis=0).reshape(-1)
        outs = [summed[o : o + w] for o, w in zip(out_offsets, out_widths)]
        grad_b_in, grad_b_qkv, grad_b, grad_g1, grad_s1, grad_g2, grad_s2 = outs
        return (
            block_out, grad_input, grad_w_qkv, grad_b_qkv, grad_w_o, grad_b, grad_w_in, grad_b_in,
            grad_w_out, grad_b, grad_g1, grad_s1, grad_g2, grad_s2,
        )

    return on_device


def solution(mesh):
    two, one = P("dp", None), P("dp")
    n = mesh.shape["dp"]
    on_device = make(n)

    return jax.shard_map(
        on_device,
        mesh=mesh,
        in_specs=(two, two, two, one, two, one, two, one, two, one, one, one, one, one, P(), P(), P()),
        out_specs=(two, two, two, one, two, one, two, one, two, one, one, one, one, one),
        check_vma=False,
    )
```

profile of v0, /device:TPU:0, one launch (start us, length us, event | category | flops | bytes accessed | tf_op | source)
XLA Modules:
  0.0 195.4 jit_solution(3798500372138744319)
XLA Ops:
  1.3 2.1 %shard_map.272 = (bf16[32,1792]{1,0:T(8,128)(2,1)}, bf16[32,1792]{1,0:T(8,128)(2,1)}, bf16[32,1792]{1,0:T(8,128)(2,1)}, bf16[32,1792]{1,0:T(8,128)(2,1)}, bf16[1...) custom-call(s32[2]{0:T(128)} %pad_add_fusion.1.br, bf16[32,3072]{1,0:T(8,128)(2,1)} %qkv_ref.1, bf16[32,4096]{1,0:T(8,128)(2,1)} %in_ref.1, ...), custom_call_target="tpu_custom_call" | custom-call | bytes 1639240 | tf_op jit(solution)/shard_map/pallas_call | solution.py:41
  3.4 5.1 %collective-permute-start.2 = (bf16[32,1792]{1,0:T(8,128)(2,1)}, bf16[32,1792]{1,0:T(8,128)(2,1)S(1)}, u32[]{:S(2)}, u32[]{:S(2)}) collective-permute-start(bf16[32,1792]{1,0:T(8,128)(2,1)} %get-tuple-element.83), channel_id=1, source_target_pairs={{0,24},{1,25},{2,26},{3,27},{4,28},{5,29},{6,30},{7,31},{8,0},{9,1... | collective-permute-start | bytes 344072 | tf_op jit(solution)/shard_map/ppermute | solution.py:92
  11.0 4.1 %all-to-all-start = ((bf16[32,8,128]{2,1,0:T(8,128)(2,1)}), bf16[32,8,128]{2,1,0:T(8,128)(2,1)S(1)}, u32[]{:S(2)}, u32[]{:S(2)}) async-start(bf16[32,8,128]{2,1,0:T(8,128)(2,1)} %get-tuple-element.78), calls=%async_computation | async-start | bytes 131072 | tf_op jit(solution)/shard_map/all_to_all | solution.py:180
  18.8 2.5 %collective-permute-start.18 = (bf16[160,1024]{1,0:T(8,128)(2,1)}, bf16[160,1024]{1,0:T(8,128)(2,1)S(1)}, u32[]{:S(2)}, u32[]{:S(2)}) collective-permute-start(bf16[160,1024]{1,0:T(8,128)(2,1)} %get-tuple-element.91.rest_8_), channel_id=1, source_target_pairs={{0,6},{1,7},{2,4},{3,5},{4,2},{5,3},{6,0},{7,1},{8,14},{9,15},{10,... | collective-permute-start | bytes 983048 | tf_op jit(solution)/shard_map/ppermute | solution.py:95
  23.1 2.2 %collective-permute-start.4 = (bf16[128,1024]{1,0:T(8,128)(2,1)}, bf16[128,1024]{1,0:T(8,128)(2,1)S(1)}, u32[]{:S(2)}, u32[]{:S(2)}) collective-permute-start(bf16[128,1024]{1,0:T(8,128)(2,1)} %x.3), channel_id=1, source_target_pairs={{0,16},{1,17},{2,18},{3,19},{4,20},{5,21},{6,22},{7,23},{8,24},{9,... | collective-permute-start | bytes 786440 | tf_op jit(solution)/shard_map/ppermute | solution.py:92
  28.4 4.7 %collective-permute-done.16.rest_12_ = bf16[160,1024]{1,0:T(8,128)(2,1)} collective-permute-done((bf16[160,1024]{1,0:T(8,128)(2,1)}, bf16[160,1024]{1,0:T(8,128)(2,1)}, u32[]{:S(2)}, u32[]{:S(2)}) %collective-permute-start.16) | collective-permute-done | bytes 327712 | tf_op jit(solution)/shard_map/ppermute | solution.py:95
  37.3 5.5 %collective-permute-done.4.x2 = bf16[128,1024]{1,0:T(8,128)(2,1)S(1)} collective-permute-done((bf16[128,1024]{1,0:T(8,128)(2,1)}, bf16[128,1024]{1,0:T(8,128)(2,1)S(1)}, u32[]{:S(2)}, u32[]{:S(2)}) %collective-permute-start.4) | collective-permute-done | bytes 262176 | tf_op jit(solution)/shard_map/ppermute | solution.py:92
  46.5 9.5 %collective-permute-done.9.rest_4_ = bf16[4,32,1792]{2,1,0:T(8,128)(2,1)S(1)} collective-permute-done((bf16[4,32,1792]{2,1,0:T(8,128)(2,1)S(1)}, bf16[4,32,1792]{2,1,0:T(8,128)(2,1)S(1)}, u32[]{:S(2)}, u32[]{:S(2)}) %collective-permute-start.9) | collective-permute-done | bytes 458784 | tf_op jit(solution)/shard_map/ppermute | solution.py:95
  60.7 2.3 %collective-permute-start.24 = (bf16[128,1024]{1,0:T(8,128)(2,1)}, bf16[128,1024]{1,0:T(8,128)(2,1)S(1)}, u32[]{:S(2)}, u32[]{:S(2)}) collective-permute-start(bf16[128,1024]{1,0:T(8,128)(2,1)} %g0.1), channel_id=1, source_target_pairs={{0,16},{1,17},{2,18},{3,19},{4,20},{5,21},{6,22},{7,23},{8,24},{9,... | collective-permute-start | bytes 786440 | tf_op jit(solution)/shard_map/ppermute | solution.py:92
  68.3 15.4 %shard_map.274 = (bf16[512,1024]{1,0:T(8,128)(2,1)S(1)}, bf16[512,1024]{1,0:T(8,128)(2,1)S(1)}, bf16[512,256]{1,0:T(8,128)(2,1)S(1)}, bf16[512,256]{1,0:T(8,128)...) custom-call(s32[2]{0:T(128)S(1)} %copy-done.11, ...), custom_call_target="tpu_custom_call" | custom-call | flops 3355443200 | bytes 25189384 | tf_op jit(solution)/shard_map/pallas_call | solution.py:41
  83.8 7.2 %shard_map.276 = (bf16[512,1024]{1,0:T(8,128)(2,1)S(1)}, bf16[512,1024]{1,0:T(8,128)(2,1)S(1)}, f32[4,256,1024]{2,1,0:T(8,128)S(1)}, bf16[4,256,1024]{2,1,0:T(8,128)(2,1)S(1)}, f32[1,1024]{1,0:T(1,128)S(1)}) custom-call(s32[2]{0:T(128)S(1)} %copy-done.11, f32[512,1]{1,0:T(8,128)S(1)} %copy.35.live_ref, bf16[128,1024]{1,0:T(8,128)(2,1)S(1)} %copy-done.15, ...), custom_call_target="tpu_custom_call" | custom-call | flops 3221225472 | bytes 15734792 | tf_op jit(solution)/shard_map/pallas_call | solution.py:41
  91.1 7.2 %shard_map.277 = (bf16[512,768]{1,0:T(8,128)(2,1)S(1)}, f32[4,128,1024]{2,1,0:T(8,128)S(1)}, bf16[4,128,1024]{2,1,0:T(8,128)(2,1)S(1)}, f32[1,768]{1,0:T(1,128)S(1)}) custom-call(s32[2]{0:T(128)S(1)} %copy-done.11, bf16[512,1024]{1,0:T(8,128)(2,1)S(1)} %get-tuple-element.101.grad, bf16[512,256]{1,0:T(8,128)(2,1)S(1)} %get-tuple-element.104.mixed, ...), custom_call_target="tpu_custom_call" | custom-call | flops 1610612736 | bytes 9178120 | tf_op jit(solution)/shard_map/pallas_call | solution.py:41
  98.8 4.0 %collective-permute-start.20 = (bf16[128,1024]{1,0:T(8,128)(2,1)S(1)}, bf16[128,1024]{1,0:T(8,128)(2,1)S(1)}, u32[]{:S(2)}, u32[]{:S(2)}) collective-permute-start(bf16[128,1024]{1,0:T(8,128)(2,1)S(1)} %get-tuple-element.93), channel_id=1, source_target_pairs={{0,24},{1,25},{2,26},{3,27},{4,28},{5,29},{6,30},{7,31},{8,0},{9,1... | collective-permute-start | bytes 786440 | tf_op jit(solution)/shard_map/ppermute | solution.py:92
  111.0 10.1 %collective-permute-done.21.p2 = bf16[128,1024]{1,0:T(8,128)(2,1)S(1)} collective-permute-done((bf16[128,1024]{1,0:T(8,128)(2,1)S(1)}, bf16[128,1024]{1,0:T(8,128)(2,1)S(1)}, u32[]{:S(2)}, u32[]{:S(2)}) %collective-permute-start.21) | collective-permute-done | bytes 262176 | tf_op jit(solution)/shard_map/ppermute | solution.py:92
  124.1 5.4 %shard_map.278 = (f32[128,1024]{1,0:T(8,128)S(1)}, bf16[128,1024]{1,0:T(8,128)(2,1)S(1)}, bf16[128,1024]{1,0:T(8,128)(2,1)S(1)}, bf16[128,1024]{1,0:T(8,128)(2,1)S(1)}, f32[32,8,128]{2,1,0:T(8,128)}) custom-call(s32[2]{0:T(128)S(1)} %copy-done.11, f32[512,1024]{1,0:T(8,128)S(1)} %get-tuple-element.102.xhat, ...), custom_call_target="tpu_custom_call" | custom-call | flops 1879048192 | bytes 10107912 | tf_op jit(solution)/shard_map/pallas_call | solution.py:41
  132.5 4.2 %all-to-all-start.1 = ((f32[32,8,128]{2,1,0:T(8,128)}), f32[32,8,128]{2,1,0:T(8,128)}, u32[]{:S(2)}, u32[]{:S(2)}) async-start(f32[32,8,128]{2,1,0:T(8,128)} %get-tuple-element.129), calls=%async_computation.1 | async-start | bytes 262144 | tf_op jit(solution)/shard_map/all_to_all | solution.py:557
  136.7 10.6 %collective-permute-done.31.rest_2_ = bf16[128,1024]{1,0:T(8,128)(2,1)S(1)} collective-permute-done((bf16[128,1024]{1,0:T(8,128)(2,1)}, bf16[128,1024]{1,0:T(8,128)(2,1)S(1)}, u32[]{:S(2)}, u32[]{:S(2)}) %collective-permute-start.31) | collective-permute-done | bytes 262176 | tf_op jit(solution)/shard_map/ppermute | solution.py:95
  148.2 3.7 %collective-permute-start.26 = (bf16[128,1024]{1,0:T(8,128)(2,1)}, bf16[128,1024]{1,0:T(8,128)(2,1)}, u32[]{:S(2)}, u32[]{:S(2)}) collective-permute-start(bf16[128,1024]{1,0:T(8,128)(2,1)} %copy-done.25), channel_id=1, source_target_pairs={{0,24},{1,25},{2,26},{3,27},{4,28},{5,29},{6,30},{7,31},{8,0},{9,1... | collective-permute-start | bytes 786440 | tf_op jit(solution)/shard_map/ppermute | solution.py:92
  157.2 2.0 %collective-permute-start.33 = (bf16[32,768]{1,0:T(8,128)(2,1)S(1)}, bf16[32,768]{1,0:T(8,128)(2,1)S(1)}, u32[]{:S(2)}, u32[]{:S(2)}) collective-permute-start(bf16[32,768]{1,0:T(8,128)(2,1)S(1)} %get-tuple-element.126), channel_id=1, source_target_pairs={{0,8},{1,9},{2,10},{3,11},{4,12},{5,13},{6,14},{7,15},{8,16},{9,17... | collective-permute-start | bytes 147464 | tf_op jit(solution)/shard_map/ppermute | solution.py:92
  159.8 2.5 %shard_map.284 = (f32[128,1024]{1,0:T(8,128)}, f32[32,1024]{1,0:T(8,128)S(1)}, bf16[32,1024]{1,0:T(8,128)(2,1)S(1)}, bf16[32,1024]{1,0:T(8,128)(2,1)S(1)}, bf16[32,1024]{1,0:T(8,128)(2,1)S(1)}) custom-call(s32[2]{0:T(128)S(1)} %copy-done.11, f32[256,1024]{1,0:T(8,128)S(1)} %get-tuple-element.133.rest_0_, bf16[256,1024]{1,0:T(8,128)(2,1)} %collective-permute-done.37.rest_1_, ...), custom_call_target="tpu_custom_call" | custom-call | bytes 3473416 | tf_op jit(solution)/shard_map/pallas_call | solution.py:41
  162.3 3.4 %collective-permute-start.34 = (bf16[32,768]{1,0:T(8,128)(2,1)S(1)}, bf16[32,768]{1,0:T(8,128)(2,1)S(1)}, u32[]{:S(2)}, u32[]{:S(2)}) collective-permute-start(bf16[32,768]{1,0:T(8,128)(2,1)S(1)} %get-tuple-element.127), channel_id=1, source_target_pairs={{0,16},{1,17},{2,18},{3,19},{4,20},{5,21},{6,22},{7,23},{8,24},{9,... | collective-permute-start | bytes 147464 | tf_op jit(solution)/shard_map/ppermute | solution.py:92
  167.6 14.7 %collective-permute-done.27.p2 = bf16[128,1024]{1,0:T(8,128)(2,1)} collective-permute-done((bf16[128,1024]{1,0:T(8,128)(2,1)}, bf16[128,1024]{1,0:T(8,128)(2,1)}, u32[]{:S(2)}, u32[]{:S(2)}) %collective-permute-start.27) | collective-permute-done | bytes 262176 | tf_op jit(solution)/shard_map/ppermute | solution.py:92
  182.4 3.9 %collective-permute-start.42 = (bf16[32,1024]{1,0:T(8,128)(2,1)S(1)}, bf16[32,1024]{1,0:T(8,128)(2,1)S(1)}, u32[]{:S(2)}, u32[]{:S(2)}) collective-permute-start(bf16[32,1024]{1,0:T(8,128)(2,1)S(1)} %get-tuple-element.140), channel_id=1, source_target_pairs={{0,24},{1,25},{2,26},{3,27},{4,28},{5,29},{6,30},{7,31},{8,0},{9,1... | collective-permute-start | bytes 196616 | tf_op jit(solution)/shard_map/ppermute | solution.py:92
  187.3 3.0 %shard_map.279 = bf16[128,1024]{1,0:T(8,128)(2,1)} custom-call(bf16[128,1024]{1,0:T(8,128)(2,1)S(1)} %copy-done, bf16[128,1024]{1,0:T(8,128)(2,1)S(1)} %slice.39.grad, f32[128,1024]{1,0:T(8,128)S(1)} %copy-done.4, bf16[128,1024]{1,0:T(8,128)(2,1)} %collective-permute-done.26.p1, bf16[128,1024]{1,0:T(8,128)(2,1)} %collective-permute-done.27.p2, ...), custom_call_target="tpu_custom_call" | custom-call | bytes 2097152 | tf_op jit(solution)/shard_map/pallas_call | solution.py:41
  (165 shorter events, 59.0 us)
Async XLA Ops:
  9.5 17.2 %collective-permute-start.14 = (bf16[160,1024]{1,0:T(8,128)(2,1)}, bf16[160,1024]{1,0:T(8,128)(2,1)}, u32[]{:S(2)}, u32[]{:S(2)}) collective-permute-start(bf16[160,1024]{1,0:T(8,128)(2,1)} %get-tuple-element.91.rest_8_), channel_id=1, source_target_pairs={{0,2},{1,3},{2,0},{3,1},{4,6},{5,7},{6,4},{7,5},{8,10},{9,11},{10,... | collective-permute-start | bytes 983048 | tf_op jit(solution)/shard_map/ppermute | solution.py:95
  11.0 46.2 %all-to-all-start = ((bf16[32,8,128]{2,1,0:T(8,128)(2,1)}), bf16[32,8,128]{2,1,0:T(8,128)(2,1)S(1)}, u32[]{:S(2)}, u32[]{:S(2)}) async-start(bf16[32,8,128]{2,1,0:T(8,128)(2,1)} %get-tuple-element.78), calls=%async_computation | async-start | bytes 131072 | tf_op jit(solution)/shard_map/all_to_all | solution.py:180
  15.2 17.9 %collective-permute-start.16 = (bf16[160,1024]{1,0:T(8,128)(2,1)}, bf16[160,1024]{1,0:T(8,128)(2,1)}, u32[]{:S(2)}, u32[]{:S(2)}) collective-permute-start(bf16[160,1024]{1,0:T(8,128)(2,1)} %get-tuple-element.91.rest_8_), channel_id=1, source_target_pairs={{0,4},{1,5},{2,6},{3,7},{4,0},{5,1},{6,2},{7,3},{8,12},{9,13},{10,... | collective-permute-start | bytes 983048 | tf_op jit(solution)/shard_map/ppermute | solution.py:95
  23.1 19.8 %collective-permute-start.4 = (bf16[128,1024]{1,0:T(8,128)(2,1)}, bf16[128,1024]{1,0:T(8,128)(2,1)S(1)}, u32[]{:S(2)}, u32[]{:S(2)}) collective-permute-start(bf16[128,1024]{1,0:T(8,128)(2,1)} %x.3), channel_id=1, source_target_pairs={{0,16},{1,17},{2,18},{3,19},{4,20},{5,21},{6,22},{7,23},{8,24},{9,... | collective-permute-start | bytes 786440 | tf_op jit(solution)/shard_map/ppermute | solution.py:92
  26.8 17.8 %collective-permute-start.5 = (bf16[128,1024]{1,0:T(8,128)(2,1)}, bf16[128,1024]{1,0:T(8,128)(2,1)S(1)}, u32[]{:S(2)}, u32[]{:S(2)}) collective-permute-start(bf16[128,1024]{1,0:T(8,128)(2,1)} %x.3), channel_id=1, source_target_pairs={{0,24},{1,25},{2,26},{3,27},{4,28},{5,29},{6,30},{7,31},{8,0},{9,1... | collective-permute-start | bytes 786440 | tf_op jit(solution)/shard_map/ppermute | solution.py:92
  34.8 21.3 %collective-permute-start.9 = (bf16[4,32,1792]{2,1,0:T(8,128)(2,1)S(1)}, bf16[4,32,1792]{2,1,0:T(8,128)(2,1)S(1)}, u32[]{:S(2)}, u32[]{:S(2)}) collective-permute-start(bf16[4,32,1792]{2,1,0:T(8,128)(2,1)S(1)} %bitcast.24), channel_id=1, source_target_pairs={{0,4},{1,5},{2,6},{3,7},{4,0},{5,1},{6,2},{7,3},{8,12},{9,13},{10,... | collective-permute-start | bytes 1376264 | tf_op jit(solution)/shard_map/ppermute | solution.py:95
  36.8 19.2 %collective-permute-start.11 = (bf16[4,32,1792]{2,1,0:T(8,128)(2,1)S(1)}, bf16[4,32,1792]{2,1,0:T(8,128)(2,1)}, u32[]{:S(2)}, u32[]{:S(2)}) collective-permute-start(bf16[4,32,1792]{2,1,0:T(8,128)(2,1)S(1)} %bitcast.25), channel_id=1, source_target_pairs={{0,6},{1,7},{2,4},{3,5},{4,2},{5,3},{6,0},{7,1},{8,14},{9,15},{10,... | collective-permute-start | bytes 1376264 | tf_op jit(solution)/shard_map/ppermute | solution.py:95
  59.1 24.7 %collective-permute-start.23 = (bf16[128,1024]{1,0:T(8,128)(2,1)}, bf16[128,1024]{1,0:T(8,128)(2,1)S(1)}, u32[]{:S(2)}, u32[]{:S(2)}) collective-permute-start(bf16[128,1024]{1,0:T(8,128)(2,1)} %g0.1), channel_id=1, source_target_pairs={{0,8},{1,9},{2,10},{3,11},{4,12},{5,13},{6,14},{7,15},{8,16},{9,17... | collective-permute-start | bytes 786440 | tf_op jit(solution)/shard_map/ppermute | solution.py:92
  60.7 23.1 %collective-permute-start.24 = (bf16[128,1024]{1,0:T(8,128)(2,1)}, bf16[128,1024]{1,0:T(8,128)(2,1)S(1)}, u32[]{:S(2)}, u32[]{:S(2)}) collective-permute-start(bf16[128,1024]{1,0:T(8,128)(2,1)} %g0.1), channel_id=1, source_target_pairs={{0,16},{1,17},{2,18},{3,19},{4,20},{5,21},{6,22},{7,23},{8,24},{9,... | collective-permute-start | bytes 786440 | tf_op jit(solution)/shard_map/ppermute | solution.py:92
  63.0 20.8 %collective-permute-start.25 = (bf16[128,1024]{1,0:T(8,128)(2,1)}, bf16[128,1024]{1,0:T(8,128)(2,1)S(1)}, u32[]{:S(2)}, u32[]{:S(2)}) collective-permute-start(bf16[128,1024]{1,0:T(8,128)(2,1)} %g0.1), channel_id=1, source_target_pairs={{0,24},{1,25},{2,26},{3,27},{4,28},{5,29},{6,30},{7,31},{8,0},{9,1... | collective-permute-start | bytes 786440 | tf_op jit(solution)/shard_map/ppermute | solution.py:92
  102.9 18.2 %collective-permute-start.21 = (bf16[128,1024]{1,0:T(8,128)(2,1)S(1)}, bf16[128,1024]{1,0:T(8,128)(2,1)S(1)}, u32[]{:S(2)}, u32[]{:S(2)}) collective-permute-start(bf16[128,1024]{1,0:T(8,128)(2,1)S(1)} %get-tuple-element.94), channel_id=1, source_target_pairs={{0,16},{1,17},{2,18},{3,19},{4,20},{5,21},{6,22},{7,23},{8,24},{9,... | collective-permute-start | bytes 786440 | tf_op jit(solution)/shard_map/ppermute | solution.py:92
  104.4 18.9 %collective-permute-start.30 = (bf16[128,1024]{1,0:T(8,128)(2,1)S(1)}, bf16[128,1024]{1,0:T(8,128)(2,1)S(1)}, u32[]{:S(2)}, u32[]{:S(2)}) collective-permute-start(bf16[128,1024]{1,0:T(8,128)(2,1)S(1)} %get-tuple-element.122), channel_id=1, source_target_pairs={{0,2},{1,3},{2,0},{3,1},{4,6},{5,7},{6,4},{7,5},{8,10},{9,11},{10,... | collective-permute-start | bytes 786440 | tf_op jit(solution)/shard_map/ppermute | solution.py:95
  107.1 44.9 %collective-permute-start.37 = (bf16[256,1024]{1,0:T(8,128)(2,1)}, bf16[256,1024]{1,0:T(8,128)(2,1)}, u32[]{:S(2)}, u32[]{:S(2)}) collective-permute-start(bf16[256,1024]{1,0:T(8,128)(2,1)} %get-tuple-element.134), channel_id=1, source_target_pairs={{0,2},{1,3},{2,0},{3,1},{4,6},{5,7},{6,4},{7,5},{8,10},{9,11},{10,... | collective-permute-start | bytes 1572872 | tf_op jit(solution)/shard_map/ppermute | solution.py:95
  108.2 43.8 %collective-permute-start.38 = (bf16[256,1024]{1,0:T(8,128)(2,1)}, bf16[256,1024]{1,0:T(8,128)(2,1)}, u32[]{:S(2)}, u32[]{:S(2)}) collective-permute-start(bf16[256,1024]{1,0:T(8,128)(2,1)} %get-tuple-element.135), channel_id=1, source_target_pairs={{0,4},{1,5},{2,6},{3,7},{4,0},{5,1},{6,2},{7,3},{8,12},{9,13},{10,... | collective-permute-start | bytes 1572872 | tf_op jit(solution)/shard_map/ppermute | solution.py:95
  109.7 47.5 %collective-permute-start.39 = (bf16[256,1024]{1,0:T(8,128)(2,1)}, bf16[256,1024]{1,0:T(8,128)(2,1)}, u32[]{:S(2)}, u32[]{:S(2)}) collective-permute-start(bf16[256,1024]{1,0:T(8,128)(2,1)} %get-tuple-element.136), channel_id=1, source_target_pairs={{0,6},{1,7},{2,4},{3,5},{4,2},{5,3},{6,0},{7,1},{8,14},{9,15},{10,... | collective-permute-start | bytes 1572872 | tf_op jit(solution)/shard_map/ppermute | solution.py:95
  121.8 25.6 %collective-permute-start.31 = (bf16[128,1024]{1,0:T(8,128)(2,1)}, bf16[128,1024]{1,0:T(8,128)(2,1)S(1)}, u32[]{:S(2)}, u32[]{:S(2)}) collective-permute-start(bf16[128,1024]{1,0:T(8,128)(2,1)} %get-tuple-element.123), channel_id=1, source_target_pairs={{0,4},{1,5},{2,6},{3,7},{4,0},{5,1},{6,2},{7,3},{8,12},{9,13},{10,... | collective-permute-start | bytes 786440 | tf_op jit(solution)/shard_map/ppermute | solution.py:95
  123.3 24.9 %collective-permute-start.32 = (bf16[128,1024]{1,0:T(8,128)(2,1)}, bf16[128,1024]{1,0:T(8,128)(2,1)}, u32[]{:S(2)}, u32[]{:S(2)}) collective-permute-start(bf16[128,1024]{1,0:T(8,128)(2,1)} %get-tuple-element.124), channel_id=1, source_target_pairs={{0,6},{1,7},{2,4},{3,5},{4,2},{5,3},{6,0},{7,1},{8,14},{9,15},{10,... | collective-permute-start | bytes 786440 | tf_op jit(solution)/shard_map/ppermute | solution.py:95
  132.5 21.0 %all-to-all-start.1 = ((f32[32,8,128]{2,1,0:T(8,128)}), f32[32,8,128]{2,1,0:T(8,128)}, u32[]{:S(2)}, u32[]{:S(2)}) async-start(f32[32,8,128]{2,1,0:T(8,128)} %get-tuple-element.129), calls=%async_computation.1 | async-start | bytes 262144 | tf_op jit(solution)/shard_map/all_to_all | solution.py:557
  148.2 17.5 %collective-permute-start.26 = (bf16[128,1024]{1,0:T(8,128)(2,1)}, bf16[128,1024]{1,0:T(8,128)(2,1)}, u32[]{:S(2)}, u32[]{:S(2)}) collective-permute-start(bf16[128,1024]{1,0:T(8,128)(2,1)} %copy-done.25), channel_id=1, source_target_pairs={{0,24},{1,25},{2,26},{3,27},{4,28},{5,29},{6,30},{7,31},{8,0},{9,1... | collective-permute-start | bytes 786440 | tf_op jit(solution)/shard_map/ppermute | solution.py:92
  151.9 30.4 %collective-permute-start.27 = (bf16[128,1024]{1,0:T(8,128)(2,1)}, bf16[128,1024]{1,0:T(8,128)(2,1)}, u32[]{:S(2)}, u32[]{:S(2)}) collective-permute-start(bf16[128,1024]{1,0:T(8,128)(2,1)} %copy-done.24), channel_id=1, source_target_pairs={{0,16},{1,17},{2,18},{3,19},{4,20},{5,21},{6,22},{7,23},{8,24},{9,... | collective-permute-start | bytes 786440 | tf_op jit(solution)/shard_map/ppermute | solution.py:92
  151.9 30.4 %collective-permute-start.28 = (bf16[128,1024]{1,0:T(8,128)(2,1)}, bf16[128,1024]{1,0:T(8,128)(2,1)}, u32[]{:S(2)}, u32[]{:S(2)}) collective-permute-start(bf16[128,1024]{1,0:T(8,128)(2,1)} %copy-done.23), channel_id=1, source_target_pairs={{0,8},{1,9},{2,10},{3,11},{4,12},{5,13},{6,14},{7,15},{8,16},{9,17... | collective-permute-start | bytes 786440 | tf_op jit(solution)/shard_map/ppermute | solution.py:92
  157.2 25.2 %collective-permute-start.33 = (bf16[32,768]{1,0:T(8,128)(2,1)S(1)}, bf16[32,768]{1,0:T(8,128)(2,1)S(1)}, u32[]{:S(2)}, u32[]{:S(2)}) collective-permute-start(bf16[32,768]{1,0:T(8,128)(2,1)S(1)} %get-tuple-element.126), channel_id=1, source_target_pairs={{0,8},{1,9},{2,10},{3,11},{4,12},{5,13},{6,14},{7,15},{8,16},{9,17... | collective-permute-start | bytes 147464 | tf_op jit(solution)/shard_map/ppermute | solution.py:92
  162.3 29.9 %collective-permute-start.34 = (bf16[32,768]{1,0:T(8,128)(2,1)S(1)}, bf16[32,768]{1,0:T(8,128)(2,1)S(1)}, u32[]{:S(2)}, u32[]{:S(2)}) collective-permute-start(bf16[32,768]{1,0:T(8,128)(2,1)S(1)} %get-tuple-element.127), channel_id=1, source_target_pairs={{0,16},{1,17},{2,18},{3,19},{4,20},{5,21},{6,22},{7,23},{8,24},{9,... | collective-permute-start | bytes 147464 | tf_op jit(solution)/shard_map/ppermute | solution.py:92
  165.7 26.5 %collective-permute-start.35 = (bf16[32,768]{1,0:T(8,128)(2,1)S(1)}, bf16[32,768]{1,0:T(8,128)(2,1)S(1)}, u32[]{:S(2)}, u32[]{:S(2)}) collective-permute-start(bf16[32,768]{1,0:T(8,128)(2,1)S(1)} %get-tuple-element.128), channel_id=1, source_target_pairs={{0,24},{1,25},{2,26},{3,27},{4,28},{5,29},{6,30},{7,31},{8,0},{9,1... | collective-permute-start | bytes 147464 | tf_op jit(solution)/shard_map/ppermute | solution.py:92
  (50 other events, 733.7 us)
where the time goes:
time: 196 us; the launch traced here: 195 us
  starting transfers between devices  63.4 us (32%)
  waiting for transfers between devices  58.3 us (30%)
  Pallas kernels  52.8 us (27%)
  local copies, waits for them, and re-layouts  14.5 us (7%)
  other arithmetic  5.33 us (3%)
    pallas_call x14, Pallas kernels, call(): pl.pallas_call(body, out_shape=tuple(outs), in_specs=[pl.BlockSpec(memory...  52.8 us
    ppermute x21, starting transfers between devices, shift(): lax.ppermute(v, 'dp', [(b * R + r, (b + k) % NB * R + r) for b in range(N...  36.4 us
    ppermute x21, waiting for transfers between devices, shift(): lax.ppermute(v, 'dp', [(b * R + r, (b + k) % NB * R + r) for b in range(N...  32.2 us
    ppermute x22, waiting for transfers between devices, swap(): return lax.ppermute(v, 'dp', [(d, d ^ mask) for d in range(n)])  26.2 us
    ppermute x22, starting transfers between devices, swap(): return lax.ppermute(v, 'dp', [(d, d ^ mask) for d in range(n)])  18.6 us
    unnamed x59, local copies, waits for them, and re-layouts  12.5 us
    all_to_all x1, starting transfers between devices, on_device(): small_back = lax.all_to_all(small_grads, 'dp', 0, 0, tiled=True)  4.2 us
    all_to_all x1, starting transfers between devices, on_device(): small_in = lax.all_to_all(small_out, 'dp', 0, 0, tiled=True)  4.13 us
  transfers between devices with their start and end apart: 45, of which 9 were waited for; matrix products, arithmetic and copies ran while one was open for 3% of the time, Pallas kernels for 22%

commit v1 on v0

--- a/solution.py
+++ b/solution.py
@@ -32,11 +32,11 @@
     return lax.broadcasted_iota(I32, shape, axis)
 
 
-def call(body, ins, outs, scratch=(), flops=0, extra=4 << 20, hbm=()):
+def call(body, ins, outs, scratch=(), flops=0, extra=4 << 20, hbm=(), alias=None):
     spaces = {"v": pltpu.VMEM, "s": pltpu.SMEM, "a": pl.ANY}
     arrays = [a for _, a in ins]
     nbytes = sum(a.size * a.dtype.itemsize for a in arrays) + sum(math.prod(o.shape) * o.dtype.itemsize for o in outs)
-    room = sum(math.prod(t.shape) * jnp.dtype(t.dtype).itemsize for t in scratch if t.memory_space == pltpu.VMEM)
+    room = sum(math.prod(t.shape) * jnp.dtype(t.dtype).itemsize for t in scratch if getattr(t, "memory_space", None) == pltpu.VMEM)
     room += sum(a.size * a.dtype.itemsize for s, a in ins if s == "v") + sum(math.prod(o.shape) * o.dtype.itemsize for i, o in enumerate(outs) if i not in hbm)
     return pl.pallas_call(
         body,
@@ -44,6 +44,7 @@
         in_specs=[pl.BlockSpec(memory_space=spaces[s]) for s, _ in ins],
         out_specs=tuple(pl.BlockSpec(memory_space=pltpu.HBM if i in hbm else pltpu.VMEM) for i in range(len(outs))),
         scratch_shapes=list(scratch),
+        input_output_aliases=alias or {},
         compiler_params=pltpu.CompilerParams(vmem_limit_bytes=int(room * 1.02) + extra),
         cost_estimate=pl.CostEstimate(flops=int(flops), bytes_accessed=int(nbytes), transcendentals=0),
     )(*arrays)
@@ -87,20 +88,24 @@
     R = n // NB
     assert R * NB == n and R & (R - 1) == 0
 
-    def shift(v, k):
-        k = k % NB
-        return lax.ppermute(v, "dp", [(b * R + r, (b + k) % NB * R + r) for b in range(NB) for r in range(R)])
+    def across(v, mask):
+        return lax.ppermute(v, "dp", [(d, d ^ (mask * R)) for d in range(n)])
 
     def swap(v, mask):
         return lax.ppermute(v, "dp", [(d, d ^ mask) for d in range(n)])
 
     def gather_r(own):
-        got = {0: own}
-        for m in range(2, R, 2):
-            got[m] = swap(own, m)
-        for m in range(0, R, 2):
-            got[m + 1] = swap(got[m], 1)
-        return [got[m] for m in range(R)]
+        half = own.shape[0] // 2
+        got = [(0, 0, own)]
+        if R == 8:
+            from_x, from_y = swap(own, 2), swap(own, 4)
+            got += [(2, 0, from_x), (4, 0, from_y)]
+            got.append((6, 0, swap(from_y[:half], 2)))
+            got.append((6, half, swap(from_x[half:], 4)))
+        else:
+            for m in range(2, R, 2):
+                got.append((m, 0, swap(own, m)))
+        return got + [(m + 1, at, swap(v, 1)) for m, at, v in got]
 
     def on_device(
         block_in, grad_out, w_qkv, b_qkv, w_o, b_o, w_in, b_in, w_out, b_out,
@@ -115,12 +120,13 @@
         J = R // 2
         MF = NB * rows + ff_dev
         MA = NB * rows
+        MS = MA + 8
         idx = lax.axis_index("dp").astype(I32)
         b, r = idx // R, idx % R
         br = jnp.stack([b, r])
 
         slots1 = jnp.arange(T, dtype=I32)
-        owners = [(b - k) % NB * R + r for k in range(NB)]
+        owners = [(b ^ k) * R + r for k in range(NB)]
         device = jnp.concatenate([jnp.full((T,), o, I32) for o in owners])
         slots = jnp.tile(slots1, NB)
         count = seq_lens.shape[0]
@@ -152,7 +158,7 @@
         def pack_body(br, qkv_ref, in_ref, o_ref, out_ref, *rest):
             vectors, outs = rest[: len(small)], rest[len(small) :]
             for k in range(NB):
-                to = lax.rem(br[0] + k, NB)
+                to = br[0] ^ k
                 for s in range(3):
                     outs[k][:, s * QB : (s + 1) * QB] = qkv_ref[:, lanes(s * NB + to, QB)]
                 outs[k][:, 3 * QB :] = in_ref[:, lanes(to, FB)]
@@ -172,14 +178,18 @@
         )
         columns, own_two, small_out = packed[:NB], packed[NB], packed[NB + 1]
 
-        mine = jnp.concatenate([columns[0]] + [shift(columns[k], k) for k in range(1, NB)]).reshape(NB, rows, W1)
+        def blocks_of(own, after):
+            two = across(after, 2)
+            return [own, across(after, 1), two, across(two, 1)]
+
+        mine = jnp.concatenate([columns[0]] + [across(columns[k], k) for k in range(1, NB)]).reshape(NB, rows, W1)
         two = gather_r(own_two)
         one = gather_r(mine)
         after, _ = lax.optimization_barrier((block_in, mine))
-        tokens = [block_in] + [shift(after, k) for k in range(1, NB)]
+        tokens = blocks_of(block_in, after)
         small_in = lax.all_to_all(small_out, "dp", 0, 0, tiled=True)
-        after, _ = lax.optimization_barrier((grad_out, tokens))
-        grads_in = [grad_out] + [shift(after, k) for k in range(1, NB)]
+        after, _ = lax.optimization_barrier((grad_out, tokens[1]))
+        grads_in = blocks_of(grad_out, after)
 
         def pick(width_mod, off, base, width):
             return (iota((width, width_mod.shape[1]), 0) + base == off + width_mod).astype(BF)
@@ -210,36 +220,39 @@
             dec_body, [("s", br), ("v", small_in)], [sds((1, 3 * QB), F32), sds((1, FB), F32)] + [row] * 5
         )
 
-        def load_one(br, pieces, w1, sems):
+        def load_one(br, parts, w1, sems):
             copies = []
-            for m in range(R):
-                for k in range(NB):
-                    copies.append(
-                        pltpu.make_async_copy(
-                            pieces[m].at[k], w1.at[lax.rem(br[0] + (NB - k), NB), br[1] ^ m], sems.at[m * NB + k]
+            for (m, start, _), ref in zip(one, parts):
+                for k in range(ref.shape[0]):
+                    sem = sems.at[len(copies)]
+                    copies.append(pltpu.make_async_copy(ref.at[k], w1.at[br[0] ^ (start + k), br[1] ^ m], sem))
+            return copies
+
+        def load_two(br, parts, wout, wo, sems):
+            copies = []
+            for (m, start, _), ref in zip(two, parts):
+                size = ref.shape[0]
+                for to, first, last in ((wout, 0, ff_dev), (wo, ff_dev, ff_dev + rows)):
+                    low, high = max(start, first), min(start + size, last)
+                    if low < high:
+                        copies.append(
+                            pltpu.make_async_copy(
+                                ref.at[pl.ds(low - start, high - low)],
+                                to.at[br[1] ^ m, pl.ds(low - first, high - low)],
+                                sems.at[len(copies)],
+                            )
                         )
-                    )
             return copies
-
-        def load_out(br, pieces, wout, sems):
-            return [
-                pltpu.make_async_copy(pieces[m].at[pl.ds(0, ff_dev)], wout.at[br[1] ^ m], sems.at[m]) for m in range(R)
-            ]
-
-        def load_o(br, pieces, wo, sems):
-            return [
-                pltpu.make_async_copy(pieces[m].at[pl.ds(ff_dev, rows)], wo.at[br[1] ^ m], sems.at[m]) for m in range(R)
-            ]
 
         dma = pltpu.SemaphoreType.DMA
         PAIRS = QB // 128
 
         def fwd_body(br, x0, x1, x2, x3, cos, sin, mask_ref, bq, bi, g1, s1, g2, s2, *rest):
-            one, two, rest = rest[:R], rest[R : 2 * R], rest[2 * R :]
-            act1, act2, q, k, v, probs, mixed, hidden, dgelu, xhat_ref, w1, wo, wout, own, p1h, p2h, p3h = rest[:17]
-            p1, p2, p3, sem1, semo, semout, semp = rest[17:]
-            c1, co, cout = load_one(br, one, w1, sem1), load_o(br, two, wo, semo), load_out(br, two, wout, semout)
-            for c in c1 + co + cout:
+            one_refs, two_refs, rest = rest[: len(one)], rest[len(one) : len(one) + len(two)], rest[len(one) + len(two) :]
+            act1, act2, q, k, v, probs, mixed, hidden, dgelu, xhat_ref, w1, wo, wout, own, later, away = rest[:16]
+            stage, sem1, sem2, semp = rest[16:]
+            c1, c2 = load_one(br, one_refs, w1, sem1), load_two(br, two_refs, wout, wo, sem2)
+            for c in c1 + c2:
                 c.start()
             for i, x in enumerate((x0, x1, x2, x3)):
 
@@ -298,7 +311,7 @@
                 return carry
 
             lax.fori_loop(0, FB // 256, feed, 0)
-            for c in co + cout:
+            for c in c2:
                 c.wait()
 
             def project_out(t, carry):
@@ -306,46 +319,52 @@
                 y = dot_nn(mixed[...], wo[:, :, cols].reshape(QB, 256))
                 y = y + dot_nn(hidden[...], wout[:, :, cols].reshape(FB, 256))
                 own[:, cols] = y[:T]
-                for i, ref in enumerate((p1, p2, p3)):
-                    ref[:, cols] = y[(i + 1) * T : (i + 2) * T].astype(BF)
+                later[:, cols] = y[2 * T : 3 * T]
+                stage[:T, cols] = y[T : 2 * T].astype(BF)
+                stage[T:, cols] = y[3 * T :].astype(BF)
                 return carry
 
             lax.fori_loop(0, D // 256, project_out, 0)
-            sends = [pltpu.make_async_copy(a, z, semp.at[i]) for i, (a, z) in enumerate(((p1, p1h), (p2, p2h), (p3, p3h)))]
-            for c in sends:
-                c.start()
-            for c in sends:
-                c.wait()
+            send = pltpu.make_async_copy(stage, away, semp)
+            send.start()
+            send.wait()
 
         tab = sds((NT, D), BF)
         third = sds((NT, QB), BF)
         block = sds((T, D), BF)
-        act1, act2, q, k, v, probs, mixed, hidden, dgelu, xhat, full_one, full_o, full_out, own_part, *parts = call(
+        act1, act2, q, k, v, probs, mixed, hidden, dgelu, xhat, full_one, full_o, full_out, own_part, later_part, away_part = call(
             fwd_body,
             [("s", br)] + [("v", x) for x in tokens]
             + [("v", a) for a in (cosine, sines, mask, bias_qkv, bias_in, gain_one, shift_one, gain_two, shift_two)]
-            + [("a", a) for a in one + two],
+            + [("a", a) for _, _, a in one + two],
             [tab, tab, third, third, third, sds((NB * PAIRS, 2 * T, T), F32), third, sds((NT, FB), BF), sds((NT, FB), F32),
              sds((NT, D), F32), sds((NB, R, rows, W1), BF), sds((R, rows, D), BF), sds((R, ff_dev, D), BF),
-             sds((T, D), F32), block, block, block],
-            [pltpu.VMEM((T, D), BF)] * 3 + [dma((R * NB,)), dma((R,)), dma((R,)), dma((3,))], hbm=(14, 15, 16),
+             sds((T, D), F32), sds((T, D), F32), sds((2 * T, D), BF)],
+            [pltpu.VMEM((2 * T, D), BF), dma((R * NB,)), dma((3 * R,)), dma], hbm=(15,),
             flops=2 * NT * D * W1 + 2 * NT * D * (QB + FB) + 8 * NT * T * QB,
         )
 
-        returned = [shift(parts[k - 1], -k) for k in range(1, NB)]
-
-        def total_body(x, live_ref, bo, own, p1, p2, p3, out):
+        got_one = across(away_part, 1)
+
+        def pass_body(keep, got, out):
             def fn(rws):
-                y = x[rws].astype(F32) + bo[...] + own[rws]
-                for ref in (p1, p2, p3):
-                    y = y + ref[rws].astype(F32)
+                out[rws] = (keep[rws] + got[pl.ds(T, T)].astype(F32)).astype(BF)
+
+            by_rows(T, T, fn)
+
+        (pass_part,) = call(pass_body, [("v", later_part), ("v", got_one)], [block])
+        got_two = across(pass_part, 2)
+
+        def total_body(x, live_ref, bo, own, p1, p2, out):
+            def fn(rws):
+                y = x[rws].astype(F32) + bo[...] + own[rws] + p1[rws].astype(F32) + p2[rws].astype(F32)
                 out[rws] = (y * live_ref[rws]).astype(BF)
 
-            by_rows(T, 32, fn)
+            by_rows(T, T, fn)
 
         (block_out,) = call(
             total_body,
-            [("v", a) for a in (block_in, live[:T], bias_o, own_part, *returned)], [block],
+            [("v", a) for a in (block_in, live[:T], bias_o, own_part, got_one, got_two)], [block],
         )
 
         def bwd1_body(br, live_ref, g0, g1, g2, g3, act2, hidden, dgelu, wout, *rest):
@@ -463,7 +482,7 @@
         dqkv, keep_a, send_a, sum_qkv = call(
             bwd2_body,
             [("s", br)] + [("v", a) for a in (grad_r, mixed, act1, q, k, v, probs, cosine, sines, full_o)],
-            [sds((NT, 3 * QB), BF), sds((J, MA, D), F32), sds((J, MA, D), BF), sds((1, 3 * QB), F32)],
+            [sds((NT, 3 * QB), BF), sds((J, MS, D), F32), sds((J, MS, D), BF), sds((1, 3 * QB), F32)],
             [pltpu.VMEM((NT, QB), BF), pltpu.VMEM((R, rows, 3 * QB), F32), pltpu.VMEM((R, rows, D), F32),
              pltpu.VMEM((256, NT), BF)],
             flops=2 * NT * D * (3 * QB + 2 * QB) + 16 * NT * T * QB,
@@ -477,7 +496,7 @@
                     y = keep[j, rws] + got[j, rws].astype(F32)
                     outs[j][rws] = y if j == 0 else y.astype(BF)
 
-                by_rows(size, 32, fn)
+                by_rows(size, size, fn)
 
         def merge(keep, send):
             size = keep.shape[1]
@@ -486,14 +505,12 @@
             return [outs[0]] + [swap(outs[j], 2 * j) for j in range(1, J)]
 
         merged_f = merge(keep_f, send_f)
-        merged_a = merge(keep_a, send_a)
-
         out_widths = [FB * NB // n, 3 * D // n] + [D // n] * 5
         out_offsets = [sum(out_widths[:i]) for i in range(len(out_widths))]
         WO = -(-sum(out_widths) // 128) * 128
 
-        def bwd3_body(br, xhat, w1, dqkv, dhid, grad, sum_in, sum_qkv, g1, g2, *rest):
-            own, p1h, p2h, p3h, small, p1, p2, p3, gs, sums, semp = rest
+        def bwd3_body(br, xhat, w1, dqkv, dhid, grad, sum_in, sum_qkv, g1, g2, keep_in, send_in, *rest):
+            own, p1h, p2h, p3h, keep, send, p1, p2, p3, gs, sums, tot, semp = rest
             gs[...] = jnp.sum(grad[:T].astype(F32), axis=0, keepdims=True)
 
             def back(t, carry):
@@ -541,20 +558,25 @@
             total = place(total, gs[...], whole, 2)
             for i in range(4):
                 total = place(total, sums[i : i + 1], whole, 3 + i)
-            for i in range(8):
-                small[:, i] = total[:, i * 128 : (i + 1) * 128] if (i + 1) * 128 <= WO else jnp.zeros((n, 128), F32)
+            tot[...] = total
+            for j in range(J):
+                for ref, m in ((keep, 2 * j), (send, 2 * j + 1)):
+                    lines = [tot[pl.ds(to * R + (br[1] ^ m), 1), :] for to in range(NB)]
+                    lines.append(jnp.zeros((MS - MA - NB, WO), F32))
+                    ref[j, MA:, :WO] = jnp.concatenate(lines, axis=0).astype(ref.dtype)
             for c in sends:
                 c.wait()
 
-        own_g, g_1, g_2, g_3, small_grads = call(
+        own_g, g_1, g_2, g_3, keep_a, send_a = call(
             bwd3_body,
-            [("s", br)] + [("v", a) for a in (xhat, full_one, dqkv, dhid, grad_r, sum_in, sum_qkv, gain_one, gain_two)],
-            [sds((T, D), F32), block, block, block, sds((n, 8, 128), F32)],
-            [pltpu.VMEM((T, D), BF)] * 3 + [pltpu.VMEM((1, D), F32), pltpu.VMEM((8, D), F32), dma((3,))], hbm=(1, 2, 3),
+            [("s", br)] + [("v", a) for a in (xhat, full_one, dqkv, dhid, grad_r, sum_in, sum_qkv, gain_one, gain_two, keep_a, send_a)],
+            [sds((T, D), F32), block, block, block, sds((J, MS, D), F32), sds((J, MS, D), BF)],
+            [pltpu.VMEM((T, D), BF)] * 3 + [pltpu.VMEM((1, D), F32), pltpu.VMEM((8, D), F32), pltpu.VMEM((n, WO), F32), dma((3,))], hbm=(1, 2, 3),
+            alias={10: 4, 11: 5},
             flops=2 * NT * D * W1,
         )
-        g_back = [shift(g, -k) for k, g in ((1, g_1), (2, g_2), (3, g_3))]
-        small_back = lax.all_to_all(small_grads, "dp", 0, 0, tiled=True)
+        g_back = [across(g, k) for k, g in ((1, g_1), (2, g_2), (3, g_3))]
+        merged_a = merge(keep_a, send_a)
 
         def input_body(x, grad, own, p1, p2, p3, out):
             def fn(rws):
@@ -567,7 +589,7 @@
                 mean_gx = jnp.mean(g * xh, axis=-1, keepdims=True)
                 out[rws] = (grad[rws].astype(F32) + rstd * (g - mean_g - xh * mean_gx)).astype(BF)
 
-            by_rows(T, 32, fn)
+            by_rows(T, T, fn)
 
         (grad_input,) = call(input_body, [("v", a) for a in (block_in, grad_r[:T], own_g, *g_back)], [block])
 
@@ -582,7 +604,7 @@
 
             by_rows(ff_dev, min(32, ff_dev), out_rows)
             for k, ref in enumerate((z0, z1, z2, z3)):
-                at = pl.ds(pl.multiple_of(lax.rem(br[0] + k, NB) * rows, rows), rows)
+                at = pl.ds(pl.multiple_of((br[0] ^ k) * rows, rows), rows)
                 y = got[0][at]
                 for other in got[1:]:
                     y = y + other[at].astype(F32)
@@ -601,34 +623,44 @@
                     y = y + other[c * rows : (c + 1) * rows, 3 * QB :].astype(F32)
                 w_o_ref[:, c * QB : (c + 1) * QB] = y
             for k, ref in enumerate((z0, z1, z2, z3)):
-                at = pl.ds(pl.multiple_of(lax.rem(br[0] + k, NB) * rows, rows), rows)
+                at = pl.ds(pl.multiple_of((br[0] ^ k) * rows, rows), rows)
                 y = got[0][at, : 3 * QB]
                 for other in got[1:]:
                     y = y + other[at, : 3 * QB].astype(F32)
-                ref[...] = y if k == 0 else y.astype(BF)
+                ref[:rows] = y if k == 0 else y.astype(BF)
+                y = got[0][MA:, :WO]
+                for other in got[1:]:
+                    y = y + other[MA:, :WO].astype(F32)
+                y = jnp.sum(jnp.where(iota(y.shape, 0) == (br[0] ^ k), y, 0.0), axis=0, keepdims=True)
+                ref[rows:, :WO] = jnp.broadcast_to(y, (8, WO)).astype(ref.dtype)
 
         grad_w_o, za0, *za = call(
             plane_a_body, [("s", br)] + [("v", a) for a in merged_a],
-            [sds((rows, D), F32), sds((rows, 3 * QB), F32)] + [sds((rows, 3 * QB), BF)] * 3,
-        )
-        zf = [zf0] + [shift(z, k + 1) for k, z in enumerate(zf)]
-        za = [za0] + [shift(z, k + 1) for k, z in enumerate(za)]
+            [sds((rows, D), F32), sds((rows + 8, 3 * QB), F32)] + [sds((rows + 8, 3 * QB), BF)] * 3,
+        )
+        zf = [zf0] + [across(z, k + 1) for k, z in enumerate(zf)]
+        za = [za0] + [across(z, k + 1) for k, z in enumerate(za)]
 
         def place_f_body(br, z0, z1, z2, z3, out):
             for k, ref in enumerate((z0, z1, z2, z3)):
-                out[:, lanes(lax.rem(br[0] + (NB - k), NB), FB)] = ref[...].astype(F32)
-
-        def place_a_body(br, z0, z1, z2, z3, out):
+                out[:, lanes(br[0] ^ k, FB)] = ref[...].astype(F32)
+
+        def place_a_body(br, z0, z1, z2, z3, out, *small):
+            y = sum(ref[rows:, :WO].astype(F32) for ref in (z0, z1, z2, z3))
+            for ref, at, width in zip(small, out_offsets, out_widths):
+                ref[...] = y[:1, at : at + width]
             for k, ref in enumerate((z0, z1, z2, z3)):
-                at = lax.rem(br[0] + (NB - k), NB)
+                at = br[0] ^ k
                 for s in range(3):
-                    out[:, lanes(s * NB + at, QB)] = ref[:, s * QB : (s + 1) * QB].astype(F32)
+                    out[:, lanes(s * NB + at, QB)] = ref[:rows, s * QB : (s + 1) * QB].astype(F32)
 
         (grad_w_in,) = call(place_f_body, [("s", br)] + [("v", z) for z in zf], [sds((rows, NB * FB), F32)])
-        (grad_w_qkv,) = call(place_a_body, [("s", br)] + [("v", z) for z in za], [sds((rows, 3 * D), F32)])
-
-        summed = jnp.sum(small_back, axis=0).reshape(-1)
-        outs = [summed[o : o + w] for o, w in zip(out_offsets, out_widths)]
+        grad_w_qkv, *outs = call(
+            place_a_body, [("s", br)] + [("v", z) for z in za],
+            [sds((rows, 3 * D), F32)] + [sds((1, w), F32) for w in out_widths],
+        )
+        outs = [o.reshape(-1) for o in outs]
+
         grad_b_in, grad_b_qkv, grad_b, grad_g1, grad_s1, grad_g2, grad_s2 = outs
         return (
             block_out, grad_input, grad_w_qkv, grad_b_qkv, grad_w_o, grad_b, grad_w_in, grad_b_in,

time: 196 us -> 212 us (1.082)
  waiting for transfers between devices: 58.3 us -> 84.8 us
  starting transfers between devices: 63.4 us -> 54 us
  local copies, waits for them, and re-layouts: 14.5 us -> 18.7 us
  Pallas kernels: 52.8 us -> 48.6 us
    ppermute x21 -> x20, waiting for transfers between devices: 32.2 us -> 50.1 us  [across(): return lax.ppermute(v, 'dp', [(d, d ^ mask * R) for d in range(n)])]
    ppermute x22 -> x26, waiting for transfers between devices: 26.2 us -> 34.7 us  [swap(): return lax.ppermute(v, 'dp', [(d, d ^ mask) for d in range(n)])]
    unnamed x59 -> x63, local copies, waits for them, and re-layouts: 12.5 us -> 17 us
    ppermute x21 -> x20, starting transfers between devices: 36.4 us -> 32.2 us  [across(): return lax.ppermute(v, 'dp', [(d, d ^ mask * R) for d in range(n)])]
    all_to_all x1 -> x0, starting transfers between devices: 4.2 us -> none  [on_device(): small_back = lax.all_to_all(small_grads, 'dp', 0, 0, tiled=True)]
    pallas_call x14 -> x15, Pallas kernels: 52.8 us -> 48.6 us  [call(): pl.pallas_call(body, out_shape=tuple(outs), in_specs=[pl.BlockSpec(memory...]
    ppermute x22 -> x26, starting transfers between devices: 18.6 us -> 16.8 us  [swap(): return lax.ppermute(v, 'dp', [(d, d ^ mask) for d in range(n)])]
  transfers between devices with their start and end apart: 45 -> 47, of which waited for: 9 -> 14; matrix products, arithmetic and copies ran while one was open for 3% -> 2% of each run, Pallas kernels for 22% -> 18%
where the time goes in v1:
time: 212 us; the launch traced here: 211 us
  waiting for transfers between devices  84.8 us (40%)
  starting transfers between devices  54 us (25%)
  Pallas kernels  48.6 us (23%)
  local copies, waits for them, and re-layouts  18.7 us (9%)
  other arithmetic  3.67 us (2%)
    ppermute x20, waiting for transfers between devices, across(): return lax.ppermute(v, 'dp', [(d, d ^ mask * R) for d in range(n)])  50.1 us
    pallas_call x15, Pallas kernels, call(): pl.pallas_call(body, out_shape=tuple(outs), in_specs=[pl.BlockSpec(memory...  48.6 us
    ppermute x26, waiting for transfers between devices, swap(): return lax.ppermute(v, 'dp', [(d, d ^ mask) for d in range(n)])  34.7 us
    ppermute x20, starting transfers between devices, across(): return lax.ppermute(v, 'dp', [(d, d ^ mask * R) for d in range(n)])  32.2 us
    unnamed x63, local copies, waits for them, and re-layouts  17 us
    ppermute x26, starting transfers between devices, swap(): return lax.ppermute(v, 'dp', [(d, d ^ mask) for d in range(n)])  16.8 us
    all_to_all x1, starting transfers between devices, on_device(): small_in = lax.all_to_all(small_out, 'dp', 0, 0, tiled=True)  5.11 us
  transfers between devices with their start and end apart: 47, of which 14 were waited for; matrix products, arithmetic and copies ran while one was open for 2% of the time, Pallas kernels for 18%

profile of v1, /device:TPU:0, one launch (start us, length us, event | category | flops | bytes accessed | tf_op | source)
XLA Modules:
  0.0 210.9 jit_solution(1947948932370699290)
XLA Ops:
  1.3 2.1 shard_map.272
  3.4 5.1 %collective-permute-start.2 = (bf16[32,1792]{1,0:T(8,128)(2,1)}, bf16[32,1792]{1,0:T(8,128)(2,1)S(1)}, u32[]{:S(2)}, u32[]{:S(2)}) collective-permute-start(bf16[32,1792]{1,0:T(8,128)(2,1)} %get-tuple-element.91), channel_id=1, source_target_pairs={{0,24},{1,25},{2,26},{3,27},{4,28},{5,29},{6,30},{7,31},{8,16},{9,... | collective-permute-start | bytes 344072 | tf_op jit(solution)/shard_map/ppermute | solution.py:92
  12.8 5.6 %collective-permute-done.1 = bf16[32,1792]{1,0:T(8,128)(2,1)S(1)} collective-permute-done((bf16[32,1792]{1,0:T(8,128)(2,1)}, bf16[32,1792]{1,0:T(8,128)(2,1)S(1)}, u32[]{:S(2)}, u32[]{:S(2)}) %collective-permute-start.1) | collective-permute-done | bytes 114720 | tf_op jit(solution)/shard_map/ppermute | solution.py:92
  19.6 5.1 %all-to-all-start = ((bf16[32,8,128]{2,1,0:T(8,128)(2,1)}), bf16[32,8,128]{2,1,0:T(8,128)(2,1)S(1)}, u32[]{:S(2)}, u32[]{:S(2)}) async-start(bf16[32,8,128]{2,1,0:T(8,128)(2,1)} %get-tuple-element.86), calls=%async_computation | async-start | bytes 131072 | tf_op jit(solution)/shard_map/all_to_all | solution.py:190
  24.7 2.7 %collective-permute-start.4 = (bf16[128,1024]{1,0:T(8,128)(2,1)}, bf16[128,1024]{1,0:T(8,128)(2,1)}, u32[]{:S(2)}, u32[]{:S(2)}) collective-permute-start(bf16[128,1024]{1,0:T(8,128)(2,1)} %x.3), channel_id=1, source_target_pairs={{0,16},{1,17},{2,18},{3,19},{4,20},{5,21},{6,22},{7,23},{8,24},{9,... | collective-permute-start | bytes 786440 | tf_op jit(solution)/shard_map/ppermute | solution.py:92
  33.2 8.0 %collective-permute-done.4.x2 = bf16[128,1024]{1,0:T(8,128)(2,1)} collective-permute-done((bf16[128,1024]{1,0:T(8,128)(2,1)}, bf16[128,1024]{1,0:T(8,128)(2,1)}, u32[]{:S(2)}, u32[]{:S(2)}) %collective-permute-start.4) | collective-permute-done | bytes 262176 | tf_op jit(solution)/shard_map/ppermute | solution.py:92
  41.4 2.2 %collective-permute-done.17.rest_13_ = bf16[80,1024]{1,0:T(8,128)(2,1)} collective-permute-done((bf16[80,1024]{1,0:T(8,128)(2,1)S(1)}, bf16[80,1024]{1,0:T(8,128)(2,1)}, u32[]{:S(2)}, u32[]{:S(2)}) %collective-permute-start.17) | collective-permute-done | bytes 163872 | tf_op jit(solution)/shard_map/ppermute | solution.py:95
  49.9 7.4 %collective-permute-done.5.x3 = bf16[128,1024]{1,0:T(8,128)(2,1)S(1)} collective-permute-done((bf16[128,1024]{1,0:T(8,128)(2,1)}, bf16[128,1024]{1,0:T(8,128)(2,1)S(1)}, u32[]{:S(2)}, u32[]{:S(2)}) %collective-permute-start.5) | collective-permute-done | bytes 262176 | tf_op jit(solution)/shard_map/ppermute | solution.py:92
  63.6 1.8 collective-permute-done.8.rest_3_
  65.4 2.0 collective-permute-done.9.rest_4_
  78.6 16.9 %shard_map.274 = (bf16[512,1024]{1,0:T(8,128)(2,1)S(1)}, bf16[512,1024]{1,0:T(8,128)(2,1)S(1)}, bf16[512,256]{1,0:T(8,128)(2,1)S(1)}, bf16[512,256]{1,0:T(8,128)...) custom-call(s32[2]{0:T(128)S(1)} %copy-done.13, ...), custom_call_target="tpu_custom_call" | custom-call | flops 3355443200 | bytes 25451528 | tf_op jit(solution)/shard_map/pallas_call | solution.py:41
  95.6 7.6 %shard_map.277 = (bf16[512,1024]{1,0:T(8,128)(2,1)S(1)}, bf16[512,1024]{1,0:T(8,128)(2,1)S(1)}, f32[4,256,1024]{2,1,0:T(8,128)S(1)}, bf16[4,256,1024]{2,1,0:T(8,128)(2,1)S(1)}, f32[1,1024]{1,0:T(1,128)S(1)}) custom-call(s32[2]{0:T(128)S(1)} %copy-done.13, f32[512,1]{1,0:T(8,128)S(1)} %copy.37.live_ref, bf16[128,1024]{1,0:T(8,128)(2,1)S(1)} %copy-done.24, ...), custom_call_target="tpu_custom_call" | custom-call | flops 3221225472 | bytes 15734792 | tf_op jit(solution)/shard_map/pallas_call | solution.py:41
  103.2 7.1 %shard_map.278 = (bf16[512,768]{1,0:T(8,128)(2,1)S(1)}, f32[4,136,1024]{2,1,0:T(8,128)S(1)}, bf16[4,136,1024]{2,1,0:T(8,128)(2,1)S(1)}, f32[1,768]{1,0:T(1,128)S(1)}) custom-call(s32[2]{0:T(128)S(1)} %copy-done.13, bf16[512,1024]{1,0:T(8,128)(2,1)S(1)} %get-tuple-element.108.grad, bf16[512,256]{1,0:T(8,128)(2,1)S(1)} %get-tuple-element.111.mixed, ...), custom_call_target="tpu_custom_call" | custom-call | flops 1610612736 | bytes 9374728 | tf_op jit(solution)/shard_map/pallas_call | solution.py:41
  110.4 4.9 %shard_map.279 = (f32[128,1024]{1,0:T(8,128)S(1)}, bf16[128,1024]{1,0:T(8,128)(2,1)S(1)}, bf16[128,1024]{1,0:T(8,128)(2,1)S(1)}, bf16[128,1024]{1,0:T(8,128)(2,1...) custom-call(s32[2]{0:T(128)S(1)} %copy-done.13, ...), custom_call_target="tpu_custom_call", output_to_operand_aliasing={{4}: (10, {}), {5}: (11, {})} | custom-call | flops 1879048192 | bytes 16661512 | tf_op jit(solution)/shard_map/pallas_call | solution.py:41
  123.1 6.6 %collective-permute-done.24.got.p1 = bf16[256,1024]{1,0:T(8,128)(2,1)S(1)} collective-permute-done((bf16[256,1024]{1,0:T(8,128)(2,1)S(1)}, bf16[256,1024]{1,0:T(8,128)(2,1)S(1)}, u32[]{:S(2)}, u32[]{:S(2)}) %collective-permute-start.24) | collective-permute-done | bytes 524320 | tf_op jit(solution)/shard_map/ppermute | solution.py:92
  131.9 26.0 %collective-permute-done.34.rest_2_ = bf16[136,1024]{1,0:T(8,128)(2,1)S(1)} collective-permute-done((bf16[136,1024]{1,0:T(8,128)(2,1)S(1)}, bf16[136,1024]{1,0:T(8,128)(2,1)S(1)}, u32[]{:S(2)}, u32[]{:S(2)}) %collective-permute-start.34) | collective-permute-done | bytes 278560 | tf_op jit(solution)/shard_map/ppermute | solution.py:95
  158.7 3.1 %collective-permute-start.30 = (bf16[128,1024]{1,0:T(8,128)(2,1)S(1)}, bf16[128,1024]{1,0:T(8,128)(2,1)S(1)}, u32[]{:S(2)}, u32[]{:S(2)}) collective-permute-start(bf16[128,1024]{1,0:T(8,128)(2,1)S(1)} %get-tuple-element.126), channel_id=1, source_target_pairs={{0,16},{1,17},{2,18},{3,19},{4,20},{5,21},{6,22},{7,23},{8,24},{9,... | collective-permute-start | bytes 786440 | tf_op jit(solution)/shard_map/ppermute | solution.py:92
  162.3 1.7 collective-permute-start.25
  166.0 2.3 %collective-permute-start.36 = (bf16[40,768]{1,0:T(8,128)(2,1)S(1)}, bf16[40,768]{1,0:T(8,128)(2,1)S(1)}, u32[]{:S(2)}, u32[]{:S(2)}) collective-permute-start(bf16[40,768]{1,0:T(8,128)(2,1)S(1)} %get-tuple-element.135), channel_id=1, source_target_pairs={{0,8},{1,9},{2,10},{3,11},{4,12},{5,13},{6,14},{7,15},{8,0},{9,1},... | collective-permute-start | bytes 184328 | tf_op jit(solution)/shard_map/ppermute | solution.py:92
  171.2 16.4 %collective-permute-done.30.p2 = bf16[128,1024]{1,0:T(8,128)(2,1)S(1)} collective-permute-done((bf16[128,1024]{1,0:T(8,128)(2,1)S(1)}, bf16[128,1024]{1,0:T(8,128)(2,1)S(1)}, u32[]{:S(2)}, u32[]{:S(2)}) %collective-permute-start.30) | collective-permute-done | bytes 262176 | tf_op jit(solution)/shard_map/ppermute | solution.py:92
  189.5 5.1 %collective-permute-start.43 = (bf16[32,1024]{1,0:T(8,128)(2,1)}, bf16[32,1024]{1,0:T(8,128)(2,1)S(1)}, u32[]{:S(2)}, u32[]{:S(2)}) collective-permute-start(bf16[32,1024]{1,0:T(8,128)(2,1)} %get-tuple-element.149), channel_id=1, source_target_pairs={{0,8},{1,9},{2,10},{3,11},{4,12},{5,13},{6,14},{7,15},{8,0},{9,1},... | collective-permute-start | bytes 196616 | tf_op jit(solution)/shard_map/ppermute | solution.py:92
  194.5 4.2 %collective-permute-done.25.p2 = bf16[128,1024]{1,0:T(8,128)(2,1)S(1)} collective-permute-done((bf16[128,1024]{1,0:T(8,128)(2,1)S(1)}, bf16[128,1024]{1,0:T(8,128)(2,1)S(1)}, u32[]{:S(2)}, u32[]{:S(2)}) %collective-permute-start.25) | collective-permute-done | bytes 262176 | tf_op jit(solution)/shard_map/ppermute | solution.py:92
  200.0 3.1 %collective-permute-start.45 = (bf16[32,1024]{1,0:T(8,128)(2,1)}, bf16[32,1024]{1,0:T(8,128)(2,1)}, u32[]{:S(2)}, u32[]{:S(2)}) collective-permute-start(bf16[32,1024]{1,0:T(8,128)(2,1)} %get-tuple-element.151), channel_id=1, source_target_pairs={{0,24},{1,25},{2,26},{3,27},{4,28},{5,29},{6,30},{7,31},{8,16},{9,... | collective-permute-start | bytes 196616 | tf_op jit(solution)/shard_map/ppermute | solution.py:92
  208.0 1.7 shard_map.286
  (174 shorter events, 60.9 us)
Async XLA Ops:
  9.2 18.3 %collective-permute-start.15 = (bf16[160,1024]{1,0:T(8,128)(2,1)}, bf16[160,1024]{1,0:T(8,128)(2,1)S(1)}, u32[]{:S(2)}, u32[]{:S(2)}) collective-permute-start(bf16[160,1024]{1,0:T(8,128)(2,1)} %get-tuple-element.99.rest_10_), channel_id=1, source_target_pairs={{0,2},{1,3},{2,0},{3,1},{4,6},{5,7},{6,4},{7,5},{8,10},{9,11},{10,... | collective-permute-start | bytes 983048 | tf_op jit(solution)/shard_map/ppermute | solution.py:95
  10.8 18.1 %collective-permute-start.16 = (bf16[160,1024]{1,0:T(8,128)(2,1)}, bf16[160,1024]{1,0:T(8,128)(2,1)S(1)}, u32[]{:S(2)}, u32[]{:S(2)}) collective-permute-start(bf16[160,1024]{1,0:T(8,128)(2,1)} %get-tuple-element.99.rest_10_), channel_id=1, source_target_pairs={{0,4},{1,5},{2,6},{3,7},{4,0},{5,1},{6,2},{7,3},{8,12},{9,13},{10,... | collective-permute-start | bytes 983048 | tf_op jit(solution)/shard_map/ppermute | solution.py:95
  12.8 18.3 %collective-permute-start.19 = (bf16[160,1024]{1,0:T(8,128)(2,1)}, bf16[160,1024]{1,0:T(8,128)(2,1)S(1)}, u32[]{:S(2)}, u32[]{:S(2)}) collective-permute-start(bf16[160,1024]{1,0:T(8,128)(2,1)} %get-tuple-element.99.rest_10_), channel_id=1, source_target_pairs={{0,1},{1,0},{2,3},{3,2},{4,5},{5,4},{6,7},{7,6},{8,9},{9,8},{10,11... | collective-permute-start | bytes 983048 | tf_op jit(solution)/shard_map/ppermute | solution.py:95
  19.6 48.0 %all-to-all-start = ((bf16[32,8,128]{2,1,0:T(8,128)(2,1)}), bf16[32,8,128]{2,1,0:T(8,128)(2,1)S(1)}, u32[]{:S(2)}, u32[]{:S(2)}) async-start(bf16[32,8,128]{2,1,0:T(8,128)(2,1)} %get-tuple-element.86), calls=%async_computation | async-start | bytes 131072 | tf_op jit(solution)/shard_map/all_to_all | solution.py:190
  24.7 16.5 %collective-permute-start.4 = (bf16[128,1024]{1,0:T(8,128)(2,1)}, bf16[128,1024]{1,0:T(8,128)(2,1)}, u32[]{:S(2)}, u32[]{:S(2)}) collective-permute-start(bf16[128,1024]{1,0:T(8,128)(2,1)} %x.3), channel_id=1, source_target_pairs={{0,16},{1,17},{2,18},{3,19},{4,20},{5,21},{6,22},{7,23},{8,24},{9,... | collective-permute-start | bytes 786440 | tf_op jit(solution)/shard_map/ppermute | solution.py:92
  27.5 17.2 %collective-permute-start.6 = (bf16[4,32,1792]{2,1,0:T(8,128)(2,1)S(1)}, bf16[4,32,1792]{2,1,0:T(8,128)(2,1)S(1)}, u32[]{:S(2)}, u32[]{:S(2)}) collective-permute-start(bf16[4,32,1792]{2,1,0:T(8,128)(2,1)S(1)} %bitcast.27), channel_id=1, source_target_pairs={{0,2},{1,3},{2,0},{3,1},{4,6},{5,7},{6,4},{7,5},{8,10},{9,11},{10,... | collective-permute-start | bytes 1376264 | tf_op jit(solution)/shard_map/ppermute | solution.py:95
  28.9 16.4 %collective-permute-start.7 = (bf16[4,32,1792]{2,1,0:T(8,128)(2,1)S(1)}, bf16[4,32,1792]{2,1,0:T(8,128)(2,1)S(1)}, u32[]{:S(2)}, u32[]{:S(2)}) collective-permute-start(bf16[4,32,1792]{2,1,0:T(8,128)(2,1)S(1)} %bitcast.28), channel_id=1, source_target_pairs={{0,4},{1,5},{2,6},{3,7},{4,0},{5,1},{6,2},{7,3},{8,12},{9,13},{10,... | collective-permute-start | bytes 1376264 | tf_op jit(solution)/shard_map/ppermute | solution.py:95
  43.6 17.8 %collective-permute-start.20 = (bf16[160,1024]{1,0:T(8,128)(2,1)S(1)}, bf16[160,1024]{1,0:T(8,128)(2,1)S(1)}, u32[]{:S(2)}, u32[]{:S(2)}) collective-permute-start(bf16[160,1024]{1,0:T(8,128)(2,1)S(1)} %collective-permute-done.15.rest_11_), channel_id=1, source_target_pairs={{0,1},{1,0},{2,3},{3,2},{4,5},{5,4},{6,7},{7,6},{8,9},{9,8},{10,11... | collective-permute-start | bytes 983048 | tf_op jit(solution)/shard_map/ppermute | solution.py:95
  44.7 17.4 %collective-permute-start.21 = (bf16[160,1024]{1,0:T(8,128)(2,1)S(1)}, bf16[160,1024]{1,0:T(8,128)(2,1)S(1)}, u32[]{:S(2)}, u32[]{:S(2)}) collective-permute-start(bf16[160,1024]{1,0:T(8,128)(2,1)S(1)} %collective-permute-done.16.rest_12_), channel_id=1, source_target_pairs={{0,1},{1,0},{2,3},{3,2},{4,5},{5,4},{6,7},{7,6},{8,9},{9,8},{10,11... | collective-permute-start | bytes 983048 | tf_op jit(solution)/shard_map/ppermute | solution.py:95
  68.6 26.9 %collective-permute-start.26 = (bf16[128,1024]{1,0:T(8,128)(2,1)}, bf16[128,1024]{1,0:T(8,128)(2,1)S(1)}, u32[]{:S(2)}, u32[]{:S(2)}) collective-permute-start(bf16[128,1024]{1,0:T(8,128)(2,1)} %g0.1), channel_id=1, source_target_pairs={{0,8},{1,9},{2,10},{3,11},{4,12},{5,13},{6,14},{7,15},{8,0},{9,1},... | collective-permute-start | bytes 786440 | tf_op jit(solution)/shard_map/ppermute | solution.py:92
  69.6 26.0 %collective-permute-start.28 = (bf16[128,1024]{1,0:T(8,128)(2,1)}, bf16[128,1024]{1,0:T(8,128)(2,1)S(1)}, u32[]{:S(2)}, u32[]{:S(2)}) collective-permute-start(bf16[128,1024]{1,0:T(8,128)(2,1)} %collective-permute-done.27.g2), channel_id=1, source_target_pairs={{0,8},{1,9},{2,10},{3,11},{4,12},{5,13},{6,14},{7,15},{8,0},{9,1},... | collective-permute-start | bytes 786440 | tf_op jit(solution)/shard_map/ppermute | solution.py:92
  103.1 16.1 %collective-permute-start.39 = (bf16[4,256,1024]{2,1,0:T(8,128)(2,1)S(1)}, bf16[4,256,1024]{2,1,0:T(8,128)(2,1)S(1)}, u32[]{:S(2)}, u32[]{:S(2)}) collective-permute-start(bf16[4,256,1024]{2,1,0:T(8,128)(2,1)S(1)} %get-tuple-element.143), channel_id=1, source_target_pairs={{0,1},{1,0},{2,3},{3,2},{4,5},{5,4},{6,7},{7,6},{8,9},{9,8},{10,11... | collective-permute-start | bytes 6291464 | tf_op jit(solution)/shard_map/ppermute | solution.py:95
  119.6 42.3 %collective-permute-start.40 = (bf16[256,1024]{1,0:T(8,128)(2,1)S(1)}, bf16[256,1024]{1,0:T(8,128)(2,1)S(1)}, u32[]{:S(2)}, u32[]{:S(2)}) collective-permute-start(bf16[256,1024]{1,0:T(8,128)(2,1)S(1)} %get-tuple-element.145), channel_id=1, source_target_pairs={{0,2},{1,3},{2,0},{3,1},{4,6},{5,7},{6,4},{7,5},{8,10},{9,11},{10,... | collective-permute-start | bytes 1572872 | tf_op jit(solution)/shard_map/ppermute | solution.py:95
  121.0 41.3 %collective-permute-start.41 = (bf16[256,1024]{1,0:T(8,128)(2,1)S(1)}, bf16[256,1024]{1,0:T(8,128)(2,1)S(1)}, u32[]{:S(2)}, u32[]{:S(2)}) collective-permute-start(bf16[256,1024]{1,0:T(8,128)(2,1)S(1)} %get-tuple-element.146), channel_id=1, source_target_pairs={{0,4},{1,5},{2,6},{3,7},{4,0},{5,1},{6,2},{7,3},{8,12},{9,13},{10,... | collective-permute-start | bytes 1572872 | tf_op jit(solution)/shard_map/ppermute | solution.py:95
  122.4 43.6 %collective-permute-start.42 = (bf16[256,1024]{1,0:T(8,128)(2,1)S(1)}, bf16[256,1024]{1,0:T(8,128)(2,1)S(1)}, u32[]{:S(2)}, u32[]{:S(2)}) collective-permute-start(bf16[256,1024]{1,0:T(8,128)(2,1)S(1)} %get-tuple-element.147), channel_id=1, source_target_pairs={{0,6},{1,7},{2,4},{3,5},{4,2},{5,3},{6,0},{7,1},{8,14},{9,15},{10,... | collective-permute-start | bytes 1572872 | tf_op jit(solution)/shard_map/ppermute | solution.py:95
  129.8 28.1 %collective-permute-start.34 = (bf16[136,1024]{1,0:T(8,128)(2,1)S(1)}, bf16[136,1024]{1,0:T(8,128)(2,1)S(1)}, u32[]{:S(2)}, u32[]{:S(2)}) collective-permute-start(bf16[136,1024]{1,0:T(8,128)(2,1)S(1)} %get-tuple-element.132), channel_id=1, source_target_pairs={{0,4},{1,5},{2,6},{3,7},{4,0},{5,1},{6,2},{7,3},{8,12},{9,13},{10,... | collective-permute-start | bytes 835592 | tf_op jit(solution)/shard_map/ppermute | solution.py:95
  131.2 27.6 %collective-permute-start.35 = (bf16[136,1024]{1,0:T(8,128)(2,1)S(1)}, bf16[136,1024]{1,0:T(8,128)(2,1)S(1)}, u32[]{:S(2)}, u32[]{:S(2)}) collective-permute-start(bf16[136,1024]{1,0:T(8,128)(2,1)S(1)} %get-tuple-element.133), channel_id=1, source_target_pairs={{0,6},{1,7},{2,4},{3,5},{4,2},{5,3},{6,0},{7,1},{8,14},{9,15},{10,... | collective-permute-start | bytes 835592 | tf_op jit(solution)/shard_map/ppermute | solution.py:95
  158.7 28.9 %collective-permute-start.30 = (bf16[128,1024]{1,0:T(8,128)(2,1)S(1)}, bf16[128,1024]{1,0:T(8,128)(2,1)S(1)}, u32[]{:S(2)}, u32[]{:S(2)}) collective-permute-start(bf16[128,1024]{1,0:T(8,128)(2,1)S(1)} %get-tuple-element.126), channel_id=1, source_target_pairs={{0,16},{1,17},{2,18},{3,19},{4,20},{5,21},{6,22},{7,23},{8,24},{9,... | collective-permute-start | bytes 786440 | tf_op jit(solution)/shard_map/ppermute | solution.py:92
  161.9 26.9 %collective-permute-start.31 = (bf16[128,1024]{1,0:T(8,128)(2,1)S(1)}, bf16[128,1024]{1,0:T(8,128)(2,1)S(1)}, u32[]{:S(2)}, u32[]{:S(2)}) collective-permute-start(bf16[128,1024]{1,0:T(8,128)(2,1)S(1)} %get-tuple-element.127), channel_id=1, source_target_pairs={{0,24},{1,25},{2,26},{3,27},{4,28},{5,29},{6,30},{7,31},{8,16},{9,... | collective-permute-start | bytes 786440 | tf_op jit(solution)/shard_map/ppermute | solution.py:92
  162.3 36.4 %collective-permute-start.25 = (bf16[128,1024]{1,0:T(8,128)(2,1)S(1)}, bf16[128,1024]{1,0:T(8,128)(2,1)S(1)}, u32[]{:S(2)}, u32[]{:S(2)}) collective-permute-start(bf16[128,1024]{1,0:T(8,128)(2,1)S(1)} %shard_map.275), channel_id=1, source_target_pairs={{0,16},{1,17},{2,18},{3,19},{4,20},{5,21},{6,22},{7,23},{8,24},{9,... | collective-permute-start | bytes 786440 | tf_op jit(solution)/shard_map/ppermute | solution.py:92
  166.0 33.4 %collective-permute-start.36 = (bf16[40,768]{1,0:T(8,128)(2,1)S(1)}, bf16[40,768]{1,0:T(8,128)(2,1)S(1)}, u32[]{:S(2)}, u32[]{:S(2)}) collective-permute-start(bf16[40,768]{1,0:T(8,128)(2,1)S(1)} %get-tuple-element.135), channel_id=1, source_target_pairs={{0,8},{1,9},{2,10},{3,11},{4,12},{5,13},{6,14},{7,15},{8,0},{9,1},... | collective-permute-start | bytes 184328 | tf_op jit(solution)/shard_map/ppermute | solution.py:92
  170.5 35.8 %collective-permute-start.37 = (bf16[40,768]{1,0:T(8,128)(2,1)}, bf16[40,768]{1,0:T(8,128)(2,1)}, u32[]{:S(2)}, u32[]{:S(2)}) collective-permute-start(bf16[40,768]{1,0:T(8,128)(2,1)} %get-tuple-element.136), channel_id=1, source_target_pairs={{0,16},{1,17},{2,18},{3,19},{4,20},{5,21},{6,22},{7,23},{8,24},{9,... | collective-permute-start | bytes 184328 | tf_op jit(solution)/shard_map/ppermute | solution.py:92
  187.6 18.7 %collective-permute-start.38 = (bf16[40,768]{1,0:T(8,128)(2,1)}, bf16[40,768]{1,0:T(8,128)(2,1)}, u32[]{:S(2)}, u32[]{:S(2)}) collective-permute-start(bf16[40,768]{1,0:T(8,128)(2,1)} %get-tuple-element.137), channel_id=1, source_target_pairs={{0,24},{1,25},{2,26},{3,27},{4,28},{5,29},{6,30},{7,31},{8,16},{9,... | collective-permute-start | bytes 184328 | tf_op jit(solution)/shard_map/ppermute | solution.py:92
  189.5 18.5 %collective-permute-start.43 = (bf16[32,1024]{1,0:T(8,128)(2,1)}, bf16[32,1024]{1,0:T(8,128)(2,1)S(1)}, u32[]{:S(2)}, u32[]{:S(2)}) collective-permute-start(bf16[32,1024]{1,0:T(8,128)(2,1)} %get-tuple-element.149), channel_id=1, source_target_pairs={{0,8},{1,9},{2,10},{3,11},{4,12},{5,13},{6,14},{7,15},{8,0},{9,1},... | collective-permute-start | bytes 196616 | tf_op jit(solution)/shard_map/ppermute | solution.py:92
  (54 other events, 561.3 us)

commit v2 on v1

--- a/solution.py
+++ b/solution.py
@@ -1,3 +1,4 @@
+import functools
 import math
 
 import jax
@@ -14,6 +15,7 @@
 NB = 4
 QB = D // NB
 NEG = -1e30
+SHARE = 1.0
 
 F32 = jnp.float32
 BF = jnp.bfloat16
@@ -33,11 +35,11 @@
 
 
 def call(body, ins, outs, scratch=(), flops=0, extra=4 << 20, hbm=(), alias=None):
-    spaces = {"v": pltpu.VMEM, "s": pltpu.SMEM, "a": pl.ANY}
+    spaces = {"v": pltpu.VMEM, "s": pltpu.SMEM, "a": pl.ANY, "h": pltpu.HBM}
     arrays = [a for _, a in ins]
     nbytes = sum(a.size * a.dtype.itemsize for a in arrays) + sum(math.prod(o.shape) * o.dtype.itemsize for o in outs)
     room = sum(math.prod(t.shape) * jnp.dtype(t.dtype).itemsize for t in scratch if getattr(t, "memory_space", None) == pltpu.VMEM)
-    room += sum(a.size * a.dtype.itemsize for s, a in ins if s == "v") + sum(math.prod(o.shape) * o.dtype.itemsize for i, o in enumerate(outs) if i not in hbm)
+    room += SHARE * (sum(a.size * a.dtype.itemsize for s, a in ins if s == "v") + sum(math.prod(o.shape) * o.dtype.itemsize for i, o in enumerate(outs) if i not in hbm))
     return pl.pallas_call(
         body,
         out_shape=tuple(outs),
@@ -59,7 +61,7 @@
         fn(pl.ds(pl.multiple_of(i * chunk, chunk), chunk))
         return carry
 
-    lax.fori_loop(0, count // chunk, step, 0)
+    lax.fori_loop(0, count // chunk, step, 0, unroll=True)
 
 
 def lanes(i, width):
@@ -94,10 +96,10 @@
     def swap(v, mask):
         return lax.ppermute(v, "dp", [(d, d ^ mask) for d in range(n)])
 
-    def gather_r(own):
+    def gather_r(own, tag):
         half = own.shape[0] // 2
         got = [(0, 0, own)]
-        if R == 8:
+        if R == 8 and tag == "one":
             from_x, from_y = swap(own, 2), swap(own, 4)
             got += [(2, 0, from_x), (4, 0, from_y)]
             got.append((6, 0, swap(from_y[:half], 2)))
@@ -182,14 +184,15 @@
             two = across(after, 2)
             return [own, across(after, 1), two, across(two, 1)]
 
-        mine = jnp.concatenate([columns[0]] + [across(columns[k], k) for k in range(1, NB)]).reshape(NB, rows, W1)
-        two = gather_r(own_two)
-        one = gather_r(mine)
-        after, _ = lax.optimization_barrier((block_in, mine))
+        two = gather_r(own_two, "two")
+        crossed = [across(columns[k], k) for k in range(1, NB)]
+        after, _ = lax.optimization_barrier((block_in, crossed))
+        mine = jnp.concatenate([columns[0]] + crossed).reshape(NB, rows, W1)
+        one = gather_r(mine, "one")
         tokens = blocks_of(block_in, after)
         small_in = lax.all_to_all(small_out, "dp", 0, 0, tiled=True)
         after, _ = lax.optimization_barrier((grad_out, tokens[1]))
-        grads_in = blocks_of(grad_out, after)
+        grads_in = [grad_out] + [across(after, k) for k in range(1, NB)]
 
         def pick(width_mod, off, base, width):
             return (iota((width, width_mod.shape[1]), 0) + base == off + width_mod).astype(BF)
@@ -220,12 +223,13 @@
             dec_body, [("s", br), ("v", small_in)], [sds((1, 3 * QB), F32), sds((1, FB), F32)] + [row] * 5
         )
 
-        def load_one(br, parts, w1, sems):
+        def load_one(br, parts, w1, sems, low, high):
+            cols = pl.ds(low, high - low)
             copies = []
             for (m, start, _), ref in zip(one, parts):
                 for k in range(ref.shape[0]):
-                    sem = sems.at[len(copies)]
-                    copies.append(pltpu.make_async_copy(ref.at[k], w1.at[br[0] ^ (start + k), br[1] ^ m], sem))
+                    to = w1.at[br[0] ^ (start + k), br[1] ^ m, :, cols]
+                    copies.append(pltpu.make_async_copy(ref.at[k, :, cols], to, sems.at[int(low > 0), len(copies)]))
             return copies
 
         def load_two(br, parts, wout, wo, sems):
@@ -247,17 +251,20 @@
         dma = pltpu.SemaphoreType.DMA
         PAIRS = QB // 128
 
-        def fwd_body(br, x0, x1, x2, x3, cos, sin, mask_ref, bq, bi, g1, s1, g2, s2, *rest):
+        def fwd_body(br, h0, h1, h2, h3, cos, sin, mask_ref, bq, bi, g1, s1, g2, s2, *rest):
             one_refs, two_refs, rest = rest[: len(one)], rest[len(one) : len(one) + len(two)], rest[len(one) + len(two) :]
             act1, act2, q, k, v, probs, mixed, hidden, dgelu, xhat_ref, w1, wo, wout, own, later, away = rest[:16]
-            stage, sem1, sem2, semp = rest[16:]
-            c1, c2 = load_one(br, one_refs, w1, sem1), load_two(br, two_refs, wout, wo, sem2)
-            for c in c1 + c2:
+            stage, x_ref, semx, sem1, sem2, semp = rest[16:]
+            cx = [pltpu.make_async_copy(h, x_ref.at[i], semx.at[i]) for i, h in enumerate((h0, h1, h2, h3))]
+            c1, c1f = load_one(br, one_refs, w1, sem1, 0, 3 * QB), load_one(br, one_refs, w1, sem1, 3 * QB, W1)
+            c2 = load_two(br, two_refs, wout, wo, sem2)
+            for c in cx + c1 + c1f + c2:
                 c.start()
-            for i, x in enumerate((x0, x1, x2, x3)):
-
-                def norm(rws, i=i, x=x):
-                    centered, rstd = stats(x[rws].astype(F32))
+            for i in range(NB):
+                cx[i].wait()
+
+                def norm(rws, i=i):
+                    centered, rstd = stats(x_ref[i, rws].astype(F32))
                     xhat = centered * rstd
                     to = pl.ds(pl.multiple_of(i * T + rws.start, T), T)
                     xhat_ref[to] = xhat
@@ -295,7 +302,9 @@
                     mixed[rws, cols] = dot_nn(pb, split_heads(v[rws, cols])).astype(BF)
                 return carry
 
-            lax.fori_loop(0, NB, attend, 0)
+            lax.fori_loop(0, NB, attend, 0, unroll=True)
+            for c in c1f:
+                c.wait()
 
             def feed(t, carry):
                 cols = lanes(t, 256)
@@ -310,7 +319,7 @@
                 by_rows(NT, 256, act)
                 return carry
 
-            lax.fori_loop(0, FB // 256, feed, 0)
+            lax.fori_loop(0, FB // 256, feed, 0, unroll=True)
             for c in c2:
                 c.wait()
 
@@ -324,7 +333,7 @@
                 stage[T:, cols] = y[3 * T :].astype(BF)
                 return carry
 
-            lax.fori_loop(0, D // 256, project_out, 0)
+            lax.fori_loop(0, D // 256, project_out, 0, unroll=True)
             send = pltpu.make_async_copy(stage, away, semp)
             send.start()
             send.wait()
@@ -334,13 +343,14 @@
         block = sds((T, D), BF)
         act1, act2, q, k, v, probs, mixed, hidden, dgelu, xhat, full_one, full_o, full_out, own_part, later_part, away_part = call(
             fwd_body,
-            [("s", br)] + [("v", x) for x in tokens]
+            [("s", br)] + [("h", x) for x in tokens]
             + [("v", a) for a in (cosine, sines, mask, bias_qkv, bias_in, gain_one, shift_one, gain_two, shift_two)]
-            + [("a", a) for _, _, a in one + two],
+            + [("h", a) for _, _, a in one + two],
             [tab, tab, third, third, third, sds((NB * PAIRS, 2 * T, T), F32), third, sds((NT, FB), BF), sds((NT, FB), F32),
              sds((NT, D), F32), sds((NB, R, rows, W1), BF), sds((R, rows, D), BF), sds((R, ff_dev, D), BF),
              sds((T, D), F32), sds((T, D), F32), sds((2 * T, D), BF)],
-            [pltpu.VMEM((2 * T, D), BF), dma((R * NB,)), dma((3 * R,)), dma], hbm=(15,),
+            [pltpu.VMEM((2 * T, D), BF), pltpu.VMEM((NB, T, D), BF), dma((NB,)), dma((2, R * NB)), dma((3 * R,)), dma],
+            hbm=(15,),
             flops=2 * NT * D * W1 + 2 * NT * D * (QB + FB) + 8 * NT * T * QB,
         )
 
@@ -352,20 +362,6 @@
 
             by_rows(T, T, fn)
 
-        (pass_part,) = call(pass_body, [("v", later_part), ("v", got_one)], [block])
-        got_two = across(pass_part, 2)
-
-        def total_body(x, live_ref, bo, own, p1, p2, out):
-            def fn(rws):
-                y = x[rws].astype(F32) + bo[...] + own[rws] + p1[rws].astype(F32) + p2[rws].astype(F32)
-                out[rws] = (y * live_ref[rws]).astype(BF)
-
-            by_rows(T, T, fn)
-
-        (block_out,) = call(
-            total_body,
-            [("v", a) for a in (block_in, live[:T], bias_o, own_part, got_one, got_two)], [block],
-        )
 
         def bwd1_body(br, live_ref, g0, g1, g2, g3, act2, hidden, dgelu, wout, *rest):
             grad, dhid, keep, send, sum_in, term, flip = rest
@@ -384,14 +380,14 @@
                 term[pl.ds(t * per, per)] = y.reshape(per, ff_dev, D)
                 return carry
 
-            lax.fori_loop(0, FB // 256, term_out, 0)
+            lax.fori_loop(0, FB // 256, term_out, 0, unroll=True)
 
             def to_out(j, carry):
                 keep[j, MA:] = term[br[1] ^ (2 * j)]
                 send[j, MA:] = term[br[1] ^ (2 * j + 1)].astype(BF)
                 return carry
 
-            lax.fori_loop(0, J, to_out, 0)
+            lax.fori_loop(0, J, to_out, 0, unroll=True)
 
             def d_hidden(t, carry):
                 cols = lanes(t, 256)
@@ -402,7 +398,7 @@
                 sum_in[:, cols] = jnp.sum(y.astype(F32), axis=0, keepdims=True)
                 return carry
 
-            lax.fori_loop(0, FB // 256, d_hidden, 0)
+            lax.fori_loop(0, FB // 256, d_hidden, 0, unroll=True)
 
             term_r = term.reshape(R * ff_dev // rows, rows, D) if ff_dev != rows else term
 
@@ -416,9 +412,9 @@
                     send[j, at] = term_r[br[1] ^ (2 * j + 1)].astype(BF)
                     return carry
 
-                return lax.fori_loop(0, J, one_j, carry)
-
-            lax.fori_loop(0, NB, term_in, 0)
+                return lax.fori_loop(0, J, one_j, carry, unroll=True)
+
+            lax.fori_loop(0, NB, term_in, 0, unroll=True)
 
         grad_r, dhid, keep_f, send_f, sum_in = call(
             bwd1_body,
@@ -440,7 +436,7 @@
                     send[j, c * rows : (c + 1) * rows, 3 * QB :] = term_o[br[1] ^ (2 * j + 1), :, cols].astype(BF)
                 return carry
 
-            lax.fori_loop(0, J, to_o, 0)
+            lax.fori_loop(0, J, to_o, 0, unroll=True)
             dmix[...] = dot_nt(grad[...], wo[...].reshape(QB, D)).astype(BF)
 
             def attend(i, carry):
@@ -462,7 +458,7 @@
                     dqkv[rws, 2 * QB + p * 128 : 2 * QB + (p + 1) * 128] = dv.astype(BF)
                 return carry
 
-            lax.fori_loop(0, NB, attend, 0)
+            lax.fori_loop(0, NB, attend, 0, unroll=True)
             sum_qkv[...] = jnp.sum(dqkv[...].astype(F32), axis=0, keepdims=True)
 
             def term_qkv(t, carry):
@@ -475,9 +471,9 @@
                     send[j, at, : 3 * QB] = term[br[1] ^ (2 * j + 1)].astype(BF)
                     return carry
 
-                return lax.fori_loop(0, J, one_j, carry)
-
-            lax.fori_loop(0, NB, term_qkv, 0)
+                return lax.fori_loop(0, J, one_j, carry, unroll=True)
+
+            lax.fori_loop(0, NB, term_qkv, 0, unroll=True)
 
         dqkv, keep_a, send_a, sum_qkv = call(
             bwd2_body,
@@ -488,8 +484,11 @@
             flops=2 * NT * D * (3 * QB + 2 * QB) + 16 * NT * T * QB,
         )
 
-        def merge_body(keep, got, *outs):
+        def merge_body(extra, keep, got, *rest):
             size = keep.shape[1]
+            outs = rest[extra:]
+            if extra:
+                pass_body(*rest[:extra], outs[J])
             for j in range(J):
 
                 def fn(rws, j=j):
@@ -498,19 +497,23 @@
 
                 by_rows(size, size, fn)
 
-        def merge(keep, send):
+        def merge(keep, send, passed=()):
             size = keep.shape[1]
             got = swap(send, 1)
-            outs = call(merge_body, [("v", keep), ("v", got)], [sds((size, D), F32)] + [sds((size, D), BF)] * (J - 1))
-            return [outs[0]] + [swap(outs[j], 2 * j) for j in range(1, J)]
-
-        merged_f = merge(keep_f, send_f)
+            outs = call(
+                functools.partial(merge_body, len(passed)), [("v", a) for a in (keep, got, *passed)],
+                [sds((size, D), F32)] + [sds((size, D), BF)] * (J - 1) + [block] * bool(passed),
+            )
+            return [outs[0]] + [swap(outs[j], 2 * j) for j in range(1, J)], outs[J:]
+
+        merged_f, (pass_part,) = merge(keep_f, send_f, (later_part, got_one))
+        got_two = across(pass_part, 2)
         out_widths = [FB * NB // n, 3 * D // n] + [D // n] * 5
         out_offsets = [sum(out_widths[:i]) for i in range(len(out_widths))]
         WO = -(-sum(out_widths) // 128) * 128
 
         def bwd3_body(br, xhat, w1, dqkv, dhid, grad, sum_in, sum_qkv, g1, g2, keep_in, send_in, *rest):
-            own, p1h, p2h, p3h, keep, send, p1, p2, p3, gs, sums, tot, semp = rest
+            own, later, away, keep, send, stage, gs, sums, tot, semp = rest
             gs[...] = jnp.sum(grad[:T].astype(F32), axis=0, keepdims=True)
 
             def back(t, carry):
@@ -520,16 +523,16 @@
                 xh = xhat[:, cols]
                 y = d1 * g1[:, cols] + d2 * g2[:, cols]
                 own[:, cols] = y[:T]
-                for i, ref in enumerate((p1, p2, p3)):
-                    ref[:, cols] = y[(i + 1) * T : (i + 2) * T].astype(BF)
+                later[:, cols] = y[2 * T : 3 * T]
+                stage[:T, cols] = y[T : 2 * T].astype(BF)
+                stage[T:, cols] = y[3 * T :].astype(BF)
                 for i, z in enumerate((d1 * xh, d1, d2 * xh, d2)):
                     sums[i : i + 1, cols] = jnp.sum(z, axis=0, keepdims=True)
                 return carry
 
-            lax.fori_loop(0, D // QB, back, 0)
-            sends = [pltpu.make_async_copy(a, z, semp.at[i]) for i, (a, z) in enumerate(((p1, p1h), (p2, p2h), (p3, p3h)))]
-            for c in sends:
-                c.start()
+            lax.fori_loop(0, D // QB, back, 0, unroll=True)
+            sending = pltpu.make_async_copy(stage, away, semp)
+            sending.start()
 
             total = jnp.zeros((n, WO), F32)
 
@@ -564,37 +567,31 @@
                     lines = [tot[pl.ds(to * R + (br[1] ^ m), 1), :] for to in range(NB)]
                     lines.append(jnp.zeros((MS - MA - NB, WO), F32))
                     ref[j, MA:, :WO] = jnp.concatenate(lines, axis=0).astype(ref.dtype)
-            for c in sends:
-                c.wait()
-
-        own_g, g_1, g_2, g_3, keep_a, send_a = call(
+            sending.wait()
+
+        own_g, later_g, away_g, keep_a, send_a = call(
             bwd3_body,
             [("s", br)] + [("v", a) for a in (xhat, full_one, dqkv, dhid, grad_r, sum_in, sum_qkv, gain_one, gain_two, keep_a, send_a)],
-            [sds((T, D), F32), block, block, block, sds((J, MS, D), F32), sds((J, MS, D), BF)],
-            [pltpu.VMEM((T, D), BF)] * 3 + [pltpu.VMEM((1, D), F32), pltpu.VMEM((8, D), F32), pltpu.VMEM((n, WO), F32), dma((3,))], hbm=(1, 2, 3),
-            alias={10: 4, 11: 5},
+            [sds((T, D), F32), sds((T, D), F32), sds((2 * T, D), BF), sds((J, MS, D), F32), sds((J, MS, D), BF)],
+            [pltpu.VMEM((2 * T, D), BF), pltpu.VMEM((1, D), F32), pltpu.VMEM((8, D), F32), pltpu.VMEM((n, WO), F32), dma], hbm=(2,),
+            alias={10: 3, 11: 4},
             flops=2 * NT * D * W1,
         )
-        g_back = [across(g, k) for k, g in ((1, g_1), (2, g_2), (3, g_3))]
-        merged_a = merge(keep_a, send_a)
-
-        def input_body(x, grad, own, p1, p2, p3, out):
+        back_one = across(away_g, 1)
+        (pass_g,) = call(pass_body, [("v", later_g), ("v", back_one)], [block])
+        back_two = across(pass_g, 2)
+        merged_a, _ = merge(keep_a, send_a)
+
+        def total_body(x, live_ref, bo, own, p1, p2, out):
             def fn(rws):
-                centered, rstd = stats(x[rws].astype(F32))
-                xh = centered * rstd
-                g = own[rws]
-                for ref in (p1, p2, p3):
-                    g = g + ref[rws].astype(F32)
-                mean_g = jnp.mean(g, axis=-1, keepdims=True)
-                mean_gx = jnp.mean(g * xh, axis=-1, keepdims=True)
-                out[rws] = (grad[rws].astype(F32) + rstd * (g - mean_g - xh * mean_gx)).astype(BF)
+                y = x[rws].astype(F32) + bo[...] + own[rws] + p1[rws].astype(F32) + p2[rws].astype(F32)
+                out[rws] = (y * live_ref[rws]).astype(BF)
 
             by_rows(T, T, fn)
 
-        (grad_input,) = call(input_body, [("v", a) for a in (block_in, grad_r[:T], own_g, *g_back)], [block])
-
-        def plane_f_body(br, *rest):
-            got, (w_out_ref, z0, z1, z2, z3) = rest[:J], rest[J:]
+        def plane_f_body(br, x, live_ref, bo, own, p1, p2, *rest):
+            got, (w_out_ref, z0, z1, z2, z3, out) = rest[:J], rest[J:]
+            total_body(x, live_ref, bo, own, p1, p2, out)
 
             def out_rows(rws):
                 y = got[0][pl.ds(pl.multiple_of(MA + rws.start, 8), rws.size)]
@@ -610,9 +607,10 @@
                     y = y + other[at].astype(F32)
                 ref[...] = y if k == 0 else y.astype(BF)
 
-        grad_w_out, zf0, *zf = call(
-            plane_f_body, [("s", br)] + [("v", a) for a in merged_f],
-            [sds((ff_dev, D), F32), sds((rows, FB), F32)] + [sds((rows, FB), BF)] * 3,
+        grad_w_out, zf0, *zf, block_out = call(
+            plane_f_body,
+            [("s", br)] + [("v", a) for a in (block_in, live[:T], bias_o, own_part, got_one, got_two, *merged_f)],
+            [sds((ff_dev, D), F32), sds((rows, FB), F32)] + [sds((rows, FB), BF)] * 3 + [block],
         )
 
         def plane_a_body(br, *rest):
@@ -645,26 +643,45 @@
             for k, ref in enumerate((z0, z1, z2, z3)):
                 out[:, lanes(br[0] ^ k, FB)] = ref[...].astype(F32)
 
+        small_order = (0, 1, 2, 2, 3, 4, 5, 6)
+
         def place_a_body(br, z0, z1, z2, z3, out, *small):
             y = sum(ref[rows:, :WO].astype(F32) for ref in (z0, z1, z2, z3))
-            for ref, at, width in zip(small, out_offsets, out_widths):
-                ref[...] = y[:1, at : at + width]
+            for ref, which in zip(small, small_order):
+                ref[...] = y[:1, out_offsets[which] : out_offsets[which] + out_widths[which]]
             for k, ref in enumerate((z0, z1, z2, z3)):
                 at = br[0] ^ k
                 for s in range(3):
                     out[:, lanes(s * NB + at, QB)] = ref[:rows, s * QB : (s + 1) * QB].astype(F32)
 
-        (grad_w_in,) = call(place_f_body, [("s", br)] + [("v", z) for z in zf], [sds((rows, NB * FB), F32)])
-        grad_w_qkv, *outs = call(
-            place_a_body, [("s", br)] + [("v", z) for z in za],
-            [sds((rows, 3 * D), F32)] + [sds((1, w), F32) for w in out_widths],
+        def input_body(x, grad, own, p1, p2, out):
+            def fn(rws):
+                centered, rstd = stats(x[rws].astype(F32))
+                xh = centered * rstd
+                g = own[rws] + p1[rws].astype(F32) + p2[rws].astype(F32)
+                mean_g = jnp.mean(g, axis=-1, keepdims=True)
+                mean_gx = jnp.mean(g * xh, axis=-1, keepdims=True)
+                out[rws] = (grad[rws].astype(F32) + rstd * (g - mean_g - xh * mean_gx)).astype(BF)
+
+            by_rows(T, T, fn)
+
+        def final_body(br, *rest):
+            ins, outs = rest[:13], rest[13:]
+            place_f_body(br, *ins[5:9], outs[1])
+            input_body(*ins[:5], outs[0])
+            place_a_body(br, *ins[9:13], *outs[2:])
+
+        grad_input, grad_w_in, grad_w_qkv, *outs = call(
+            final_body,
+            [("s", br)] + [("v", a) for a in (block_in, grad_r[:T], own_g, back_one, back_two, *zf, *za)],
+            [block, sds((rows, NB * FB), F32), sds((rows, 3 * D), F32)] + [sds((1, out_widths[i]), F32) for i in small_order],
         )
         outs = [o.reshape(-1) for o in outs]
 
-        grad_b_in, grad_b_qkv, grad_b, grad_g1, grad_s1, grad_g2, grad_s2 = outs
+        grad_b_in, grad_b_qkv, grad_b_o, grad_b_out, grad_g1, grad_s1, grad_g2, grad_s2 = outs
         return (
-            block_out, grad_input, grad_w_qkv, grad_b_qkv, grad_w_o, grad_b, grad_w_in, grad_b_in,
-            grad_w_out, grad_b, grad_g1, grad_s1, grad_g2, grad_s2,
+            block_out, grad_input, grad_w_qkv, grad_b_qkv, grad_w_o, grad_b_o, grad_w_in, grad_b_in,
+            grad_w_out, grad_b_out, grad_g1, grad_s1, grad_g2, grad_s2,
         )
 
     return on_device

time: 212 us -> 163 us (0.77)
  waiting for transfers between devices: 84.8 us -> 55 us
  Pallas kernels: 48.6 us -> 35.2 us
  local copies, waits for them, and re-layouts: 18.7 us -> 10.1 us
  starting transfers between devices: 54 us -> 57 us
    ppermute x26 -> x24, waiting for transfers between devices: 34.7 us -> 5.15 us  [swap(): return lax.ppermute(v, 'dp', [(d, d ^ mask) for d in range(n)])]
    pallas_call x15 -> x12, Pallas kernels: 48.6 us -> 35.2 us  [call(): pl.pallas_call(body, out_shape=tuple(outs), in_specs=[pl.BlockSpec(memory...]
    unnamed x63 -> x44, local copies, waits for them, and re-layouts: 17 us -> 9.79 us
    ppermute x26 -> x24, starting transfers between devices: 16.8 us -> 20 us  [swap(): return lax.ppermute(v, 'dp', [(d, d ^ mask) for d in range(n)])]
    ppermute x20 -> x19, starting transfers between devices: 32.2 us -> 33 us  [across(): return lax.ppermute(v, 'dp', [(d, d ^ mask * R) for d in range(n)])]
    ppermute x20 -> x19, waiting for transfers between devices: 50.1 us -> 49.9 us  [across(): return lax.ppermute(v, 'dp', [(d, d ^ mask * R) for d in range(n)])]
  transfers between devices with their start and end apart: 47 -> 44, of which waited for: 14 -> 13; matrix products, arithmetic and copies ran while one was open for 2% -> 3% of each run, Pallas kernels for 18% -> 16%
where the time goes in v2:
time: 163 us
  starting transfers between devices  57 us (35%)
  waiting for transfers between devices  55 us (34%)
  Pallas kernels  35.2 us (22%)
  local copies, waits for them, and re-layouts  10.1 us (6%)
  other arithmetic  4.34 us (3%)
    ppermute x19, waiting for transfers between devices, across(): return lax.ppermute(v, 'dp', [(d, d ^ mask * R) for d in range(n)])  49.9 us
    pallas_call x12, Pallas kernels, call(): pl.pallas_call(body, out_shape=tuple(outs), in_specs=[pl.BlockSpec(memory...  35.2 us
    ppermute x19, starting transfers between devices, across(): return lax.ppermute(v, 'dp', [(d, d ^ mask * R) for d in range(n)])  33 us
    ppermute x24, starting transfers between devices, swap(): return lax.ppermute(v, 'dp', [(d, d ^ mask) for d in range(n)])  20 us
    unnamed x44, local copies, waits for them, and re-layouts  9.79 us
    ppermute x24, waiting for transfers between devices, swap(): return lax.ppermute(v, 'dp', [(d, d ^ mask) for d in range(n)])  5.15 us
    all_to_all x1, starting transfers between devices, on_device(): small_in = lax.all_to_all(small_out, 'dp', 0, 0, tiled=True)  3.97 us
  transfers between devices with their start and end apart: 44, of which 13 were waited for; matrix products, arithmetic and copies ran while one was open for 3% of the time, Pallas kernels for 16%

profile of v2, /device:TPU:0, one launch (start us, length us, event | category | flops | bytes accessed | tf_op | source)
XLA Modules:
  0.0 162.7 jit_solution(11975184671781132607)
XLA Ops:
  1.3 2.1 %shard_map.272 = (bf16[32,1792]{1,0:T(8,128)(2,1)}, bf16[32,1792]{1,0:T(8,128)(2,1)}, bf16[32,1792]{1,0:T(8,128)(2,1)}, bf16[32,1792]{1,0:T(8,128)(2,1)}, bf16[1...) custom-call(s32[2]{0:T(128)} %pad_add_fusion.1.br, bf16[32,3072]{1,0:T(8,128)(2,1)} %qkv_ref.1, bf16[32,4096]{1,0:T(8,128)(2,1)} %in_ref.1, ...), custom_call_target="tpu_custom_call" | custom-call | bytes 1639240 | tf_op jit(solution)/shard_map/pallas_call | solution.py:43
  3.4 3.1 %collective-permute-start = (bf16[32,1792]{1,0:T(8,128)(2,1)}, bf16[32,1792]{1,0:T(8,128)(2,1)S(1)}, u32[]{:S(2)}, u32[]{:S(2)}) collective-permute-start(bf16[32,1792]{1,0:T(8,128)(2,1)} %get-tuple-element.92), channel_id=1, source_target_pairs={{0,8},{1,9},{2,10},{3,11},{4,12},{5,13},{6,14},{7,15},{8,0},{9,1},... | collective-permute-start | bytes 344072 | tf_op jit(solution)/shard_map/ppermute | solution.py:94
  6.4 2.6 %collective-permute-start.1 = (bf16[32,1792]{1,0:T(8,128)(2,1)}, bf16[32,1792]{1,0:T(8,128)(2,1)S(1)}, u32[]{:S(2)}, u32[]{:S(2)}) collective-permute-start(bf16[32,1792]{1,0:T(8,128)(2,1)} %get-tuple-element.93), channel_id=1, source_target_pairs={{0,16},{1,17},{2,18},{3,19},{4,20},{5,21},{6,22},{7,23},{8,24},{9,... | collective-permute-start | bytes 344072 | tf_op jit(solution)/shard_map/ppermute | solution.py:94
  12.3 4.0 %all-to-all-start = ((bf16[32,8,128]{2,1,0:T(8,128)(2,1)}), bf16[32,8,128]{2,1,0:T(8,128)(2,1)S(1)}, u32[]{:S(2)}, u32[]{:S(2)}) async-start(bf16[32,8,128]{2,1,0:T(8,128)(2,1)} %get-tuple-element.90), calls=%async_computation | async-start | bytes 131072 | tf_op jit(solution)/shard_map/all_to_all | solution.py:193
  16.3 2.7 %collective-permute-start.17 = (bf16[160,1024]{1,0:T(8,128)(2,1)}, bf16[160,1024]{1,0:T(8,128)(2,1)}, u32[]{:S(2)}, u32[]{:S(2)}) collective-permute-start(bf16[160,1024]{1,0:T(8,128)(2,1)} %get-tuple-element.103.rest_10_), channel_id=1, source_target_pairs={{0,6},{1,7},{2,4},{3,5},{4,2},{5,3},{6,0},{7,1},{8,14},{9,15},{10,... | collective-permute-start | bytes 983048 | tf_op jit(solution)/shard_map/ppermute | solution.py:97
  20.9 3.9 %collective-permute-start.4 = (bf16[128,1024]{1,0:T(8,128)(2,1)}, bf16[128,1024]{1,0:T(8,128)(2,1)}, u32[]{:S(2)}, u32[]{:S(2)}) collective-permute-start(bf16[128,1024]{1,0:T(8,128)(2,1)} %rest_0_.1), channel_id=1, source_target_pairs={{0,16},{1,17},{2,18},{3,19},{4,20},{5,21},{6,22},{7,23},{8,24},{9,... | collective-permute-start | bytes 786440 | tf_op jit(solution)/shard_map/ppermute | solution.py:94
  31.0 5.3 %collective-permute-done.4.h2 = bf16[128,1024]{1,0:T(8,128)(2,1)} collective-permute-done((bf16[128,1024]{1,0:T(8,128)(2,1)}, bf16[128,1024]{1,0:T(8,128)(2,1)}, u32[]{:S(2)}, u32[]{:S(2)}) %collective-permute-start.4) | collective-permute-done | bytes 262176 | tf_op jit(solution)/shard_map/ppermute | solution.py:94
  43.8 3.6 %collective-permute-done.5.h3 = bf16[128,1024]{1,0:T(8,128)(2,1)} collective-permute-done((bf16[128,1024]{1,0:T(8,128)(2,1)}, bf16[128,1024]{1,0:T(8,128)(2,1)}, u32[]{:S(2)}, u32[]{:S(2)}) %collective-permute-start.5) | collective-permute-done | bytes 262176 | tf_op jit(solution)/shard_map/ppermute | solution.py:94
  51.9 2.9 %collective-permute-start.24 = (bf16[128,1024]{1,0:T(8,128)(2,1)}, bf16[128,1024]{1,0:T(8,128)(2,1)S(1)}, u32[]{:S(2)}, u32[]{:S(2)}) collective-permute-start(bf16[128,1024]{1,0:T(8,128)(2,1)} %g0.1), channel_id=1, source_target_pairs={{0,16},{1,17},{2,18},{3,19},{4,20},{5,21},{6,22},{7,23},{8,24},{9,... | collective-permute-start | bytes 786440 | tf_op jit(solution)/shard_map/ppermute | solution.py:94
  59.1 9.6 %shard_map.274 = (bf16[512,1024]{1,0:T(8,128)(2,1)S(1)}, bf16[512,1024]{1,0:T(8,128)(2,1)S(1)}, bf16[512,256]{1,0:T(8,128)(2,1)S(1)}, bf16[512,256]{1,0:T(8,128)...) custom-call(s32[2]{0:T(128)S(1)} %copy-done.9, ...), custom_call_target="tpu_custom_call" | custom-call | flops 3355443200 | bytes 25451528 | tf_op jit(solution)/shard_map/pallas_call | solution.py:43
  69.5 4.0 %collective-permute-done.24.g2 = bf16[128,1024]{1,0:T(8,128)(2,1)S(1)} collective-permute-done((bf16[128,1024]{1,0:T(8,128)(2,1)}, bf16[128,1024]{1,0:T(8,128)(2,1)S(1)}, u32[]{:S(2)}, u32[]{:S(2)}) %collective-permute-start.24) | collective-permute-done | bytes 262176 | tf_op jit(solution)/shard_map/ppermute | solution.py:94
  73.5 4.6 %shard_map.275 = (bf16[512,1024]{1,0:T(8,128)(2,1)S(1)}, bf16[512,1024]{1,0:T(8,128)(2,1)S(1)}, f32[4,256,1024]{2,1,0:T(8,128)S(1)}, bf16[4,256,1024]{2,1,0:T(8,128)(2,1)S(1)}, f32[1,1024]{1,0:T(1,128)S(1)}) custom-call(s32[2]{0:T(128)S(1)} %copy-done.9, f32[512,1]{1,0:T(8,128)S(1)} %copy.36.live_ref, bf16[128,1024]{1,0:T(8,128)(2,1)S(1)} %copy-done.15, ...), custom_call_target="tpu_custom_call" | custom-call | flops 3221225472 | bytes 15734792 | tf_op jit(solution)/shard_map/pallas_call | solution.py:43
  78.2 4.8 %shard_map.278 = (bf16[512,768]{1,0:T(8,128)(2,1)S(1)}, f32[4,136,1024]{2,1,0:T(8,128)S(1)}, bf16[4,136,1024]{2,1,0:T(8,128)(2,1)S(1)}, f32[1,768]{1,0:T(1,128)S(1)}) custom-call(s32[2]{0:T(128)S(1)} %copy-done.9, bf16[512,1024]{1,0:T(8,128)(2,1)S(1)} %get-tuple-element.120.grad, bf16[512,256]{1,0:T(8,128)(2,1)S(1)} %get-tuple-element.123.mixed, ...), custom_call_target="tpu_custom_call" | custom-call | flops 1610612736 | bytes 9374728 | tf_op jit(solution)/shard_map/pallas_call | solution.py:43
  83.0 4.0 %shard_map.279 = (f32[128,1024]{1,0:T(8,128)S(1)}, f32[128,1024]{1,0:T(8,128)S(1)}, bf16[256,1024]{1,0:T(8,128)(2,1)S(1)}, f32[4,136,1024]{2,1,0:T(8,128)S(1)}, bf16[4,136,1024]{2,1,0:T(8,128)(2,1)S(1)}) custom-call(s32[2]{0:T(128)S(1)} %copy-done.9, f32[512,1024]{1,0:T(8,128)S(1)} %get-tuple-element.121.xhat, ...), custom_call_target="tpu_custom_call", output_to_operand_aliasing={{3}: (10, {}), {4}: (11, {})} | custom-call | flops 1879048192 | bytes 16923656 | tf_op jit(solution)/shard_map/pallas_call | solution.py:43
  87.7 5.7 %collective-permute-start.22 = (bf16[256,1024]{1,0:T(8,128)(2,1)S(1)}, bf16[256,1024]{1,0:T(8,128)(2,1)S(1)}, u32[]{:S(2)}, u32[]{:S(2)}) collective-permute-start(bf16[256,1024]{1,0:T(8,128)(2,1)S(1)} %get-tuple-element.105), channel_id=1, source_target_pairs={{0,8},{1,9},{2,10},{3,11},{4,12},{5,13},{6,14},{7,15},{8,0},{9,1},... | collective-permute-start | bytes 1572872 | tf_op jit(solution)/shard_map/ppermute | solution.py:94
  96.4 9.7 %collective-permute-done.22.rest_1_.p1 = bf16[256,1024]{1,0:T(8,128)(2,1)S(1)} collective-permute-done((bf16[256,1024]{1,0:T(8,128)(2,1)S(1)}, bf16[256,1024]{1,0:T(8,128)(2,1)S(1)}, u32[]{:S(2)}, u32[]{:S(2)}) %collective-permute-start.22) | collective-permute-done | bytes 524320 | tf_op jit(solution)/shard_map/ppermute | solution.py:94
  106.1 2.2 %collective-permute-start.39 = (bf16[136,1024]{1,0:T(8,128)(2,1)S(1)}, bf16[136,1024]{1,0:T(8,128)(2,1)S(1)}, u32[]{:S(2)}, u32[]{:S(2)}) collective-permute-start(bf16[136,1024]{1,0:T(8,128)(2,1)S(1)} %get-tuple-element.148), channel_id=1, source_target_pairs={{0,6},{1,7},{2,4},{3,5},{4,2},{5,3},{6,0},{7,1},{8,14},{9,15},{10,... | collective-permute-start | bytes 835592 | tf_op jit(solution)/shard_map/ppermute | solution.py:97
  110.4 6.4 %collective-permute-done.31.got.rest_3_ = bf16[256,1024]{1,0:T(8,128)(2,1)S(1)} collective-permute-done((bf16[256,1024]{1,0:T(8,128)(2,1)S(1)}, bf16[256,1024]{1,0:T(8,128)(2,1)S(1)}, u32[]{:S(2)}, u32[]{:S(2)}) %collective-permute-start.31) | collective-permute-done | bytes 524320 | tf_op jit(solution)/shard_map/ppermute | solution.py:94
  119.5 2.7 %collective-permute-start.27 = (bf16[128,1024]{1,0:T(8,128)(2,1)S(1)}, bf16[128,1024]{1,0:T(8,128)(2,1)S(1)}, u32[]{:S(2)}, u32[]{:S(2)}) collective-permute-start(bf16[128,1024]{1,0:T(8,128)(2,1)S(1)} %get-tuple-element.114), channel_id=1, source_target_pairs={{0,16},{1,17},{2,18},{3,19},{4,20},{5,21},{6,22},{7,23},{8,24},{9,... | collective-permute-start | bytes 786440 | tf_op jit(solution)/shard_map/ppermute | solution.py:94
  126.4 13.4 %collective-permute-done.27.p2 = bf16[128,1024]{1,0:T(8,128)(2,1)S(1)} collective-permute-done((bf16[128,1024]{1,0:T(8,128)(2,1)S(1)}, bf16[128,1024]{1,0:T(8,128)(2,1)S(1)}, u32[]{:S(2)}, u32[]{:S(2)}) %collective-permute-start.27) | collective-permute-done | bytes 262176 | tf_op jit(solution)/shard_map/ppermute | solution.py:94
  143.6 2.7 %shard_map.277 = (f32[128,1024]{1,0:T(8,128)}, f32[32,1024]{1,0:T(8,128)S(1)}, bf16[32,1024]{1,0:T(8,128)(2,1)S(1)}, bf16[32,1024]{1,0:T(8,128)(2,1)S(1)}, bf16[...) custom-call(s32[2]{0:T(128)S(1)} %copy-done.9, bf16[128,1024]{1,0:T(8,128)(2,1)S(1)} %copy-done, ...), custom_call_target="tpu_custom_call" | custom-call | bytes 5313032 | tf_op jit(solution)/shard_map/pallas_call | solution.py:43
  147.8 1.9 %collective-permute-start.34 = (bf16[32,1024]{1,0:T(8,128)(2,1)S(1)}, bf16[32,1024]{1,0:T(8,128)(2,1)S(1)}, u32[]{:S(2)}, u32[]{:S(2)}) collective-permute-start(bf16[32,1024]{1,0:T(8,128)(2,1)S(1)} %get-tuple-element.141), channel_id=1, source_target_pairs={{0,16},{1,17},{2,18},{3,19},{4,20},{5,21},{6,22},{7,23},{8,24},{9,... | collective-permute-start | bytes 196616 | tf_op jit(solution)/shard_map/ppermute | solution.py:94
  153.7 6.5 %collective-permute-done.41.rest_11_ = bf16[40,768]{1,0:T(8,128)(2,1)S(1)} collective-permute-done((bf16[40,768]{1,0:T(8,128)(2,1)S(1)}, bf16[40,768]{1,0:T(8,128)(2,1)S(1)}, u32[]{:S(2)}, u32[]{:S(2)}) %collective-permute-start.41) | collective-permute-done | bytes 61472 | tf_op jit(solution)/shard_map/ppermute | solution.py:94
  160.2 2.4 %shard_map.283 = (bf16[128,1024]{1,0:T(8,128)(2,1)}, f32[32,4096]{1,0:T(8,128)}, f32[32,3072]{1,0:T(8,128)}, f32[1,128]{1,0:T(1,128)}, f32[1,96]{1,0:T(1,128)}, ...) custom-call(s32[2]{0:T(128)S(1)} %copy-done.9, ...), custom_call_target="tpu_custom_call" | custom-call | bytes 3651208 | tf_op jit(solution)/shard_map/pallas_call | solution.py:43
  (144 shorter events, 50.9 us)
Async XLA Ops:
  3.4 12.9 %collective-permute-start = (bf16[32,1792]{1,0:T(8,128)(2,1)}, bf16[32,1792]{1,0:T(8,128)(2,1)S(1)}, u32[]{:S(2)}, u32[]{:S(2)}) collective-permute-start(bf16[32,1792]{1,0:T(8,128)(2,1)} %get-tuple-element.92), channel_id=1, source_target_pairs={{0,8},{1,9},{2,10},{3,11},{4,12},{5,13},{6,14},{7,15},{8,0},{9,1},... | collective-permute-start | bytes 344072 | tf_op jit(solution)/shard_map/ppermute | solution.py:94
  6.4 12.6 %collective-permute-start.1 = (bf16[32,1792]{1,0:T(8,128)(2,1)}, bf16[32,1792]{1,0:T(8,128)(2,1)S(1)}, u32[]{:S(2)}, u32[]{:S(2)}) collective-permute-start(bf16[32,1792]{1,0:T(8,128)(2,1)} %get-tuple-element.93), channel_id=1, source_target_pairs={{0,16},{1,17},{2,18},{3,19},{4,20},{5,21},{6,22},{7,23},{8,24},{9,... | collective-permute-start | bytes 344072 | tf_op jit(solution)/shard_map/ppermute | solution.py:94
  10.7 14.7 %collective-permute-start.16 = (bf16[160,1024]{1,0:T(8,128)(2,1)}, bf16[160,1024]{1,0:T(8,128)(2,1)}, u32[]{:S(2)}, u32[]{:S(2)}) collective-permute-start(bf16[160,1024]{1,0:T(8,128)(2,1)} %get-tuple-element.103.rest_10_), channel_id=1, source_target_pairs={{0,4},{1,5},{2,6},{3,7},{4,0},{5,1},{6,2},{7,3},{8,12},{9,13},{10,... | collective-permute-start | bytes 983048 | tf_op jit(solution)/shard_map/ppermute | solution.py:97
  12.3 38.4 %all-to-all-start = ((bf16[32,8,128]{2,1,0:T(8,128)(2,1)}), bf16[32,8,128]{2,1,0:T(8,128)(2,1)S(1)}, u32[]{:S(2)}, u32[]{:S(2)}) async-start(bf16[32,8,128]{2,1,0:T(8,128)(2,1)} %get-tuple-element.90), calls=%async_computation | async-start | bytes 131072 | tf_op jit(solution)/shard_map/all_to_all | solution.py:193
  19.9 17.8 %collective-permute-start.7 = (bf16[4,32,1792]{2,1,0:T(8,128)(2,1)S(1)}, bf16[4,32,1792]{2,1,0:T(8,128)(2,1)S(1)}, u32[]{:S(2)}, u32[]{:S(2)}) collective-permute-start(bf16[4,32,1792]{2,1,0:T(8,128)(2,1)S(1)} %bitcast.28), channel_id=1, source_target_pairs={{0,4},{1,5},{2,6},{3,7},{4,0},{5,1},{6,2},{7,3},{8,12},{9,13},{10,... | collective-permute-start | bytes 1376264 | tf_op jit(solution)/shard_map/ppermute | solution.py:97
  20.9 15.4 %collective-permute-start.4 = (bf16[128,1024]{1,0:T(8,128)(2,1)}, bf16[128,1024]{1,0:T(8,128)(2,1)}, u32[]{:S(2)}, u32[]{:S(2)}) collective-permute-start(bf16[128,1024]{1,0:T(8,128)(2,1)} %rest_0_.1), channel_id=1, source_target_pairs={{0,16},{1,17},{2,18},{3,19},{4,20},{5,21},{6,22},{7,23},{8,24},{9,... | collective-permute-start | bytes 786440 | tf_op jit(solution)/shard_map/ppermute | solution.py:94
  25.4 14.9 %collective-permute-start.6 = (bf16[4,32,1792]{2,1,0:T(8,128)(2,1)S(1)}, bf16[4,32,1792]{2,1,0:T(8,128)(2,1)S(1)}, u32[]{:S(2)}, u32[]{:S(2)}) collective-permute-start(bf16[4,32,1792]{2,1,0:T(8,128)(2,1)S(1)} %bitcast.29), channel_id=1, source_target_pairs={{0,2},{1,3},{2,0},{3,1},{4,6},{5,7},{6,4},{7,5},{8,10},{9,11},{10,... | collective-permute-start | bytes 1376264 | tf_op jit(solution)/shard_map/ppermute | solution.py:97
  28.6 14.5 %collective-permute-start.10 = (bf16[4,32,1792]{2,1,0:T(8,128)(2,1)S(1)}, bf16[4,32,1792]{2,1,0:T(8,128)(2,1)S(1)}, u32[]{:S(2)}, u32[]{:S(2)}) collective-permute-start(bf16[4,32,1792]{2,1,0:T(8,128)(2,1)S(1)} %bitcast.30), channel_id=1, source_target_pairs={{0,1},{1,0},{2,3},{3,2},{4,5},{5,4},{6,7},{7,6},{8,9},{9,8},{10,11... | collective-permute-start | bytes 1376264 | tf_op jit(solution)/shard_map/ppermute | solution.py:97
  29.4 12.4 %collective-permute-start.3 = (bf16[128,1024]{1,0:T(8,128)(2,1)}, bf16[128,1024]{1,0:T(8,128)(2,1)}, u32[]{:S(2)}, u32[]{:S(2)}) collective-permute-start(bf16[128,1024]{1,0:T(8,128)(2,1)} %rest_0_.1), channel_id=1, source_target_pairs={{0,8},{1,9},{2,10},{3,11},{4,12},{5,13},{6,14},{7,15},{8,0},{9,1},... | collective-permute-start | bytes 786440 | tf_op jit(solution)/shard_map/ppermute | solution.py:94
  51.7 17.8 %collective-permute-start.23 = (bf16[128,1024]{1,0:T(8,128)(2,1)}, bf16[128,1024]{1,0:T(8,128)(2,1)S(1)}, u32[]{:S(2)}, u32[]{:S(2)}) collective-permute-start(bf16[128,1024]{1,0:T(8,128)(2,1)} %g0.1), channel_id=1, source_target_pairs={{0,8},{1,9},{2,10},{3,11},{4,12},{5,13},{6,14},{7,15},{8,0},{9,1},... | collective-permute-start | bytes 786440 | tf_op jit(solution)/shard_map/ppermute | solution.py:94
  51.9 21.6 %collective-permute-start.24 = (bf16[128,1024]{1,0:T(8,128)(2,1)}, bf16[128,1024]{1,0:T(8,128)(2,1)S(1)}, u32[]{:S(2)}, u32[]{:S(2)}) collective-permute-start(bf16[128,1024]{1,0:T(8,128)(2,1)} %g0.1), channel_id=1, source_target_pairs={{0,16},{1,17},{2,18},{3,19},{4,20},{5,21},{6,22},{7,23},{8,24},{9,... | collective-permute-start | bytes 786440 | tf_op jit(solution)/shard_map/ppermute | solution.py:94
  54.8 18.7 %collective-permute-start.25 = (bf16[128,1024]{1,0:T(8,128)(2,1)}, bf16[128,1024]{1,0:T(8,128)(2,1)S(1)}, u32[]{:S(2)}, u32[]{:S(2)}) collective-permute-start(bf16[128,1024]{1,0:T(8,128)(2,1)} %g0.1), channel_id=1, source_target_pairs={{0,24},{1,25},{2,26},{3,27},{4,28},{5,29},{6,30},{7,31},{8,16},{9,... | collective-permute-start | bytes 786440 | tf_op jit(solution)/shard_map/ppermute | solution.py:94
  78.1 30.2 %collective-permute-start.26 = (bf16[4,256,1024]{2,1,0:T(8,128)(2,1)S(1)}, bf16[4,256,1024]{2,1,0:T(8,128)(2,1)S(1)}, u32[]{:S(2)}, u32[]{:S(2)}) collective-permute-start(bf16[4,256,1024]{2,1,0:T(8,128)(2,1)S(1)} %get-tuple-element.112), channel_id=1, source_target_pairs={{0,1},{1,0},{2,3},{3,2},{4,5},{5,4},{6,7},{7,6},{8,9},{9,8},{10,11... | collective-permute-start | bytes 6291464 | tf_op jit(solution)/shard_map/ppermute | solution.py:97
  87.7 18.4 %collective-permute-start.22 = (bf16[256,1024]{1,0:T(8,128)(2,1)S(1)}, bf16[256,1024]{1,0:T(8,128)(2,1)S(1)}, u32[]{:S(2)}, u32[]{:S(2)}) collective-permute-start(bf16[256,1024]{1,0:T(8,128)(2,1)S(1)} %get-tuple-element.105), channel_id=1, source_target_pairs={{0,8},{1,9},{2,10},{3,11},{4,12},{5,13},{6,14},{7,15},{8,0},{9,1},... | collective-permute-start | bytes 1572872 | tf_op jit(solution)/shard_map/ppermute | solution.py:94
  93.3 23.4 %collective-permute-start.31 = (bf16[256,1024]{1,0:T(8,128)(2,1)S(1)}, bf16[256,1024]{1,0:T(8,128)(2,1)S(1)}, u32[]{:S(2)}, u32[]{:S(2)}) collective-permute-start(bf16[256,1024]{1,0:T(8,128)(2,1)S(1)} %get-tuple-element.137), channel_id=1, source_target_pairs={{0,8},{1,9},{2,10},{3,11},{4,12},{5,13},{6,14},{7,15},{8,0},{9,1},... | collective-permute-start | bytes 1572872 | tf_op jit(solution)/shard_map/ppermute | solution.py:94
  93.5 24.5 %collective-permute-start.37 = (bf16[136,1024]{1,0:T(8,128)(2,1)S(1)}, bf16[136,1024]{1,0:T(8,128)(2,1)S(1)}, u32[]{:S(2)}, u32[]{:S(2)}) collective-permute-start(bf16[136,1024]{1,0:T(8,128)(2,1)S(1)} %get-tuple-element.146), channel_id=1, source_target_pairs={{0,2},{1,3},{2,0},{3,1},{4,6},{5,7},{6,4},{7,5},{8,10},{9,11},{10,... | collective-permute-start | bytes 835592 | tf_op jit(solution)/shard_map/ppermute | solution.py:97
  94.9 24.6 %collective-permute-start.38 = (bf16[136,1024]{1,0:T(8,128)(2,1)S(1)}, bf16[136,1024]{1,0:T(8,128)(2,1)S(1)}, u32[]{:S(2)}, u32[]{:S(2)}) collective-permute-start(bf16[136,1024]{1,0:T(8,128)(2,1)S(1)} %get-tuple-element.147), channel_id=1, source_target_pairs={{0,4},{1,5},{2,6},{3,7},{4,0},{5,1},{6,2},{7,3},{8,12},{9,13},{10,... | collective-permute-start | bytes 835592 | tf_op jit(solution)/shard_map/ppermute | solution.py:97
  106.1 16.8 %collective-permute-start.39 = (bf16[136,1024]{1,0:T(8,128)(2,1)S(1)}, bf16[136,1024]{1,0:T(8,128)(2,1)S(1)}, u32[]{:S(2)}, u32[]{:S(2)}) collective-permute-start(bf16[136,1024]{1,0:T(8,128)(2,1)S(1)} %get-tuple-element.148), channel_id=1, source_target_pairs={{0,6},{1,7},{2,4},{3,5},{4,2},{5,3},{6,0},{7,1},{8,14},{9,15},{10,... | collective-permute-start | bytes 835592 | tf_op jit(solution)/shard_map/ppermute | solution.py:97
  109.8 30.8 %collective-permute-start.28 = (bf16[256,1024]{1,0:T(8,128)(2,1)}, bf16[256,1024]{1,0:T(8,128)(2,1)}, u32[]{:S(2)}, u32[]{:S(2)}) collective-permute-start(bf16[256,1024]{1,0:T(8,128)(2,1)} %get-tuple-element.116), channel_id=1, source_target_pairs={{0,2},{1,3},{2,0},{3,1},{4,6},{5,7},{6,4},{7,5},{8,10},{9,11},{10,... | collective-permute-start | bytes 1572872 | tf_op jit(solution)/shard_map/ppermute | solution.py:97
  116.7 24.9 %collective-permute-start.29 = (bf16[256,1024]{1,0:T(8,128)(2,1)}, bf16[256,1024]{1,0:T(8,128)(2,1)}, u32[]{:S(2)}, u32[]{:S(2)}) collective-permute-start(bf16[256,1024]{1,0:T(8,128)(2,1)} %get-tuple-element.117), channel_id=1, source_target_pairs={{0,4},{1,5},{2,6},{3,7},{4,0},{5,1},{6,2},{7,3},{8,12},{9,13},{10,... | collective-permute-start | bytes 1572872 | tf_op jit(solution)/shard_map/ppermute | solution.py:97
  118.0 23.6 %collective-permute-start.30 = (bf16[256,1024]{1,0:T(8,128)(2,1)}, bf16[256,1024]{1,0:T(8,128)(2,1)}, u32[]{:S(2)}, u32[]{:S(2)}) collective-permute-start(bf16[256,1024]{1,0:T(8,128)(2,1)} %get-tuple-element.118), channel_id=1, source_target_pairs={{0,6},{1,7},{2,4},{3,5},{4,2},{5,3},{6,0},{7,1},{8,14},{9,15},{10,... | collective-permute-start | bytes 1572872 | tf_op jit(solution)/shard_map/ppermute | solution.py:97
  119.5 20.3 %collective-permute-start.27 = (bf16[128,1024]{1,0:T(8,128)(2,1)S(1)}, bf16[128,1024]{1,0:T(8,128)(2,1)S(1)}, u32[]{:S(2)}, u32[]{:S(2)}) collective-permute-start(bf16[128,1024]{1,0:T(8,128)(2,1)S(1)} %get-tuple-element.114), channel_id=1, source_target_pairs={{0,16},{1,17},{2,18},{3,19},{4,20},{5,21},{6,22},{7,23},{8,24},{9,... | collective-permute-start | bytes 786440 | tf_op jit(solution)/shard_map/ppermute | solution.py:94
  122.9 27.8 %collective-permute-start.32 = (bf16[128,1024]{1,0:T(8,128)(2,1)}, bf16[128,1024]{1,0:T(8,128)(2,1)}, u32[]{:S(2)}, u32[]{:S(2)}) collective-permute-start(bf16[128,1024]{1,0:T(8,128)(2,1)} %shard_map.280), channel_id=1, source_target_pairs={{0,16},{1,17},{2,18},{3,19},{4,20},{5,21},{6,22},{7,23},{8,24},{9,... | collective-permute-start | bytes 786440 | tf_op jit(solution)/shard_map/ppermute | solution.py:94
  146.4 13.8 %collective-permute-start.33 = (bf16[32,1024]{1,0:T(8,128)(2,1)S(1)}, bf16[32,1024]{1,0:T(8,128)(2,1)S(1)}, u32[]{:S(2)}, u32[]{:S(2)}) collective-permute-start(bf16[32,1024]{1,0:T(8,128)(2,1)S(1)} %get-tuple-element.140), channel_id=1, source_target_pairs={{0,8},{1,9},{2,10},{3,11},{4,12},{5,13},{6,14},{7,15},{8,0},{9,1},... | collective-permute-start | bytes 196616 | tf_op jit(solution)/shard_map/ppermute | solution.py:94
  (42 other events, 453.3 us)

commit v3 on v2

--- a/solution.py
+++ b/solution.py
@@ -1,4 +1,3 @@
-import functools
 import math
 
 import jax
@@ -192,7 +191,7 @@
         tokens = blocks_of(block_in, after)
         small_in = lax.all_to_all(small_out, "dp", 0, 0, tiled=True)
         after, _ = lax.optimization_barrier((grad_out, tokens[1]))
-        grads_in = [grad_out] + [across(after, k) for k in range(1, NB)]
+        grads_in = blocks_of(grad_out, after)
 
         def pick(width_mod, off, base, width):
             return (iota((width, width_mod.shape[1]), 0) + base == off + width_mod).astype(BF)
@@ -363,8 +362,8 @@
             by_rows(T, T, fn)
 
 
-        def bwd1_body(br, live_ref, g0, g1, g2, g3, act2, hidden, dgelu, wout, *rest):
-            grad, dhid, keep, send, sum_in, term, flip = rest
+        def bwd2_body(br, live_ref, g0, g1, g2, g3, hidden, mixed, act1, q, k, v, probs, cos, sin, wo, *rest):
+            grad, dqkv, keep, send, sum_qkv, dmix, term, term_o, term_out_ref, flip = rest
             for i, g in enumerate((g0, g1, g2, g3)):
 
                 def masked(rws, i=i, g=g):
@@ -377,55 +376,18 @@
                 flip[...] = hidden[:, lanes(t, 256)].T
                 y = dot_nn(flip[...], grad[...])
                 per = 256 // ff_dev
-                term[pl.ds(t * per, per)] = y.reshape(per, ff_dev, D)
+                term_out_ref[pl.ds(t * per, per)] = y.reshape(per, ff_dev, D)
                 return carry
 
             lax.fori_loop(0, FB // 256, term_out, 0, unroll=True)
 
             def to_out(j, carry):
-                keep[j, MA:] = term[br[1] ^ (2 * j)]
-                send[j, MA:] = term[br[1] ^ (2 * j + 1)].astype(BF)
+                keep[j, MA:] = term_out_ref[br[1] ^ (2 * j)]
+                send[j, MA:] = term_out_ref[br[1] ^ (2 * j + 1)].astype(BF)
                 return carry
 
             lax.fori_loop(0, J, to_out, 0, unroll=True)
 
-            def d_hidden(t, carry):
-                cols = lanes(t, 256)
-                per = 256 // ff_dev
-                wt = wout[pl.ds(t * per, per)].reshape(256, D)
-                y = (dot_nt(grad[...], wt) * dgelu[:, cols]).astype(BF)
-                dhid[:, cols] = y
-                sum_in[:, cols] = jnp.sum(y.astype(F32), axis=0, keepdims=True)
-                return carry
-
-            lax.fori_loop(0, FB // 256, d_hidden, 0, unroll=True)
-
-            term_r = term.reshape(R * ff_dev // rows, rows, D) if ff_dev != rows else term
-
-            def term_in(t, carry):
-                flip[...] = act2[:, lanes(t, 256)].T
-                term_r[:R] = dot_nn(flip[...], dhid[...]).reshape(R, rows, D)
-                at = pl.ds(pl.multiple_of(t * rows, rows), rows)
-
-                def one_j(j, carry):
-                    keep[j, at] = term_r[br[1] ^ (2 * j)]
-                    send[j, at] = term_r[br[1] ^ (2 * j + 1)].astype(BF)
-                    return carry
-
-                return lax.fori_loop(0, J, one_j, carry, unroll=True)
-
-            lax.fori_loop(0, NB, term_in, 0, unroll=True)
-
-        grad_r, dhid, keep_f, send_f, sum_in = call(
-            bwd1_body,
-            [("s", br), ("v", live)] + [("v", g) for g in grads_in] + [("v", a) for a in (act2, hidden, dgelu, full_out)],
-            [tab, sds((NT, FB), BF), sds((J, MF, D), F32), sds((J, MF, D), BF), sds((1, FB), F32)],
-            [pltpu.VMEM((R, ff_dev, D), F32), pltpu.VMEM((256, NT), BF)],
-            flops=6 * NT * D * FB,
-        )
-
-        def bwd2_body(br, grad, mixed, act1, q, k, v, probs, cos, sin, wo, *rest):
-            dqkv, keep, send, sum_qkv, dmix, term, term_o, flip = rest
             flip[...] = mixed[...].T
             term_o[...] = dot_nn(flip[...], grad[...]).reshape(R, rows, D)
 
@@ -475,45 +437,116 @@
 
             lax.fori_loop(0, NB, term_qkv, 0, unroll=True)
 
-        dqkv, keep_a, send_a, sum_qkv = call(
+        grad_r, dqkv, keep_a, send_a, sum_qkv = call(
             bwd2_body,
-            [("s", br)] + [("v", a) for a in (grad_r, mixed, act1, q, k, v, probs, cosine, sines, full_o)],
-            [sds((NT, 3 * QB), BF), sds((J, MS, D), F32), sds((J, MS, D), BF), sds((1, 3 * QB), F32)],
-            [pltpu.VMEM((NT, QB), BF), pltpu.VMEM((R, rows, 3 * QB), F32), pltpu.VMEM((R, rows, D), F32),
+            [("s", br), ("v", live)] + [("v", g) for g in grads_in]
+            + [("v", a) for a in (hidden, mixed, act1, q, k, v, probs, cosine, sines, full_o)],
+            [tab, sds((NT, 3 * QB), BF), sds((J, MF, D), F32), sds((J, MF, D), BF), sds((1, 3 * QB), F32)],
+            [pltpu.VMEM((NT, QB), BF), pltpu.VMEM((R, rows, 3 * QB), F32), pltpu.VMEM((R, rows, D), F32), pltpu.VMEM((R, ff_dev, D), F32),
              pltpu.VMEM((256, NT), BF)],
-            flops=2 * NT * D * (3 * QB + 2 * QB) + 16 * NT * T * QB,
-        )
-
-        def merge_body(extra, keep, got, *rest):
-            size = keep.shape[1]
-            outs = rest[extra:]
-            if extra:
-                pass_body(*rest[:extra], outs[J])
+            flops=2 * NT * D * (3 * QB + 2 * QB + FB) + 16 * NT * T * QB,
+        )
+
+        def bwd1_body(br, grad, act2, dgelu, wout, *rest):
+            dhid, keep, send, sum_in, term_r, flip = rest
+
+            def d_hidden(t, carry):
+                cols = lanes(t, 256)
+                per = 256 // ff_dev
+                wt = wout[pl.ds(t * per, per)].reshape(256, D)
+                y = (dot_nt(grad[...], wt) * dgelu[:, cols]).astype(BF)
+                dhid[:, cols] = y
+                sum_in[:, cols] = jnp.sum(y.astype(F32), axis=0, keepdims=True)
+                return carry
+
+            lax.fori_loop(0, FB // 256, d_hidden, 0, unroll=True)
+
+            def term_in(t, carry):
+                flip[...] = act2[:, lanes(t, 256)].T
+                term_r[...] = dot_nn(flip[...], dhid[...]).reshape(R, rows, D)
+                at = pl.ds(pl.multiple_of(t * rows, rows), rows)
+
+                def one_j(j, carry):
+                    keep[j, at] = term_r[br[1] ^ (2 * j)]
+                    send[j, at] = term_r[br[1] ^ (2 * j + 1)].astype(BF)
+                    return carry
+
+                return lax.fori_loop(0, J, one_j, carry, unroll=True)
+
+            lax.fori_loop(0, NB, term_in, 0, unroll=True)
+
+        dhid, keep_f, send_f, sum_in = call(
+            bwd1_body,
+            [("s", br)] + [("v", a) for a in (grad_r, act2, dgelu, full_out)],
+            [sds((NT, FB), BF), sds((J, MA, D), F32), sds((J, MA, D), BF), sds((1, FB), F32)],
+            [pltpu.VMEM((R, rows, D), F32), pltpu.VMEM((256, NT), BF)],
+            flops=4 * NT * D * FB,
+        )
+
+        def merge_body(keep, got, *outs):
             for j in range(J):
-
-                def fn(rws, j=j):
-                    y = keep[j, rws] + got[j, rws].astype(F32)
-                    outs[j][rws] = y if j == 0 else y.astype(BF)
-
-                by_rows(size, size, fn)
-
-        def merge(keep, send, passed=()):
-            size = keep.shape[1]
-            got = swap(send, 1)
+                y = keep[j] + got[j].astype(F32)
+                outs[j][...] = y if j == 0 else y.astype(BF)
+
+        def merge_small_body(keep, got, keep_small, got_small, *outs):
+            for j in range(J):
+                y = keep[j] + got[j].astype(F32)
+                z = keep_small[j] + got_small[j].astype(F32)
+                outs[j][:MA] = y.astype(outs[j].dtype)
+                outs[j][MA:, :WO] = z.astype(outs[j].dtype)
+
+        def merge(keep, send, small=()):
+            size = keep.shape[1] + (8 if small else 0)
+            ins = [keep, swap(send, 1), *small]
             outs = call(
-                functools.partial(merge_body, len(passed)), [("v", a) for a in (keep, got, *passed)],
-                [sds((size, D), F32)] + [sds((size, D), BF)] * (J - 1) + [block] * bool(passed),
+                merge_small_body if small else merge_body, [("v", a) for a in ins],
+                [sds((size, D), F32)] + [sds((size, D), BF)] * (J - 1),
             )
-            return [outs[0]] + [swap(outs[j], 2 * j) for j in range(1, J)], outs[J:]
-
-        merged_f, (pass_part,) = merge(keep_f, send_f, (later_part, got_one))
+            return [outs[0]] + [swap(outs[j], 2 * j) for j in range(1, J)]
+
+        if R == 8:
+
+            def halves_body(keep, got, own, to_x, to_y, keep_x, keep_y):
+                own[...] = keep[0] + got[0].astype(F32)
+                low, high = slice(0, MA), slice(MA, MF)
+                to_x[:MA] = (keep[1, low] + got[1, low].astype(F32)).astype(BF)
+                to_x[MA:] = (keep[3, low] + got[3, low].astype(F32)).astype(BF)
+                to_y[: MF - MA] = (keep[2, high] + got[2, high].astype(F32)).astype(BF)
+                to_y[MF - MA :] = (keep[3, high] + got[3, high].astype(F32)).astype(BF)
+                keep_x[...] = keep[1, high] + got[1, high].astype(F32)
+                keep_y[...] = keep[2, low] + got[2, low].astype(F32)
+
+            assert MF == 2 * MA
+            quarter = sds((MA, D), F32)
+            own_a, to_x, to_y, keep_x, keep_y = call(
+                halves_body, [("v", keep_a), ("v", swap(send_a, 1))],
+                [sds((MF, D), F32), sds((MF, D), BF), sds((MF, D), BF), quarter, quarter],
+            )
+            got_x, got_y = swap(to_x, 2), swap(to_y, 4)
+
+            def second_body(keep_x, keep_y, got_x, got_y, to_x, to_y):
+                to_x[...] = (keep_x[...] + got_y[MA:].astype(F32)).astype(BF)
+                to_y[...] = (keep_y[...] + got_x[MA:].astype(F32)).astype(BF)
+
+            to_x, to_y = call(
+                second_body, [("v", a) for a in (keep_x, keep_y, got_x, got_y)],
+                [sds((MA, D), BF), sds((MA, D), BF)],
+            )
+            merged_a = [own_a, got_x, got_y, swap(to_x, 2), swap(to_y, 4)]
+            lower, upper = ((0, 0), (1, 0), (4, 0)), ((0, MA), (2, 0), (3, 0))
+        else:
+            merged_a = merge(keep_a, send_a)
+            lower, upper = [(j, 0) for j in range(J)], [(j, MA) for j in range(J)]
+        (pass_part,) = call(pass_body, [("v", later_part), ("v", got_one)], [block])
         got_two = across(pass_part, 2)
+
         out_widths = [FB * NB // n, 3 * D // n] + [D // n] * 5
         out_offsets = [sum(out_widths[:i]) for i in range(len(out_widths))]
         WO = -(-sum(out_widths) // 128) * 128
 
-        def bwd3_body(br, xhat, w1, dqkv, dhid, grad, sum_in, sum_qkv, g1, g2, keep_in, send_in, *rest):
-            own, later, away, keep, send, stage, gs, sums, tot, semp = rest
+        def bwd3_body(br, xhat, w1, dqkv, dhid, grad, sum_in, sum_qkv, g1, g2, *rest):
+            own, keep, send, *rest = rest
+            aways, stages, (gs, sums, tot, semp) = rest[:3], rest[3:6], rest[6:]
             gs[...] = jnp.sum(grad[:T].astype(F32), axis=0, keepdims=True)
 
             def back(t, carry):
@@ -523,16 +556,16 @@
                 xh = xhat[:, cols]
                 y = d1 * g1[:, cols] + d2 * g2[:, cols]
                 own[:, cols] = y[:T]
-                later[:, cols] = y[2 * T : 3 * T]
-                stage[:T, cols] = y[T : 2 * T].astype(BF)
-                stage[T:, cols] = y[3 * T :].astype(BF)
+                for k in range(1, NB):
+                    stages[k - 1][:, cols] = y[k * T : (k + 1) * T].astype(BF)
                 for i, z in enumerate((d1 * xh, d1, d2 * xh, d2)):
                     sums[i : i + 1, cols] = jnp.sum(z, axis=0, keepdims=True)
                 return carry
 
             lax.fori_loop(0, D // QB, back, 0, unroll=True)
-            sending = pltpu.make_async_copy(stage, away, semp)
-            sending.start()
+            sending = [pltpu.make_async_copy(a, z, semp.at[i]) for i, (a, z) in enumerate(zip(stages, aways))]
+            for c in sending:
+                c.start()
 
             total = jnp.zeros((n, WO), F32)
 
@@ -565,22 +598,21 @@
             for j in range(J):
                 for ref, m in ((keep, 2 * j), (send, 2 * j + 1)):
                     lines = [tot[pl.ds(to * R + (br[1] ^ m), 1), :] for to in range(NB)]
-                    lines.append(jnp.zeros((MS - MA - NB, WO), F32))
-                    ref[j, MA:, :WO] = jnp.concatenate(lines, axis=0).astype(ref.dtype)
-            sending.wait()
-
-        own_g, later_g, away_g, keep_a, send_a = call(
+                    lines.append(jnp.zeros((8 - NB, WO), F32))
+                    ref[j] = jnp.concatenate(lines, axis=0).astype(ref.dtype)
+            for c in sending:
+                c.wait()
+
+        own_g, keep_s, send_s, *away_g = call(
             bwd3_body,
-            [("s", br)] + [("v", a) for a in (xhat, full_one, dqkv, dhid, grad_r, sum_in, sum_qkv, gain_one, gain_two, keep_a, send_a)],
-            [sds((T, D), F32), sds((T, D), F32), sds((2 * T, D), BF), sds((J, MS, D), F32), sds((J, MS, D), BF)],
-            [pltpu.VMEM((2 * T, D), BF), pltpu.VMEM((1, D), F32), pltpu.VMEM((8, D), F32), pltpu.VMEM((n, WO), F32), dma], hbm=(2,),
-            alias={10: 3, 11: 4},
+            [("s", br)] + [("v", a) for a in (xhat, full_one, dqkv, dhid, grad_r, sum_in, sum_qkv, gain_one, gain_two)],
+            [sds((T, D), F32), sds((J, 8, WO), F32), sds((J, 8, WO), BF), block, block, block],
+            [pltpu.VMEM((T, D), BF)] * 3 + [pltpu.VMEM((1, D), F32), pltpu.VMEM((8, D), F32), pltpu.VMEM((n, WO), F32), dma((3,))],
+            hbm=(3, 4, 5),
             flops=2 * NT * D * W1,
         )
-        back_one = across(away_g, 1)
-        (pass_g,) = call(pass_body, [("v", later_g), ("v", back_one)], [block])
-        back_two = across(pass_g, 2)
-        merged_a, _ = merge(keep_a, send_a)
+        backs = [across(g, k + 1) for k, g in enumerate(away_g)]
+        merged_f = merge(keep_f, send_f, (keep_s, swap(send_s, 1)))
 
         def total_body(x, live_ref, bo, own, p1, p2, out):
             def fn(rws):
@@ -589,76 +621,77 @@
 
             by_rows(T, T, fn)
 
-        def plane_f_body(br, x, live_ref, bo, own, p1, p2, *rest):
-            got, (w_out_ref, z0, z1, z2, z3, out) = rest[:J], rest[J:]
-            total_body(x, live_ref, bo, own, p1, p2, out)
-
-            def out_rows(rws):
-                y = got[0][pl.ds(pl.multiple_of(MA + rws.start, 8), rws.size)]
+        (block_out,) = call(
+            total_body,
+            [("v", a) for a in (block_in, live[:T], bias_o, own_part, got_one, got_two)], [block],
+        )
+
+        def plane_f_body(br, *rest):
+            got, (z0, z1, z2, z3) = rest[:J], rest[J:]
+
+            def total_of(at, low, high):
+                y = got[0][at, low:high]
                 for ref in got[1:]:
-                    y = y + ref[pl.ds(pl.multiple_of(MA + rws.start, 8), rws.size)].astype(F32)
-                w_out_ref[rws] = y
-
-            by_rows(ff_dev, min(32, ff_dev), out_rows)
+                    y = y + ref[at, low:high].astype(F32)
+                return y
+
+            lines = total_of(slice(MA, MS), 0, WO)
             for k, ref in enumerate((z0, z1, z2, z3)):
                 at = pl.ds(pl.multiple_of((br[0] ^ k) * rows, rows), rows)
-                y = got[0][at]
-                for other in got[1:]:
-                    y = y + other[at].astype(F32)
-                ref[...] = y if k == 0 else y.astype(BF)
-
-        grad_w_out, zf0, *zf, block_out = call(
-            plane_f_body,
-            [("s", br)] + [("v", a) for a in (block_in, live[:T], bias_o, own_part, got_one, got_two, *merged_f)],
-            [sds((ff_dev, D), F32), sds((rows, FB), F32)] + [sds((rows, FB), BF)] * 3 + [block],
+                ref[:rows] = total_of(at, 0, FB).astype(ref.dtype)
+                y = jnp.sum(jnp.where(iota(lines.shape, 0) == (br[0] ^ k), lines, 0.0), axis=0, keepdims=True)
+                ref[rows:, :WO] = jnp.broadcast_to(y, (8, WO)).astype(ref.dtype)
+
+        zf0, *zf = call(
+            plane_f_body, [("s", br)] + [("v", a) for a in merged_f],
+            [sds((rows + 8, FB), F32)] + [sds((rows + 8, FB), BF)] * 3,
         )
 
         def plane_a_body(br, *rest):
-            got, (w_o_ref, z0, z1, z2, z3) = rest[:J], rest[J:]
+            got, (w_o_ref, w_out_ref, z0, z1, z2, z3) = rest[: len(merged_a)], rest[len(merged_a) :]
+
+            def total_of(part, start, size, low, high):
+                y = 0.0
+                for which, first in part:
+                    at = first + start
+                    if not isinstance(at, int):
+                        at = pl.multiple_of(at, 8)
+                    y = y + got[which][pl.ds(at, size), low:high].astype(F32)
+                return y
+
+            w_out_ref[...] = total_of(upper, 0, ff_dev, 0, D)
             for c in range(NB):
-                y = got[0][c * rows : (c + 1) * rows, 3 * QB :]
-                for other in got[1:]:
-                    y = y + other[c * rows : (c + 1) * rows, 3 * QB :].astype(F32)
-                w_o_ref[:, c * QB : (c + 1) * QB] = y
+                w_o_ref[:, c * QB : (c + 1) * QB] = total_of(lower, c * rows, rows, 3 * QB, D)
             for k, ref in enumerate((z0, z1, z2, z3)):
-                at = pl.ds(pl.multiple_of((br[0] ^ k) * rows, rows), rows)
-                y = got[0][at, : 3 * QB]
-                for other in got[1:]:
-                    y = y + other[at, : 3 * QB].astype(F32)
-                ref[:rows] = y if k == 0 else y.astype(BF)
-                y = got[0][MA:, :WO]
-                for other in got[1:]:
-                    y = y + other[MA:, :WO].astype(F32)
-                y = jnp.sum(jnp.where(iota(y.shape, 0) == (br[0] ^ k), y, 0.0), axis=0, keepdims=True)
-                ref[rows:, :WO] = jnp.broadcast_to(y, (8, WO)).astype(ref.dtype)
-
-        grad_w_o, za0, *za = call(
+                ref[...] = total_of(lower, (br[0] ^ k) * rows, rows, 0, 3 * QB).astype(ref.dtype)
+
+        grad_w_o, grad_w_out, za0, *za = call(
             plane_a_body, [("s", br)] + [("v", a) for a in merged_a],
-            [sds((rows, D), F32), sds((rows + 8, 3 * QB), F32)] + [sds((rows + 8, 3 * QB), BF)] * 3,
+            [sds((rows, D), F32), sds((ff_dev, D), F32), sds((rows, 3 * QB), F32)] + [sds((rows, 3 * QB), BF)] * 3,
         )
         zf = [zf0] + [across(z, k + 1) for k, z in enumerate(zf)]
         za = [za0] + [across(z, k + 1) for k, z in enumerate(za)]
 
-        def place_f_body(br, z0, z1, z2, z3, out):
-            for k, ref in enumerate((z0, z1, z2, z3)):
-                out[:, lanes(br[0] ^ k, FB)] = ref[...].astype(F32)
-
         small_order = (0, 1, 2, 2, 3, 4, 5, 6)
 
-        def place_a_body(br, z0, z1, z2, z3, out, *small):
+        def place_f_body(br, z0, z1, z2, z3, out, *small):
             y = sum(ref[rows:, :WO].astype(F32) for ref in (z0, z1, z2, z3))
             for ref, which in zip(small, small_order):
                 ref[...] = y[:1, out_offsets[which] : out_offsets[which] + out_widths[which]]
             for k, ref in enumerate((z0, z1, z2, z3)):
+                out[:, lanes(br[0] ^ k, FB)] = ref[:rows].astype(F32)
+
+        def place_a_body(br, z0, z1, z2, z3, out):
+            for k, ref in enumerate((z0, z1, z2, z3)):
                 at = br[0] ^ k
                 for s in range(3):
-                    out[:, lanes(s * NB + at, QB)] = ref[:rows, s * QB : (s + 1) * QB].astype(F32)
-
-        def input_body(x, grad, own, p1, p2, out):
+                    out[:, lanes(s * NB + at, QB)] = ref[:, s * QB : (s + 1) * QB].astype(F32)
+
+        def input_body(x, grad, own, p1, p2, p3, out):
             def fn(rws):
                 centered, rstd = stats(x[rws].astype(F32))
                 xh = centered * rstd
-                g = own[rws] + p1[rws].astype(F32) + p2[rws].astype(F32)
+                g = own[rws] + p1[rws].astype(F32) + p2[rws].astype(F32) + p3[rws].astype(F32)
                 mean_g = jnp.mean(g, axis=-1, keepdims=True)
                 mean_gx = jnp.mean(g * xh, axis=-1, keepdims=True)
                 out[rws] = (grad[rws].astype(F32) + rstd * (g - mean_g - xh * mean_gx)).astype(BF)
@@ -666,14 +699,14 @@
             by_rows(T, T, fn)
 
         def final_body(br, *rest):
-            ins, outs = rest[:13], rest[13:]
-            place_f_body(br, *ins[5:9], outs[1])
-            input_body(*ins[:5], outs[0])
-            place_a_body(br, *ins[9:13], *outs[2:])
+            ins, outs = rest[:14], rest[14:]
+            place_f_body(br, *ins[6:10], outs[1], *outs[3:])
+            place_a_body(br, *ins[10:14], outs[2])
+            input_body(*ins[:6], outs[0])
 
         grad_input, grad_w_in, grad_w_qkv, *outs = call(
             final_body,
-            [("s", br)] + [("v", a) for a in (block_in, grad_r[:T], own_g, back_one, back_two, *zf, *za)],
+            [("s", br)] + [("v", a) for a in (block_in, grad_r[:T], own_g, *backs, *zf, *za)],
             [block, sds((rows, NB * FB), F32), sds((rows, 3 * D), F32)] + [sds((1, out_widths[i]), F32) for i in small_order],
         )
         outs = [o.reshape(-1) for o in outs]

time: 163 us -> 164 us (level)
  waiting for transfers between devices: 55 us -> 58.2 us
  starting transfers between devices: 57 us -> 55 us
  Pallas kernels: 35.2 us -> 33.4 us
    ppermute x24 -> x26, waiting for transfers between devices: 5.15 us -> 22.6 us  [swap(): return lax.ppermute(v, 'dp', [(d, d ^ mask) for d in range(n)])]
    ppermute x19 -> x20, waiting for transfers between devices: 49.9 us -> 35.7 us  [across(): return lax.ppermute(v, 'dp', [(d, d ^ mask * R) for d in range(n)])]
    ppermute x19 -> x20, starting transfers between devices: 33 us -> 29.6 us  [across(): return lax.ppermute(v, 'dp', [(d, d ^ mask * R) for d in range(n)])]
    pallas_call x12 -> x14, Pallas kernels: 35.2 us -> 33.4 us  [call(): pl.pallas_call(body, out_shape=tuple(outs), in_specs=[pl.BlockSpec(memory...]
    ppermute x24 -> x26, starting transfers between devices: 20 us -> 21.5 us  [swap(): return lax.ppermute(v, 'dp', [(d, d ^ mask) for d in range(n)])]
    unnamed x44 -> x50, local copies, waits for them, and re-layouts: 9.79 us -> 9.77 us
  transfers between devices with their start and end apart: 44 -> 47, of which waited for: 13 -> 13; matrix products, arithmetic and copies ran while one was open for 3% -> 3% of each run, Pallas kernels for 16% -> 13%
where the time goes in v3:
time: 164 us
  waiting for transfers between devices  58.2 us (35%)
  starting transfers between devices  55 us (34%)
  Pallas kernels  33.4 us (20%)
  local copies, waits for them, and re-layouts  10.7 us (7%)
  other arithmetic  4.84 us (3%)
    ppermute x20, waiting for transfers between devices, across(): return lax.ppermute(v, 'dp', [(d, d ^ mask * R) for d in range(n)])  35.7 us
    pallas_call x14, Pallas kernels, call(): pl.pallas_call(body, out_shape=tuple(outs), in_specs=[pl.BlockSpec(memory...  33.4 us
    ppermute x20, starting transfers between devices, across(): return lax.ppermute(v, 'dp', [(d, d ^ mask * R) for d in range(n)])  29.6 us
    ppermute x26, waiting for transfers between devices, swap(): return lax.ppermute(v, 'dp', [(d, d ^ mask) for d in range(n)])  22.6 us
    ppermute x26, starting transfers between devices, swap(): return lax.ppermute(v, 'dp', [(d, d ^ mask) for d in range(n)])  21.5 us
    unnamed x50, local copies, waits for them, and re-layouts  9.77 us
    all_to_all x1, starting transfers between devices, on_device(): small_in = lax.all_to_all(small_out, 'dp', 0, 0, tiled=True)  3.97 us
  transfers between devices with their start and end apart: 47, of which 13 were waited for; matrix products, arithmetic and copies ran while one was open for 3% of the time, Pallas kernels for 13%

profile of v3, /device:TPU:0, one launch (start us, length us, event | category | flops | bytes accessed | tf_op | source)
XLA Modules:
  0.0 163.6 jit_solution(6354606505505502572)
XLA Ops:
  1.3 2.1 %shard_map.272 = (bf16[32,1792]{1,0:T(8,128)(2,1)}, bf16[32,1792]{1,0:T(8,128)(2,1)}, bf16[32,1792]{1,0:T(8,128)(2,1)}, bf16[32,1792]{1,0:T(8,128)(2,1)}, bf16[1...) custom-call(s32[2]{0:T(128)} %pad_add_fusion.1.br, bf16[32,3072]{1,0:T(8,128)(2,1)} %qkv_ref.1, bf16[32,4096]{1,0:T(8,128)(2,1)} %in_ref.1, ...), custom_call_target="tpu_custom_call" | custom-call | bytes 1639240 | tf_op jit(solution)/shard_map/pallas_call | solution.py:42
  3.4 3.1 %collective-permute-start = (bf16[32,1792]{1,0:T(8,128)(2,1)}, bf16[32,1792]{1,0:T(8,128)(2,1)S(1)}, u32[]{:S(2)}, u32[]{:S(2)}) collective-permute-start(bf16[32,1792]{1,0:T(8,128)(2,1)} %get-tuple-element.94), channel_id=1, source_target_pairs={{0,8},{1,9},{2,10},{3,11},{4,12},{5,13},{6,14},{7,15},{8,0},{9,1},... | collective-permute-start | bytes 344072 | tf_op jit(solution)/shard_map/ppermute | solution.py:93
  6.5 2.6 %collective-permute-start.1 = (bf16[32,1792]{1,0:T(8,128)(2,1)}, bf16[32,1792]{1,0:T(8,128)(2,1)S(1)}, u32[]{:S(2)}, u32[]{:S(2)}) collective-permute-start(bf16[32,1792]{1,0:T(8,128)(2,1)} %get-tuple-element.95), channel_id=1, source_target_pairs={{0,16},{1,17},{2,18},{3,19},{4,20},{5,21},{6,22},{7,23},{8,24},{9,... | collective-permute-start | bytes 344072 | tf_op jit(solution)/shard_map/ppermute | solution.py:93
  12.3 4.0 %all-to-all-start = ((bf16[32,8,128]{2,1,0:T(8,128)(2,1)}), bf16[32,8,128]{2,1,0:T(8,128)(2,1)S(1)}, u32[]{:S(2)}, u32[]{:S(2)}) async-start(bf16[32,8,128]{2,1,0:T(8,128)(2,1)} %get-tuple-element.92), calls=%async_computation | async-start | bytes 131072 | tf_op jit(solution)/shard_map/all_to_all | solution.py:192
  16.3 2.7 %collective-permute-start.17 = (bf16[160,1024]{1,0:T(8,128)(2,1)}, bf16[160,1024]{1,0:T(8,128)(2,1)}, u32[]{:S(2)}, u32[]{:S(2)}) collective-permute-start(bf16[160,1024]{1,0:T(8,128)(2,1)} %get-tuple-element.105.rest_10_), channel_id=1, source_target_pairs={{0,6},{1,7},{2,4},{3,5},{4,2},{5,3},{6,0},{7,1},{8,14},{9,15},{10,... | collective-permute-start | bytes 983048 | tf_op jit(solution)/shard_map/ppermute | solution.py:96
  25.6 3.1 %collective-permute-done.17.rest_13_ = bf16[160,1024]{1,0:T(8,128)(2,1)} collective-permute-done((bf16[160,1024]{1,0:T(8,128)(2,1)}, bf16[160,1024]{1,0:T(8,128)(2,1)}, u32[]{:S(2)}, u32[]{:S(2)}) %collective-permute-start.17) | collective-permute-done | bytes 327712 | tf_op jit(solution)/shard_map/ppermute | solution.py:96
  33.0 5.5 %collective-permute-done.4.h2 = bf16[128,1024]{1,0:T(8,128)(2,1)} collective-permute-done((bf16[128,1024]{1,0:T(8,128)(2,1)}, bf16[128,1024]{1,0:T(8,128)(2,1)}, u32[]{:S(2)}, u32[]{:S(2)}) %collective-permute-start.4) | collective-permute-done | bytes 262176 | tf_op jit(solution)/shard_map/ppermute | solution.py:93
  38.6 3.5 %collective-permute-start.5 = (bf16[128,1024]{1,0:T(8,128)(2,1)}, bf16[128,1024]{1,0:T(8,128)(2,1)S(1)}, u32[]{:S(2)}, u32[]{:S(2)}) collective-permute-start(bf16[128,1024]{1,0:T(8,128)(2,1)} %collective-permute-done.4.h2), channel_id=1, source_target_pairs={{0,8},{1,9},{2,10},{3,11},{4,12},{5,13},{6,14},{7,15},{8,0},{9,1},... | collective-permute-start | bytes 786440 | tf_op jit(solution)/shard_map/ppermute | solution.py:93
  44.5 8.8 %collective-permute-done.5.h3 = bf16[128,1024]{1,0:T(8,128)(2,1)S(1)} collective-permute-done((bf16[128,1024]{1,0:T(8,128)(2,1)}, bf16[128,1024]{1,0:T(8,128)(2,1)S(1)}, u32[]{:S(2)}, u32[]{:S(2)}) %collective-permute-start.5) | collective-permute-done | bytes 262176 | tf_op jit(solution)/shard_map/ppermute | solution.py:93
  56.6 3.5 %collective-permute-done.9.rest_4_ = bf16[2,32,1792]{2,1,0:T(8,128)(2,1)} collective-permute-done((bf16[2,32,1792]{2,1,0:T(8,128)(2,1)S(1)}, bf16[2,32,1792]{2,1,0:T(8,128)(2,1)}, u32[]{:S(2)}, u32[]{:S(2)}) %collective-permute-start.9) | collective-permute-done | bytes 229408 | tf_op jit(solution)/shard_map/ppermute | solution.py:96
  61.4 2.0 %collective-permute-start.26 = (bf16[128,1024]{1,0:T(8,128)(2,1)}, bf16[128,1024]{1,0:T(8,128)(2,1)S(1)}, u32[]{:S(2)}, u32[]{:S(2)}) collective-permute-start(bf16[128,1024]{1,0:T(8,128)(2,1)} %collective-permute-done.25.g2), channel_id=1, source_target_pairs={{0,8},{1,9},{2,10},{3,11},{4,12},{5,13},{6,14},{7,15},{8,0},{9,1},... | collective-permute-start | bytes 786440 | tf_op jit(solution)/shard_map/ppermute | solution.py:93
  67.3 9.4 %shard_map.274 = (bf16[512,1024]{1,0:T(8,128)(2,1)S(1)}, bf16[512,1024]{1,0:T(8,128)(2,1)S(1)}, bf16[512,256]{1,0:T(8,128)(2,1)S(1)}, bf16[512,256]{1,0:T(8,128)...) custom-call(s32[2]{0:T(128)S(1)} %copy-done.11, ...), custom_call_target="tpu_custom_call" | custom-call | flops 3355443200 | bytes 25451528 | tf_op jit(solution)/shard_map/pallas_call | solution.py:42
  76.8 6.7 %shard_map.277 = (bf16[512,1024]{1,0:T(8,128)(2,1)S(1)}, bf16[512,768]{1,0:T(8,128)(2,1)S(1)}, f32[4,256,1024]{2,1,0:T(8,128)S(1)}, bf16[4,256,1024]{2,1,0:T(8,128)(2,1)S(1)}, f32[1,768]{1,0:T(1,128)S(1)}) custom-call(s32[2]{0:T(128)S(1)} %copy-done.11, f32[512,1]{1,0:T(8,128)S(1)} %copy.35.live_ref, bf16[128,1024]{1,0:T(8,128)(2,1)S(1)} %copy-done.18, ...), custom_call_target="tpu_custom_call" | custom-call | flops 2684354560 | bytes 14423048 | tf_op jit(solution)/shard_map/pallas_call | solution.py:42
  83.5 3.1 %shard_map.278 = (bf16[512,1024]{1,0:T(8,128)(2,1)S(1)}, f32[4,128,1024]{2,1,0:T(8,128)S(1)}, bf16[4,128,1024]{2,1,0:T(8,128)(2,1)S(1)}, f32[1,1024]{1,0:T(1,128)S(1)}) custom-call(s32[2]{0:T(128)S(1)} %copy-done.11, bf16[512,1024]{1,0:T(8,128)(2,1)S(1)} %get-tuple-element.118.grad, bf16[512,1024]{1,0:T(8,128)(2,1)S(1)} %get-tuple-element.122.act2, ...), custom_call_target="tpu_custom_call" | custom-call | flops 2147483648 | bytes 10489864 | tf_op jit(solution)/shard_map/pallas_call | solution.py:42
  90.2 4.2 %shard_map.279 = (f32[128,1024]{1,0:T(8,128)S(1)}, f32[4,8,384]{2,1,0:T(8,128)S(1)}, bf16[4,8,384]{2,1,0:T(8,128)(2,1)S(1)}, bf16[128,1024]{1,0:T(8,128)(2,1)S(1...) custom-call(s32[2]{0:T(128)S(1)} %copy-done.11, f32[512,1024]{1,0:T(8,128)S(1)} %get-tuple-element.119.xhat, ...), custom_call_target="tpu_custom_call" | custom-call | flops 1879048192 | bytes 10050568 | tf_op jit(solution)/shard_map/pallas_call | solution.py:42
  97.9 4.9 %collective-permute-done.39.got_x.rest_1_ = bf16[256,1024]{1,0:T(8,128)(2,1)S(1)} collective-permute-done((bf16[256,1024]{1,0:T(8,128)(2,1)S(1)}, bf16[256,1024]{1,0:T(8,128)(2,1)S(1)}, u32[]{:S(2)}, u32[]{:S(2)}) %collective-permute-start.39) | collective-permute-done | bytes 524320 | tf_op jit(solution)/shard_map/ppermute | solution.py:96
  106.6 2.3 %collective-permute-done.32.rest_1_ = bf16[136,1024]{1,0:T(8,128)(2,1)S(1)} collective-permute-done((bf16[136,1024]{1,0:T(8,128)(2,1)S(1)}, bf16[136,1024]{1,0:T(8,128)(2,1)S(1)}, u32[]{:S(2)}, u32[]{:S(2)}) %collective-permute-start.32) | collective-permute-done | bytes 278560 | tf_op jit(solution)/shard_map/ppermute | solution.py:96
  108.9 6.1 %collective-permute-done.33.rest_2_ = bf16[136,1024]{1,0:T(8,128)(2,1)S(1)} collective-permute-done((bf16[136,1024]{1,0:T(8,128)(2,1)S(1)}, bf16[136,1024]{1,0:T(8,128)(2,1)S(1)}, u32[]{:S(2)}, u32[]{:S(2)}) %collective-permute-start.33) | collective-permute-done | bytes 278560 | tf_op jit(solution)/shard_map/ppermute | solution.py:96
  115.0 2.1 %collective-permute-start.28 = (bf16[128,1024]{1,0:T(8,128)(2,1)S(1)}, bf16[128,1024]{1,0:T(8,128)(2,1)S(1)}, u32[]{:S(2)}, u32[]{:S(2)}) collective-permute-start(bf16[128,1024]{1,0:T(8,128)(2,1)S(1)} %get-tuple-element.130), channel_id=1, source_target_pairs={{0,16},{1,17},{2,18},{3,19},{4,20},{5,21},{6,22},{7,23},{8,24},{9,... | collective-permute-start | bytes 786440 | tf_op jit(solution)/shard_map/ppermute | solution.py:93
  126.2 15.7 %collective-permute-done.28.rest_4_ = bf16[128,1024]{1,0:T(8,128)(2,1)S(1)} collective-permute-done((bf16[128,1024]{1,0:T(8,128)(2,1)S(1)}, bf16[128,1024]{1,0:T(8,128)(2,1)S(1)}, u32[]{:S(2)}, u32[]{:S(2)}) %collective-permute-start.28) | collective-permute-done | bytes 262176 | tf_op jit(solution)/shard_map/ppermute | solution.py:93
  141.9 1.9 %collective-permute-start.37 = (bf16[40,1024]{1,0:T(8,128)(2,1)}, bf16[40,1024]{1,0:T(8,128)(2,1)}, u32[]{:S(2)}, u32[]{:S(2)}) collective-permute-start(bf16[40,1024]{1,0:T(8,128)(2,1)} %get-tuple-element.143), channel_id=1, source_target_pairs={{0,24},{1,25},{2,26},{3,27},{4,28},{5,29},{6,30},{7,31},{8,16},{9,... | collective-permute-start | bytes 245768 | tf_op jit(solution)/shard_map/ppermute | solution.py:93
  144.6 4.2 %collective-permute-start.43 = (bf16[32,768]{1,0:T(8,128)(2,1)}, bf16[32,768]{1,0:T(8,128)(2,1)}, u32[]{:S(2)}, u32[]{:S(2)}) collective-permute-start(bf16[32,768]{1,0:T(8,128)(2,1)} %get-tuple-element.154), channel_id=1, source_target_pairs={{0,8},{1,9},{2,10},{3,11},{4,12},{5,13},{6,14},{7,15},{8,0},{9,1},... | collective-permute-start | bytes 147464 | tf_op jit(solution)/shard_map/ppermute | solution.py:93
  148.8 5.1 %collective-permute-done.23.p2 = bf16[128,1024]{1,0:T(8,128)(2,1)S(1)} collective-permute-done((bf16[128,1024]{1,0:T(8,128)(2,1)S(1)}, bf16[128,1024]{1,0:T(8,128)(2,1)S(1)}, u32[]{:S(2)}, u32[]{:S(2)}) %collective-permute-start.23) | collective-permute-done | bytes 262176 | tf_op jit(solution)/shard_map/ppermute | solution.py:93
  160.9 2.5 %shard_map.285 = (bf16[128,1024]{1,0:T(8,128)(2,1)}, f32[32,4096]{1,0:T(8,128)}, f32[32,3072]{1,0:T(8,128)}, f32[1,128]{1,0:T(1,128)}, f32[1,96]{1,0:T(1,128)}, ...) custom-call(s32[2]{0:T(128)S(1)} %copy-done.12, ...), custom_call_target="tpu_custom_call" | custom-call | bytes 3671688 | tf_op jit(solution)/shard_map/pallas_call | solution.py:42
  (158 shorter events, 52.9 us)
Async XLA Ops:
  12.3 47.9 %all-to-all-start = ((bf16[32,8,128]{2,1,0:T(8,128)(2,1)}), bf16[32,8,128]{2,1,0:T(8,128)(2,1)S(1)}, u32[]{:S(2)}, u32[]{:S(2)}) async-start(bf16[32,8,128]{2,1,0:T(8,128)(2,1)} %get-tuple-element.92), calls=%async_computation | async-start | bytes 131072 | tf_op jit(solution)/shard_map/all_to_all | solution.py:192
  21.5 17.1 %collective-permute-start.6 = (bf16[4,32,1792]{2,1,0:T(8,128)(2,1)S(1)}, bf16[4,32,1792]{2,1,0:T(8,128)(2,1)S(1)}, u32[]{:S(2)}, u32[]{:S(2)}) collective-permute-start(bf16[4,32,1792]{2,1,0:T(8,128)(2,1)S(1)} %bitcast.28), channel_id=1, source_target_pairs={{0,2},{1,3},{2,0},{3,1},{4,6},{5,7},{6,4},{7,5},{8,10},{9,11},{10,... | collective-permute-start | bytes 1376264 | tf_op jit(solution)/shard_map/ppermute | solution.py:96
  23.0 15.5 %collective-permute-start.4 = (bf16[128,1024]{1,0:T(8,128)(2,1)}, bf16[128,1024]{1,0:T(8,128)(2,1)}, u32[]{:S(2)}, u32[]{:S(2)}) collective-permute-start(bf16[128,1024]{1,0:T(8,128)(2,1)} %rest_0_.1), channel_id=1, source_target_pairs={{0,16},{1,17},{2,18},{3,19},{4,20},{5,21},{6,22},{7,23},{8,24},{9,... | collective-permute-start | bytes 786440 | tf_op jit(solution)/shard_map/ppermute | solution.py:93
  28.7 14.4 %collective-permute-start.7 = (bf16[4,32,1792]{2,1,0:T(8,128)(2,1)S(1)}, bf16[4,32,1792]{2,1,0:T(8,128)(2,1)S(1)}, u32[]{:S(2)}, u32[]{:S(2)}) collective-permute-start(bf16[4,32,1792]{2,1,0:T(8,128)(2,1)S(1)} %bitcast.29), channel_id=1, source_target_pairs={{0,4},{1,5},{2,6},{3,7},{4,0},{5,1},{6,2},{7,3},{8,12},{9,13},{10,... | collective-permute-start | bytes 1376264 | tf_op jit(solution)/shard_map/ppermute | solution.py:96
  32.5 22.9 %collective-permute-start.19 = (bf16[160,1024]{1,0:T(8,128)(2,1)}, bf16[160,1024]{1,0:T(8,128)(2,1)}, u32[]{:S(2)}, u32[]{:S(2)}) collective-permute-start(bf16[160,1024]{1,0:T(8,128)(2,1)} %collective-permute-done.15.rest_11_), channel_id=1, source_target_pairs={{0,1},{1,0},{2,3},{3,2},{4,5},{5,4},{6,7},{7,6},{8,9},{9,8},{10,11... | collective-permute-start | bytes 983048 | tf_op jit(solution)/shard_map/ppermute | solution.py:96
  38.6 16.9 %collective-permute-start.25 = (bf16[128,1024]{1,0:T(8,128)(2,1)}, bf16[128,1024]{1,0:T(8,128)(2,1)}, u32[]{:S(2)}, u32[]{:S(2)}) collective-permute-start(bf16[128,1024]{1,0:T(8,128)(2,1)} %g0.1), channel_id=1, source_target_pairs={{0,16},{1,17},{2,18},{3,19},{4,20},{5,21},{6,22},{7,23},{8,24},{9,... | collective-permute-start | bytes 786440 | tf_op jit(solution)/shard_map/ppermute | solution.py:93
  38.6 14.7 %collective-permute-start.5 = (bf16[128,1024]{1,0:T(8,128)(2,1)}, bf16[128,1024]{1,0:T(8,128)(2,1)S(1)}, u32[]{:S(2)}, u32[]{:S(2)}) collective-permute-start(bf16[128,1024]{1,0:T(8,128)(2,1)} %collective-permute-done.4.h2), channel_id=1, source_target_pairs={{0,8},{1,9},{2,10},{3,11},{4,12},{5,13},{6,14},{7,15},{8,0},{9,1},... | collective-permute-start | bytes 786440 | tf_op jit(solution)/shard_map/ppermute | solution.py:93
  61.3 15.4 %collective-permute-start.24 = (bf16[128,1024]{1,0:T(8,128)(2,1)S(1)}, bf16[128,1024]{1,0:T(8,128)(2,1)S(1)}, u32[]{:S(2)}, u32[]{:S(2)}) collective-permute-start(bf16[128,1024]{1,0:T(8,128)(2,1)S(1)} %copy-done.18), channel_id=1, source_target_pairs={{0,8},{1,9},{2,10},{3,11},{4,12},{5,13},{6,14},{7,15},{8,0},{9,1},... | collective-permute-start | bytes 786440 | tf_op jit(solution)/shard_map/ppermute | solution.py:93
  61.4 15.4 %collective-permute-start.26 = (bf16[128,1024]{1,0:T(8,128)(2,1)}, bf16[128,1024]{1,0:T(8,128)(2,1)S(1)}, u32[]{:S(2)}, u32[]{:S(2)}) collective-permute-start(bf16[128,1024]{1,0:T(8,128)(2,1)} %collective-permute-done.25.g2), channel_id=1, source_target_pairs={{0,8},{1,9},{2,10},{3,11},{4,12},{5,13},{6,14},{7,15},{8,0},{9,1},... | collective-permute-start | bytes 786440 | tf_op jit(solution)/shard_map/ppermute | solution.py:93
  88.0 14.9 %collective-permute-start.39 = (bf16[256,1024]{1,0:T(8,128)(2,1)S(1)}, bf16[256,1024]{1,0:T(8,128)(2,1)S(1)}, u32[]{:S(2)}, u32[]{:S(2)}) collective-permute-start(bf16[256,1024]{1,0:T(8,128)(2,1)S(1)} %get-tuple-element.147), channel_id=1, source_target_pairs={{0,2},{1,3},{2,0},{3,1},{4,6},{5,7},{6,4},{7,5},{8,10},{9,11},{10,... | collective-permute-start | bytes 1572872 | tf_op jit(solution)/shard_map/ppermute | solution.py:96
  88.6 15.7 %collective-permute-start.40 = (bf16[256,1024]{1,0:T(8,128)(2,1)S(1)}, bf16[256,1024]{1,0:T(8,128)(2,1)S(1)}, u32[]{:S(2)}, u32[]{:S(2)}) collective-permute-start(bf16[256,1024]{1,0:T(8,128)(2,1)S(1)} %get-tuple-element.148), channel_id=1, source_target_pairs={{0,4},{1,5},{2,6},{3,7},{4,0},{5,1},{6,2},{7,3},{8,12},{9,13},{10,... | collective-permute-start | bytes 1572872 | tf_op jit(solution)/shard_map/ppermute | solution.py:96
  90.1 15.9 %collective-permute-start.22 = (bf16[256,1024]{1,0:T(8,128)(2,1)S(1)}, bf16[256,1024]{1,0:T(8,128)(2,1)S(1)}, u32[]{:S(2)}, u32[]{:S(2)}) collective-permute-start(bf16[256,1024]{1,0:T(8,128)(2,1)S(1)} %get-tuple-element.107), channel_id=1, source_target_pairs={{0,8},{1,9},{2,10},{3,11},{4,12},{5,13},{6,14},{7,15},{8,0},{9,1},... | collective-permute-start | bytes 1572872 | tf_op jit(solution)/shard_map/ppermute | solution.py:93
  97.4 17.6 %collective-permute-start.33 = (bf16[136,1024]{1,0:T(8,128)(2,1)S(1)}, bf16[136,1024]{1,0:T(8,128)(2,1)S(1)}, u32[]{:S(2)}, u32[]{:S(2)}) collective-permute-start(bf16[136,1024]{1,0:T(8,128)(2,1)S(1)} %get-tuple-element.138), channel_id=1, source_target_pairs={{0,4},{1,5},{2,6},{3,7},{4,0},{5,1},{6,2},{7,3},{8,12},{9,13},{10,... | collective-permute-start | bytes 835592 | tf_op jit(solution)/shard_map/ppermute | solution.py:96
  102.9 14.2 %collective-permute-start.34 = (bf16[136,1024]{1,0:T(8,128)(2,1)S(1)}, bf16[136,1024]{1,0:T(8,128)(2,1)S(1)}, u32[]{:S(2)}, u32[]{:S(2)}) collective-permute-start(bf16[136,1024]{1,0:T(8,128)(2,1)S(1)} %get-tuple-element.139), channel_id=1, source_target_pairs={{0,6},{1,7},{2,4},{3,5},{4,2},{5,3},{6,0},{7,1},{8,14},{9,15},{10,... | collective-permute-start | bytes 835592 | tf_op jit(solution)/shard_map/ppermute | solution.py:96
  104.5 15.2 %collective-permute-start.41 = (bf16[128,1024]{1,0:T(8,128)(2,1)S(1)}, bf16[128,1024]{1,0:T(8,128)(2,1)S(1)}, u32[]{:S(2)}, u32[]{:S(2)}) collective-permute-start(bf16[128,1024]{1,0:T(8,128)(2,1)S(1)} %get-tuple-element.151), channel_id=1, source_target_pairs={{0,2},{1,3},{2,0},{3,1},{4,6},{5,7},{6,4},{7,5},{8,10},{9,11},{10,... | collective-permute-start | bytes 786440 | tf_op jit(solution)/shard_map/ppermute | solution.py:96
  106.0 16.7 %collective-permute-start.42 = (bf16[128,1024]{1,0:T(8,128)(2,1)S(1)}, bf16[128,1024]{1,0:T(8,128)(2,1)S(1)}, u32[]{:S(2)}, u32[]{:S(2)}) collective-permute-start(bf16[128,1024]{1,0:T(8,128)(2,1)S(1)} %get-tuple-element.152), channel_id=1, source_target_pairs={{0,4},{1,5},{2,6},{3,7},{4,0},{5,1},{6,2},{7,3},{8,12},{9,13},{10,... | collective-permute-start | bytes 786440 | tf_op jit(solution)/shard_map/ppermute | solution.py:96
  108.8 17.3 %collective-permute-start.27 = (bf16[128,1024]{1,0:T(8,128)(2,1)S(1)}, bf16[128,1024]{1,0:T(8,128)(2,1)S(1)}, u32[]{:S(2)}, u32[]{:S(2)}) collective-permute-start(bf16[128,1024]{1,0:T(8,128)(2,1)S(1)} %get-tuple-element.129), channel_id=1, source_target_pairs={{0,8},{1,9},{2,10},{3,11},{4,12},{5,13},{6,14},{7,15},{8,0},{9,1},... | collective-permute-start | bytes 786440 | tf_op jit(solution)/shard_map/ppermute | solution.py:93
  115.0 27.0 %collective-permute-start.28 = (bf16[128,1024]{1,0:T(8,128)(2,1)S(1)}, bf16[128,1024]{1,0:T(8,128)(2,1)S(1)}, u32[]{:S(2)}, u32[]{:S(2)}) collective-permute-start(bf16[128,1024]{1,0:T(8,128)(2,1)S(1)} %get-tuple-element.130), channel_id=1, source_target_pairs={{0,16},{1,17},{2,18},{3,19},{4,20},{5,21},{6,22},{7,23},{8,24},{9,... | collective-permute-start | bytes 786440 | tf_op jit(solution)/shard_map/ppermute | solution.py:93
  117.1 26.8 %collective-permute-start.29 = (bf16[128,1024]{1,0:T(8,128)(2,1)S(1)}, bf16[128,1024]{1,0:T(8,128)(2,1)S(1)}, u32[]{:S(2)}, u32[]{:S(2)}) collective-permute-start(bf16[128,1024]{1,0:T(8,128)(2,1)S(1)} %get-tuple-element.131), channel_id=1, source_target_pairs={{0,24},{1,25},{2,26},{3,27},{4,28},{5,29},{6,30},{7,31},{8,16},{9,... | collective-permute-start | bytes 786440 | tf_op jit(solution)/shard_map/ppermute | solution.py:93
  119.6 34.2 %collective-permute-start.23 = (bf16[128,1024]{1,0:T(8,128)(2,1)S(1)}, bf16[128,1024]{1,0:T(8,128)(2,1)S(1)}, u32[]{:S(2)}, u32[]{:S(2)}) collective-permute-start(bf16[128,1024]{1,0:T(8,128)(2,1)S(1)} %shard_map.275), channel_id=1, source_target_pairs={{0,16},{1,17},{2,18},{3,19},{4,20},{5,21},{6,22},{7,23},{8,24},{9,... | collective-permute-start | bytes 786440 | tf_op jit(solution)/shard_map/ppermute | solution.py:93
  122.7 31.9 %collective-permute-start.35 = (bf16[40,1024]{1,0:T(8,128)(2,1)S(1)}, bf16[40,1024]{1,0:T(8,128)(2,1)S(1)}, u32[]{:S(2)}, u32[]{:S(2)}) collective-permute-start(bf16[40,1024]{1,0:T(8,128)(2,1)S(1)} %get-tuple-element.141), channel_id=1, source_target_pairs={{0,8},{1,9},{2,10},{3,11},{4,12},{5,13},{6,14},{7,15},{8,0},{9,1},... | collective-permute-start | bytes 245768 | tf_op jit(solution)/shard_map/ppermute | solution.py:93
  126.2 34.2 %collective-permute-start.36 = (bf16[40,1024]{1,0:T(8,128)(2,1)}, bf16[40,1024]{1,0:T(8,128)(2,1)}, u32[]{:S(2)}, u32[]{:S(2)}) collective-permute-start(bf16[40,1024]{1,0:T(8,128)(2,1)} %get-tuple-element.142), channel_id=1, source_target_pairs={{0,16},{1,17},{2,18},{3,19},{4,20},{5,21},{6,22},{7,23},{8,24},{9,... | collective-permute-start | bytes 245768 | tf_op jit(solution)/shard_map/ppermute | solution.py:93
  141.9 18.4 %collective-permute-start.37 = (bf16[40,1024]{1,0:T(8,128)(2,1)}, bf16[40,1024]{1,0:T(8,128)(2,1)}, u32[]{:S(2)}, u32[]{:S(2)}) collective-permute-start(bf16[40,1024]{1,0:T(8,128)(2,1)} %get-tuple-element.143), channel_id=1, source_target_pairs={{0,24},{1,25},{2,26},{3,27},{4,28},{5,29},{6,30},{7,31},{8,16},{9,... | collective-permute-start | bytes 245768 | tf_op jit(solution)/shard_map/ppermute | solution.py:93
  144.6 15.8 %collective-permute-start.43 = (bf16[32,768]{1,0:T(8,128)(2,1)}, bf16[32,768]{1,0:T(8,128)(2,1)}, u32[]{:S(2)}, u32[]{:S(2)}) collective-permute-start(bf16[32,768]{1,0:T(8,128)(2,1)} %get-tuple-element.154), channel_id=1, source_target_pairs={{0,8},{1,9},{2,10},{3,11},{4,12},{5,13},{6,14},{7,15},{8,0},{9,1},... | collective-permute-start | bytes 147464 | tf_op jit(solution)/shard_map/ppermute | solution.py:93
  (48 other events, 613.1 us)

commit v4 on v3

v4 whole, which is shorter than its diff:
```python
import math

import jax
import jax.numpy as jnp
from jax import lax
from jax.experimental import pallas as pl
from jax.experimental.pallas import tpu as pltpu
from jax.sharding import PartitionSpec as P


D = 1024
HEAD = 64
ROT = 16
NB = 4
QB = D // NB
NEG = -1e30
SHARE = 1.0
TWO_STEPS = True
HALVES = False

F32 = jnp.float32
BF = jnp.bfloat16
I32 = jnp.int32


def dot_nn(left, right):
    return jnp.dot(left, right, preferred_element_type=F32)


def dot_nt(left, right):
    return lax.dot_general(left, right, (((1,), (1,)), ((), ())), preferred_element_type=F32)


def iota(shape, axis):
    return lax.broadcasted_iota(I32, shape, axis)


def call(body, ins, outs, scratch=(), flops=0, extra=4 << 20, hbm=(), alias=None):
    spaces = {"v": pltpu.VMEM, "s": pltpu.SMEM, "a": pl.ANY, "h": pltpu.HBM}
    arrays = [a for _, a in ins]
    nbytes = sum(a.size * a.dtype.itemsize for a in arrays) + sum(math.prod(o.shape) * o.dtype.itemsize for o in outs)
    room = sum(math.prod(t.shape) * jnp.dtype(t.dtype).itemsize for t in scratch if getattr(t, "memory_space", None) == pltpu.VMEM)
    room += SHARE * (sum(a.size * a.dtype.itemsize for s, a in ins if s == "v") + sum(math.prod(o.shape) * o.dtype.itemsize for i, o in enumerate(outs) if i not in hbm))
    return pl.pallas_call(
        body,
        out_shape=tuple(outs),
        in_specs=[pl.BlockSpec(memory_space=spaces[s]) for s, _ in ins],
        out_specs=tuple(pl.BlockSpec(memory_space=pltpu.HBM if i in hbm else pltpu.VMEM) for i in range(len(outs))),
        scratch_shapes=list(scratch),
        input_output_aliases=alias or {},
        compiler_params=pltpu.CompilerParams(vmem_limit_bytes=int(room * 1.02) + extra),
        cost_estimate=pl.CostEstimate(flops=int(flops), bytes_accessed=int(nbytes), transcendentals=0),
    )(*arrays)


def sds(shape, dtype):
    return jax.ShapeDtypeStruct(shape, dtype)


def by_rows(count, chunk, fn):
    def step(i, carry):
        fn(pl.ds(pl.multiple_of(i * chunk, chunk), chunk))
        return carry

    lax.fori_loop(0, count // chunk, step, 0, unroll=True)


def lanes(i, width):
    return pl.ds(pl.multiple_of(i * width, width), width)


def partner(v):
    low = iota(v.shape, 1) % HEAD < ROT // 2
    return jnp.where(low, pltpu.roll(v, v.shape[1] - ROT // 2, 1), pltpu.roll(v, ROT // 2, 1))


def split_heads(v):
    first = iota(v.shape, 1) < HEAD
    zero = jnp.zeros_like(v)
    return jnp.concatenate([jnp.where(first, v, zero), jnp.where(first, zero, v)], axis=0)


def stats(x):
    centre = jnp.mean(x, axis=-1, keepdims=True)
    centered = x - centre
    spread = jnp.mean(centered * centered, axis=-1, keepdims=True)
    return centered, lax.rsqrt(spread + 1e-05)


def make(n):
    R = n // NB
    assert R * NB == n and R & (R - 1) == 0

    def across(v, mask):
        return lax.ppermute(v, "dp", [(d, d ^ (mask * R)) for d in range(n)])

    def swap(v, mask):
        return lax.ppermute(v, "dp", [(d, d ^ mask) for d in range(n)])

    def gather_r(own, tag):
        half = own.shape[0] // 2
        got = [(0, 0, own)]
        if R == 8 and tag == "one":
            from_x, from_y = swap(own, 2), swap(own, 4)
            got += [(2, 0, from_x), (4, 0, from_y)]


            def cut_body(x, y, low, high):
                low[...] = y[:half]
                high[...] = x[half:]

            part = sds((half, *own.shape[1:]), BF)
            low, high = call(cut_body, [("v", from_x), ("v", from_y)], [part, part])
            got.append((6, 0, swap(low, 2)))
            got.append((6, half, swap(high, 4)))
        else:
            for m in range(2, R, 2):
                got.append((m, 0, swap(own, m)))
        return got + [(m + 1, at, swap(v, 1)) for m, at, v in got]

    def on_device(
        block_in, grad_out, w_qkv, b_qkv, w_o, b_o, w_in, b_in, w_out, b_out,
        ln1_gain, ln1_shift, ln2_gain, ln2_shift, seq_lens, seq_device, seq_offset,
    ):
        T = block_in.shape[0]
        NT = NB * T
        rows = w_qkv.shape[0]
        ff_dev = w_out.shape[0]
        FB = w_in.shape[1] // NB
        W1 = 3 * QB + FB
        J = R // 2
        MA = NB * rows
        MS = MA + 8
        idx = lax.axis_index("dp").astype(I32)
        b, r = idx // R, idx % R
        br = jnp.stack([b, r])

        count = seq_lens.shape[0]
        half = ROT // 2

        def table_body(br, lens, device, offset, cos, sin, mask, live):
            slot = iota((T, count), 0)
            lane = iota((T, 2 * HEAD), 1) % HEAD
            freqs = jnp.exp((lane % half).astype(F32) * (-math.log(10000.0) / half))
            freqs = jnp.where(lane < ROT, freqs, 0.0)
            causal = iota((T, T), 1) <= iota((T, T), 0)
            for k in range(NB):
                owner = (br[0] ^ k) * R + br[1]
                inside = (device[...] == owner) & (slot >= offset[...]) & (slot < offset[...] + lens[...])
                ones = jnp.where(inside, 1.0, 0.0)
                present = jnp.max(ones, axis=1, keepdims=True)
                number = jnp.sum(ones * iota((T, count), 1).astype(F32), axis=1, keepdims=True)
                position = jnp.sum(ones * (slot - offset[...]).astype(F32), axis=1, keepdims=True)
                own = (count + iota((T, 1), 0)).astype(F32)
                segment = jnp.broadcast_to(jnp.where(present > 0.0, number, own), (T, T))
                mask[k] = jnp.where((segment == segment.T) & causal, 0.0, NEG)
                rws = slice(k * T, (k + 1) * T)
                live[rws] = present
                angle = position * freqs
                cos[rws] = jnp.cos(angle)
                sin[rws] = jnp.sin(angle) * jnp.where(lane < half, -1.0, 1.0)

        table = sds((NT, 2 * HEAD), F32)
        cosine, sines, mask, live = call(
            table_body, [("s", br)] + [("v", v.reshape(1, -1)) for v in (seq_lens, seq_device, seq_offset)],
            [table, table, sds((NB, T, T), F32), sds((NT, 1), F32)],
        )

        small = [b_in, b_qkv, b_o, b_out, ln1_gain, ln1_shift, ln2_gain, ln2_shift]
        widths = [v.shape[0] for v in small]
        offsets = [sum(widths[:i]) for i in range(len(small))]
        SR = -(-sum(widths) // 128)
        W1X = W1 + 128

        def pack_body(qkv_ref, in_ref, o_ref, out_ref, *rest):
            vectors, outs = rest[: len(small)], rest[len(small) :]
            for k in range(NB):
                to = lax.div(lax.axis_index("dp").astype(I32), R) ^ k
                for s in range(3):
                    outs[k][:, s * QB : (s + 1) * QB] = qkv_ref[:, lanes(s * NB + to, QB)]
                outs[k][:, 3 * QB : W1] = in_ref[:, lanes(to, FB)]
            outs[NB][:ff_dev] = out_ref[...]
            outs[NB][ff_dev:] = o_ref[...]
            parts = [v[...].astype(F32) for v in vectors]
            if SR * 128 > sum(widths):
                parts.append(jnp.zeros((1, SR * 128 - sum(widths)), F32))
            every = jnp.concatenate(parts, axis=1)
            lines = [every[:, i * 128 : (i + 1) * 128] for i in range(SR)]
            if rows > SR:
                lines.append(jnp.zeros((rows - SR, 128), F32))
            lines = jnp.concatenate(lines, axis=0).astype(BF)
            for k in range(NB):
                outs[k][:, W1:] = lines

        packed = call(
            pack_body,
            [("v", w_qkv), ("v", w_in), ("v", w_o), ("v", w_out)] + [("v", v.reshape(1, -1)) for v in small],
            [sds((rows, W1X), BF)] * NB + [sds((ff_dev + rows, D), BF)], extra=56 << 20,
        )
        columns, own_two = packed[:NB], packed[NB]

        def blocks_of(own, after):
            two = across(after, 2)
            return [own, across(after, 1), two, across(two, 1)]

        two = gather_r(own_two, "two")
        crossed = [across(columns[k], k) for k in range(1, NB)]
        after, _ = lax.optimization_barrier((block_in, crossed))

        def join_body(*refs):
            for k in range(NB):
                refs[NB][k] = refs[k][...]

        (mine,) = call(join_body, [("v", a) for a in (columns[0], *crossed)], [sds((NB, rows, W1X), BF)])
        one = gather_r(mine, "one")
        tokens = blocks_of(block_in, after)
        after, _ = lax.optimization_barrier((grad_out, tokens[1]))
        grads_in = [grad_out] + [across(after, k) for k in range(1, NB)]

        def pick(width_mod, off, base, width):
            return (iota((width, width_mod.shape[1]), 0) + base == off + width_mod).astype(BF)

        def window(off, width):
            base = off // 128 * 128
            return base, -(-(off + width) // 128) * 128 - base

        def decode(br, got, bq, bi, g1, s1, g2, s2, bo):
            def expand(which, col):
                width, off = widths[which], offsets[which]
                base, span = window(off, width)
                total = col.shape[1]
                sel = pick(lax.rem(col, width), off, base, span)
                every = dot_nn(jnp.concatenate([got[:, i] for i in range(base // 128, (base + span) // 128)], axis=1), sel)
                return jnp.sum(jnp.where(iota((n, total), 0) == lax.div(col, width), every, 0.0), axis=0, keepdims=True)

            at = iota((1, 3 * QB), 1)
            bq[...] = expand(1, lax.div(at, QB) * D + br[0] * QB + lax.rem(at, QB))
            bi[...] = expand(0, iota((1, FB), 1) + br[0] * FB)
            whole = iota((1, D), 1)
            bo[...] = expand(2, whole) + expand(3, whole)
            for ref, which in ((g1, 4), (s1, 5), (g2, 6), (s2, 7)):
                ref[...] = expand(which, whole)

        def load_small(br, parts, got, sems):
            copies = []
            for (m, start, _), ref in zip(one, parts):
                for k in range(ref.shape[0]):
                    at = (br[0] ^ (start + k)) * R + (br[1] ^ m)
                    source = ref.at[k, pl.ds(0, 8), pl.ds(W1, 128)]
                    copies.append(pltpu.make_async_copy(source, got.at[at], sems.at[len(copies)]))
            return copies

        def load_one(br, parts, w1, sems, low, high):
            cols = pl.ds(low, high - low)
            copies = []
            for (m, start, _), ref in zip(one, parts):
                for k in range(ref.shape[0]):
                    to = w1.at[br[0] ^ (start + k), br[1] ^ m, :, cols]
                    copies.append(pltpu.make_async_copy(ref.at[k, :, cols], to, sems.at[int(low > 0), len(copies)]))
            return copies

        def load_two(br, parts, wout, wo, sems):
            copies = []
            for (m, start, _), ref in zip(two, parts):
                size = ref.shape[0]
                for to, first, last in ((wout, 0, ff_dev), (wo, ff_dev, ff_dev + rows)):
                    low, high = max(start, first), min(start + size, last)
                    if low < high:
                        copies.append(
                            pltpu.make_async_copy(
                                ref.at[pl.ds(low - start, high - low)],
                                to.at[br[1] ^ m, pl.ds(low - first, high - low)],
                                sems.at[len(copies)],
                            )
                        )
            return copies

        dma = pltpu.SemaphoreType.DMA
        PAIRS = QB // 128

        def fwd_body(br, h0, h1, h2, h3, cos, sin, mask_ref, *rest):
            one_refs, two_refs, rest = rest[: len(one)], rest[len(one) : len(one) + len(two)], rest[len(one) + len(two) :]
            act1, act2, q, k, v, probs, mixed, hidden, dgelu, xhat_ref, w1, wo, wout, own, later, away = rest[:16]
            g1, g2, bo = rest[16:19]
            stage, x_ref, semx, sem1, sem2, semp, bq, bi, s1, s2, got, semg = rest[19:]
            cx = [pltpu.make_async_copy(h, x_ref.at[i], semx.at[i]) for i, h in enumerate((h0, h1, h2, h3))]
            c1, c1f = load_one(br, one_refs, w1, sem1, 0, 3 * QB), load_one(br, one_refs, w1, sem1, 3 * QB, W1)
            c2, cg = load_two(br, two_refs, wout, wo, sem2), load_small(br, one_refs, got, semg)
            for c in cx + cg + c1 + c1f + c2:
                c.start()
            for i in range(NB):
                cx[i].wait()
                centered, rstd = stats(x_ref[i].astype(F32))
                xhat_ref[i * T : (i + 1) * T] = centered * rstd
            for c in cg:
                c.wait()
            decode(br, got, bq, bi, g1, s1, g2, s2, bo)
            for i in range(NB):
                rws = slice(i * T, (i + 1) * T)
                act1[rws] = (xhat_ref[rws] * g1[...] + s1[...]).astype(BF)
                act2[rws] = (xhat_ref[rws] * g2[...] + s2[...]).astype(BF)
            for c in c1:
                c.wait()
            for s, ref in enumerate((q, k, v)):
                wt = w1[:, :, :, s * QB : (s + 1) * QB].reshape(D, QB)

                def project(rws, s=s, ref=ref, wt=wt):
                    y = dot_nn(act1[rws], wt) + bq[:, s * QB : (s + 1) * QB]
                    for p in range(PAIRS):
                        z = y[:, p * 128 : (p + 1) * 128]
                        if s < 2:
                            z = z * cos[rws] + partner(z) * sin[rws]
                        ref[rws, p * 128 : (p + 1) * 128] = z.astype(BF)

                by_rows(NT, 256, project)

            def attend(i, carry):
                rws = pl.ds(pl.multiple_of(i * T, T), T)
                m2 = mask_ref[i]
                m2 = jnp.concatenate([m2, m2], axis=0)
                for p in range(PAIRS):
                    cols = slice(p * 128, (p + 1) * 128)
                    s = dot_nt(split_heads(q[rws, cols]), k[rws, cols]) * (1.0 / math.sqrt(HEAD)) + m2
                    e = jnp.exp(s - jnp.max(s, axis=-1, keepdims=True))
                    pr = e / jnp.sum(e, axis=-1, keepdims=True)
                    probs[i * PAIRS + p] = pr
                    pb = pr.astype(BF)
                    pb = jnp.concatenate([pb[:T], pb[T:]], axis=1)
                    mixed[rws, cols] = dot_nn(pb, split_heads(v[rws, cols])).astype(BF)
                return carry

            lax.fori_loop(0, NB, attend, 0, unroll=True)
            for c in c1f:
                c.wait()

            def feed(t, carry):
                cols = lanes(t, 256)
                wt = w1[:, :, :, pl.ds(pl.multiple_of(3 * QB + t * 256, 256), 256)].reshape(D, 256)

                def act(rws):
                    h = dot_nn(act2[rws], wt) + bi[:, cols]
                    cdf = 0.5 * (1.0 + lax.erf(h * (1.0 / math.sqrt(2.0))))
                    hidden[rws, cols] = (h * cdf).astype(BF)
                    dgelu[rws, cols] = cdf + h * (jnp.exp(-0.5 * h * h) * (1.0 / math.sqrt(2.0 * math.pi)))

                by_rows(NT, 256, act)
                return carry

            lax.fori_loop(0, FB // 256, feed, 0, unroll=True)
            for c in c2:
                c.wait()

            def project_out(t, carry):
                cols = lanes(t, 256)
                y = dot_nn(mixed[...], wo[:, :, cols].reshape(QB, 256))
                y = y + dot_nn(hidden[...], wout[:, :, cols].reshape(FB, 256))
                own[:, cols] = y[:T]
                later[:, cols] = y[2 * T : 3 * T]
                stage[:T, cols] = y[T : 2 * T].astype(BF)
                stage[T:, cols] = y[3 * T :].astype(BF)
                return carry

            lax.fori_loop(0, D // 256, project_out, 0, unroll=True)
            send = pltpu.make_async_copy(stage, away, semp)
            send.start()
            send.wait()

        tab = sds((NT, D), BF)
        third = sds((NT, QB), BF)
        block = sds((T, D), BF)
        act1, act2, q, k, v, probs, mixed, hidden, dgelu, xhat, full_one, full_o, full_out, own_part, later_part, away_part, gain_one, gain_two, bias_o = call(
            fwd_body,
            [("s", br)] + [("h", x) for x in tokens]
            + [("v", a) for a in (cosine, sines, mask)]
            + [("h", a) for _, _, a in one + two],
            [tab, tab, third, third, third, sds((NB * PAIRS, 2 * T, T), F32), third, sds((NT, FB), BF), sds((NT, FB), F32),
             sds((NT, D), F32), sds((NB, R, rows, W1), BF), sds((R, rows, D), BF), sds((R, ff_dev, D), BF),
             sds((T, D), F32), sds((T, D), F32), sds((2 * T, D), BF)] + [sds((1, D), F32)] * 3,
            [pltpu.VMEM((2 * T, D), BF), pltpu.VMEM((NB, T, D), BF), dma((NB,)), dma((2, R * NB)), dma((3 * R,)), dma,
             pltpu.VMEM((1, 3 * QB), F32), pltpu.VMEM((1, FB), F32), pltpu.VMEM((1, D), F32), pltpu.VMEM((1, D), F32),
             pltpu.VMEM((n, 8, 128), BF), dma((R * NB,))],
            hbm=(15,),
            flops=2 * NT * D * W1 + 2 * NT * D * (QB + FB) + 8 * NT * T * QB,
        )

        got_one = across(away_part, 1)

        def pass_body(keep, got, out):
            def fn(rws):
                out[rws] = (keep[rws] + got[pl.ds(T, T)].astype(F32)).astype(BF)

            by_rows(T, T, fn)


        def bwd_core_body(br, live_ref, g0, g1, g2, g3, act1, act2, q, k, v, probs, cos, sin, dgelu, wo, wout, *rest):
            grad, dqkv, dhid, keep, send, sum_qkv, sum_in, dmix, term, flip = rest
            for i, g in enumerate((g0, g1, g2, g3)):
                rws = pl.ds(i * T, T)
                grad[rws] = (g[...].astype(F32) * live_ref[rws]).astype(BF)
            dmix[...] = dot_nt(grad[...], wo[...].reshape(QB, D)).astype(BF)

            def attend(i, carry):
                rws = pl.ds(pl.multiple_of(i * T, T), T)
                for p in range(PAIRS):
                    cols = slice(p * 128, (p + 1) * 128)
                    pr = probs[i * PAIRS + p]
                    pb = pr.astype(BF)
                    dm2 = split_heads(dmix[rws, cols])
                    dp = dot_nt(dm2, v[rws, cols])
                    ds = (pr * (dp - jnp.sum(dp * pr, axis=-1, keepdims=True))).astype(BF)
                    dq = dot_nn(jnp.concatenate([ds[:T], ds[T:]], axis=1), split_heads(k[rws, cols]))
                    dk = dot_nn(ds.T, split_heads(q[rws, cols]))
                    dv = dot_nn(pb.T, dm2)
                    for s, z in enumerate((dq, dk)):
                        z = z * (1.0 / math.sqrt(HEAD))
                        z = z * cos[rws] - partner(z) * sin[rws]
                        dqkv[rws, s * QB + p * 128 : s * QB + (p + 1) * 128] = z.astype(BF)
                    dqkv[rws, 2 * QB + p * 128 : 2 * QB + (p + 1) * 128] = dv.astype(BF)
                return carry

            lax.fori_loop(0, NB, attend, 0, unroll=True)
            sum_qkv[...] = jnp.sum(dqkv[...].astype(F32), axis=0, keepdims=True)

            def d_hidden(t, carry):
                cols = lanes(t, 256)
                per = 256 // ff_dev
                wt = wout[pl.ds(t * per, per)].reshape(256, D)
                y = (dot_nt(grad[...], wt) * dgelu[:, cols]).astype(BF)
                dhid[:, cols] = y
                sum_in[:, cols] = jnp.sum(y.astype(F32), axis=0, keepdims=True)
                return carry

            lax.fori_loop(0, FB // 256, d_hidden, 0, unroll=True)

            def terms(t, carry):
                cols = lanes(t, 256)
                flip[0] = act1[:, cols].T
                flip[1] = act2[:, cols].T
                term[:, :, : 3 * QB] = dot_nn(flip[0], dqkv[...]).reshape(R, rows, 3 * QB)
                term[:, :, 3 * QB :] = dot_nn(flip[1], dhid[...]).reshape(R, rows, FB)
                at = pl.ds(pl.multiple_of(t * rows, rows), rows)
                for j in range(J):
                    keep[j, at] = term[br[1] ^ (2 * j)]
                    send[j, at] = term[br[1] ^ (2 * j + 1)].astype(BF)
                return carry

            lax.fori_loop(0, NB, terms, 0, unroll=True)

        grad_r, dqkv, dhid, keep_1, send_1, sum_qkv, sum_in = call(
            bwd_core_body,
            [("s", br), ("v", live)] + [("v", g) for g in grads_in]
            + [("v", a) for a in (act1, act2, q, k, v, probs, cosine, sines, dgelu, full_o, full_out)],
            [tab, sds((NT, 3 * QB), BF), sds((NT, FB), BF), sds((J, MA, W1), F32), sds((J, MA, W1), BF),
             sds((1, 3 * QB), F32), sds((1, FB), F32)],
            [pltpu.VMEM((NT, QB), BF), pltpu.VMEM((R, rows, W1), F32), pltpu.VMEM((2, 256, NT), BF)],
            flops=2 * NT * D * (W1 + QB + FB) + 16 * NT * T * QB,
        )

        def merge(keep, send, small=()):
            size, width = keep.shape[1:]

            def body(keep, got, *rest):
                keep_small, got_small = rest[: len(small)] or (None, None)
                outs = rest[len(small) :]
                for j in range(J):
                    y = keep[j] + got[j].astype(F32)
                    outs[j][:size] = y.astype(outs[j].dtype)
                    if small:
                        z = keep_small[j] + got_small[j].astype(F32)
                        outs[j][size:, :WO] = z.astype(outs[j].dtype)

            full = size + (8 if small else 0)
            outs = call(
                body, [("v", a) for a in (keep, swap(send, 1), *small)],
                [sds((full, width), F32)] + [sds((full, width), BF)] * (J - 1),
            )
            return [outs[0]] + [swap(outs[j], 2 * j) for j in range(1, J)]

        (pass_part,) = call(pass_body, [("v", later_part), ("v", got_one)], [block])
        got_two = across(pass_part, 2)

        out_widths = [FB * NB // n, 3 * D // n] + [D // n] * 5
        out_offsets = [sum(out_widths[:i]) for i in range(len(out_widths))]
        WO = -(-sum(out_widths) // 128) * 128

        def bwd3_body(br, xhat, w1, dqkv, dhid, grad, sum_in, sum_qkv, g1, g2, *rest):
            own, keep, send, *rest = rest
            parts = 1 if TWO_STEPS else 3
            aways, rest = rest[:parts], rest[parts:]
            later, rest = (rest[:1], rest[1:]) if TWO_STEPS else ((), rest)
            stages, (gs, sums, tot, semp) = rest[:parts], rest[parts:]
            gs[...] = jnp.sum(grad[:T].astype(F32), axis=0, keepdims=True)

            def back(t, carry):
                cols = lanes(t, QB)
                d1 = dot_nt(dqkv[...], w1[t, :, :, : 3 * QB].reshape(QB, 3 * QB))
                d2 = dot_nt(dhid[...], w1[t, :, :, 3 * QB :].reshape(QB, FB))
                xh = xhat[:, cols]
                y = d1 * g1[:, cols] + d2 * g2[:, cols]
                own[:, cols] = y[:T]
                for k in range(1, NB):
                    if not TWO_STEPS:
                        stages[k - 1][:, cols] = y[k * T : (k + 1) * T].astype(BF)
                    elif k == 2:
                        later[0][:, cols] = y[k * T : (k + 1) * T]
                    else:
                        stages[0][(k // 2) * T : (k // 2 + 1) * T, cols] = y[k * T : (k + 1) * T].astype(BF)
                for i, z in enumerate((d1 * xh, d1, d2 * xh, d2)):
                    sums[i : i + 1, cols] = jnp.sum(z, axis=0, keepdims=True)
                return carry

            lax.fori_loop(0, D // QB, back, 0, unroll=True)
            sending = [pltpu.make_async_copy(a, z, semp.at[i]) for i, (a, z) in enumerate(zip(stages, aways))]
            for c in sending:
                c.start()

            total = jnp.zeros((n, WO), F32)

            def place(total, vec, col, which):
                size = vec.shape[1]
                width, off = out_widths[which], out_offsets[which]
                mine = jnp.where(iota((n, size), 0) == lax.div(col, width), vec, 0.0)
                base = off // 128 * 128
                span = -(-(off + width) // 128) * 128 - base
                sel = pick(lax.rem(col, width), off, base, span)
                high = mine.astype(BF)
                low = (mine - high.astype(F32)).astype(BF)
                placed = dot_nt(high, sel) + dot_nt(low, sel)
                parts = []
                if base:
                    parts.append(jnp.zeros((n, base), F32))
                parts.append(placed)
                if base + span < WO:
                    parts.append(jnp.zeros((n, WO - base - span), F32))
                return total + (jnp.concatenate(parts, axis=1) if len(parts) > 1 else placed)

            whole = iota((1, D), 1)
            at = iota((1, 3 * QB), 1)
            total = place(total, sum_in[...], iota((1, FB), 1) + br[0] * FB, 0)
            total = place(total, sum_qkv[...], lax.div(at, QB) * D + br[0] * QB + lax.rem(at, QB), 1)
            total = place(total, gs[...], whole, 2)
            for i in range(4):
                total = place(total, sums[i : i + 1], whole, 3 + i)
            tot[...] = total
            for j in range(J):
                for ref, m in ((keep, 2 * j), (send, 2 * j + 1)):
                    lines = [tot[pl.ds(to * R + (br[1] ^ m), 1), :] for to in range(NB)]
                    lines.append(jnp.zeros((8 - NB, WO), F32))
                    ref[j] = jnp.concatenate(lines, axis=0).astype(ref.dtype)
            for c in sending:
                c.wait()

        pair = sds((2 * T, D), BF)
        own_g, keep_s, send_s, *away_g = call(
            bwd3_body,
            [("s", br)] + [("v", a) for a in (xhat, full_one, dqkv, dhid, grad_r, sum_in, sum_qkv, gain_one, gain_two)],
            [sds((T, D), F32), sds((J, 8, WO), F32), sds((J, 8, WO), BF)]
            + ([pair, sds((T, D), F32)] if TWO_STEPS else [block] * 3),
            [pltpu.VMEM((2 * T, D) if TWO_STEPS else (T, D), BF)] * (1 if TWO_STEPS else 3)
            + [pltpu.VMEM((1, D), F32), pltpu.VMEM((8, D), F32), pltpu.VMEM((n, WO), F32), dma((3,))],
            hbm=(3,) if TWO_STEPS else (3, 4, 5), flops=2 * NT * D * W1,
        )
        if TWO_STEPS:
            back_one = across(away_g[0], 1)
            (pass_g,) = call(pass_body, [("v", away_g[1]), ("v", back_one)], [block])
            backs = [back_one, across(pass_g, 2)]
        else:
            backs = [across(g, k + 1) for k, g in enumerate(away_g)]
        HALF = MA // 2
        if R == 8 and HALVES:

            def halves_body(keep, got, keep_small, got_small, own, to_x, to_y, keep_x, keep_y):
                def total(j, low, high):
                    return keep[j, low:high] + got[j, low:high].astype(F32)

                def small(j):
                    return keep_small[j] + got_small[j].astype(F32)

                own[:MA] = total(0, 0, MA)
                own[MA:, :WO] = small(0)
                to_x[:HALF] = total(1, 0, HALF).astype(BF)
                to_x[HALF:] = total(3, 0, HALF).astype(BF)
                for at, j in ((0, 2), (MS - HALF, 3)):
                    to_y[at : at + MA - HALF] = total(j, HALF, MA).astype(BF)
                    to_y[at + MA - HALF : at + MS - HALF, :WO] = small(j).astype(BF)
                keep_x[: MA - HALF] = total(1, HALF, MA)
                keep_x[MA - HALF :, :WO] = small(1)
                keep_y[...] = total(2, 0, HALF)

            own_1, to_x, to_y, keep_x, keep_y = call(
                halves_body,
                [("v", a) for a in (keep_1, swap(send_1, 1), keep_s, swap(send_s, 1))],
                [sds((MS, W1), F32), sds((2 * HALF, W1), BF), sds((2 * (MS - HALF), W1), BF), sds((MS - HALF, W1), F32),
                 sds((HALF, W1), F32)],
            )
            got_x, got_y = swap(to_x, 2), swap(to_y, 4)

            def second_body(keep_x, keep_y, got_x, got_y, to_x, to_y):
                to_x[...] = (keep_x[...] + got_y[MS - HALF :].astype(F32)).astype(BF)
                to_y[...] = (keep_y[...] + got_x[HALF:].astype(F32)).astype(BF)

            to_x, to_y = call(
                second_body, [("v", a) for a in (keep_x, keep_y, got_x, got_y)],
                [sds((MS - HALF, W1), BF), sds((HALF, W1), BF)],
            )
            merged_1 = [own_1, got_x, got_y, swap(to_x, 2), swap(to_y, 4)]
            lower, upper = ((0, 0), (1, 0), (4, 0)), ((0, 0), (2, -HALF), (3, -HALF))
        else:
            merged_1 = merge(keep_1, send_1, (keep_s, swap(send_s, 1)))
            lower = upper = [(j, 0) for j in range(J)]

        def terms_body(br, grad, hidden, mixed, keep, send, term, term_o, flip):
            def term_out(t, carry):
                flip[...] = hidden[:, lanes(t, 256)].T
                per = 256 // ff_dev
                term[pl.ds(t * per, per)] = dot_nn(flip[...], grad[...]).reshape(per, ff_dev, D)
                return carry

            lax.fori_loop(0, FB // 256, term_out, 0, unroll=True)
            flip[...] = mixed[...].T
            term_o[...] = dot_nn(flip[...], grad[...]).reshape(R, rows, D)
            for j in range(J):
                for ref, m in ((keep, 2 * j), (send, 2 * j + 1)):
                    ref[j, :ff_dev] = term[br[1] ^ m].astype(ref.dtype)
                    ref[j, ff_dev:] = term_o[br[1] ^ m].astype(ref.dtype)

        keep_2, send_2 = call(
            terms_body, [("s", br)] + [("v", a) for a in (grad_r, hidden, mixed)],
            [sds((J, ff_dev + rows, D), F32), sds((J, ff_dev + rows, D), BF)],
            [pltpu.VMEM((R, ff_dev, D), F32), pltpu.VMEM((R, rows, D), F32), pltpu.VMEM((256, NT), BF)],
            flops=2 * NT * D * (FB + QB),
        )
        merged_2 = merge(keep_2, send_2)

        def total_body(x, live_ref, bo, own, p1, p2, out):
            y = x[...].astype(F32) + bo[...] + own[...] + p1[:T].astype(F32) + p2[...].astype(F32)
            out[...] = (y * live_ref[:T]).astype(BF)

        (block_out,) = call(
            total_body,
            [("v", a) for a in (block_in, live, bias_o, own_part, got_one, got_two)], [block],
        )

        def plane_1_body(br, *rest):
            got, (*outs, tot) = rest[: len(merged_1)], rest[len(merged_1) :]

            def total_of(part, low, high, width):
                y = 0.0
                for which, first in part:
                    y = y + got[which][low + first : high + first, :width].astype(F32)
                return y

            tot[:HALF] = total_of(lower, 0, HALF, W1)
            tot[HALF:] = total_of(upper, HALF, MA, W1)
            lines = total_of(upper, MA, MS, WO)
            for k, ref in enumerate(outs):
                ref[:rows] = tot[pl.ds(pl.multiple_of((br[0] ^ k) * rows, rows), rows)].astype(ref.dtype)
                y = jnp.sum(jnp.where(iota(lines.shape, 0) == (br[0] ^ k), lines, 0.0), axis=0, keepdims=True)
                ref[rows:, :WO] = jnp.broadcast_to(y, (8, WO)).astype(ref.dtype)

        z0, *zs = call(
            plane_1_body, [("s", br)] + [("v", a) for a in merged_1],
            [sds((rows + 8, W1), F32)] + [sds((rows + 8, W1), BF)] * 3, [pltpu.VMEM((MA, W1), F32)],
        )
        zs = [z0] + [across(z, k + 1) for k, z in enumerate(zs)]

        def plane_2_body(*rest):
            got, (w_out_ref, w_o_ref) = rest[:J], rest[J:]
            for ref, at in ((w_out_ref, slice(0, ff_dev)), (w_o_ref, slice(ff_dev, ff_dev + rows))):
                y = got[0][at]
                for other in got[1:]:
                    y = y + other[at].astype(F32)
                ref[...] = y

        grad_w_out, grad_w_o = call(
            plane_2_body, [("v", a) for a in merged_2], [sds((ff_dev, D), F32), sds((rows, D), F32)]
        )
        small_order = (0, 1, 2, 2, 3, 4, 5, 6)

        def input_body(x, grad, own, *rest):
            *parts, out = rest

            def fn(rws):
                centered, rstd = stats(x[rws].astype(F32))
                xh = centered * rstd
                g = own[rws]
                for ref in parts:
                    g = g + ref[: T].astype(F32)
                mean_g = jnp.mean(g, axis=-1, keepdims=True)
                mean_gx = jnp.mean(g * xh, axis=-1, keepdims=True)
                out[rws] = (grad[rws].astype(F32) + rstd * (g - mean_g - xh * mean_gx)).astype(BF)

            by_rows(T, T, fn)

        (grad_input,) = call(input_body, [("v", a) for a in (block_in, grad_r, own_g, *backs)], [block])

        def final_body(br, *rest):
            z, (w_in_ref, w_qkv_ref, *small_refs) = rest[:NB], rest[NB:]
            y = sum(ref[rows:, :WO].astype(F32) for ref in z)
            for ref, which in zip(small_refs, small_order):
                ref[...] = y[:1, out_offsets[which] : out_offsets[which] + out_widths[which]]
            for k, ref in enumerate(z):
                at = br[0] ^ k
                w_in_ref[:, lanes(at, FB)] = ref[:rows, 3 * QB :].astype(F32)
                for s in range(3):
                    w_qkv_ref[:, lanes(s * NB + at, QB)] = ref[:rows, s * QB : (s + 1) * QB].astype(F32)

        grad_w_in, grad_w_qkv, *outs = call(
            final_body, [("s", br)] + [("v", z) for z in zs],
            [sds((rows, NB * FB), F32), sds((rows, 3 * D), F32)] + [sds((1, out_widths[i]), F32) for i in small_order],
        )
        outs = [o.reshape(-1) for o in outs]

        grad_b_in, grad_b_qkv, grad_b_o, grad_b_out, grad_g1, grad_s1, grad_g2, grad_s2 = outs
        return (
            block_out, grad_input, grad_w_qkv, grad_b_qkv, grad_w_o, grad_b_o, grad_w_in, grad_b_in,
            grad_w_out, grad_b_out, grad_g1, grad_s1, grad_g2, grad_s2,
        )

    return on_device


def solution(mesh):
    two, one = P("dp", None), P("dp")
    n = mesh.shape["dp"]
    on_device = make(n)

    return jax.shard_map(
        on_device,
        mesh=mesh,
        in_specs=(two, two, two, one, two, one, two, one, two, one, one, one, one, one, P(), P(), P()),
        out_specs=(two, two, two, one, two, one, two, one, two, one, one, one, one, one),
        check_vma=False,
    )
```

time: 164 us -> 165 us (level)
  the two profiles are of different devices: /device:TPU:0 before, /device:TPU:13 now
where the time goes in v4:
time: 165 us; the launch traced here: 163 us
  waiting for transfers between devices  61.2 us (37%)
  starting transfers between devices  53.8 us (33%)
  Pallas kernels  35.8 us (22%)
  local copies, waits for them, and re-layouts  11.5 us (7%)
    ppermute x16, waiting for transfers between devices, across(): return lax.ppermute(v, 'dp', [(d, d ^ mask * R) for d in range(n)])  50.5 us
    pallas_call x17, Pallas kernels, call(): pl.pallas_call(body, out_shape=tuple(outs), in_specs=[pl.BlockSpec(memory...  35.8 us
    ppermute x25, starting transfers between devices, swap(): return lax.ppermute(v, 'dp', [(d, d ^ mask) for d in range(n)])  30.7 us
    ppermute x16, starting transfers between devices, across(): return lax.ppermute(v, 'dp', [(d, d ^ mask * R) for d in range(n)])  23.1 us
    unnamed x42, local copies, waits for them, and re-layouts  11.5 us
    ppermute x25, waiting for transfers between devices, swap(): return lax.ppermute(v, 'dp', [(d, d ^ mask) for d in range(n)])  10.6 us
  transfers between devices with their start and end apart: 41, of which 16 were waited for; matrix products, arithmetic and copies ran while one was open for 0% of the time, Pallas kernels for 15%

profile of v4, /device:TPU:13, one launch (start us, length us, event | category | flops | bytes accessed | tf_op | source)
XLA Modules:
  0.0 163.4 jit_solution(10348388329246140367)
XLA Ops:
  4.2 2.3 %collective-permute-start.1 = (bf16[32,1920]{1,0:T(8,128)(2,1)}, bf16[32,1920]{1,0:T(8,128)(2,1)S(1)}, u32[]{:S(2)}, u32[]{:S(2)}) collective-permute-start(bf16[32,1920]{1,0:T(8,128)(2,1)} %get-tuple-element.86), channel_id=1, source_target_pairs={{0,16},{1,17},{2,18},{3,19},{4,20},{5,21},{6,22},{7,23},{8,24},{9,... | collective-permute-start | bytes 368648 | tf_op jit(solution)/shard_map/ppermute | solution.py:95
  8.5 3.1 %collective-permute-done.1.refs_2_ = bf16[32,1920]{1,0:T(8,128)(2,1)S(1)} collective-permute-done((bf16[32,1920]{1,0:T(8,128)(2,1)}, bf16[32,1920]{1,0:T(8,128)(2,1)S(1)}, u32[]{:S(2)}, u32[]{:S(2)}) %collective-permute-start.1) | collective-permute-done | bytes 122912 | tf_op jit(solution)/shard_map/ppermute | solution.py:95
  11.6 6.0 %collective-permute-done.2.refs_3_ = bf16[32,1920]{1,0:T(8,128)(2,1)S(1)} collective-permute-done((bf16[32,1920]{1,0:T(8,128)(2,1)}, bf16[32,1920]{1,0:T(8,128)(2,1)S(1)}, u32[]{:S(2)}, u32[]{:S(2)}) %collective-permute-start.2) | collective-permute-done | bytes 122912 | tf_op jit(solution)/shard_map/ppermute | solution.py:95
  21.4 2.8 %collective-permute-start.4 = (bf16[128,1024]{1,0:T(8,128)(2,1)}, bf16[128,1024]{1,0:T(8,128)(2,1)S(1)}, u32[]{:S(2)}, u32[]{:S(2)}) collective-permute-start(bf16[128,1024]{1,0:T(8,128)(2,1)} %x.3), channel_id=1, source_target_pairs={{0,16},{1,17},{2,18},{3,19},{4,20},{5,21},{6,22},{7,23},{8,24},{9,... | collective-permute-start | bytes 786440 | tf_op jit(solution)/shard_map/ppermute | solution.py:95
  24.3 5.6 %collective-permute-start.10 = (bf16[4,32,1920]{2,1,0:T(8,128)(2,1)S(1)}, bf16[4,32,1920]{2,1,0:T(8,128)(2,1)S(1)}, u32[]{:S(2)}, u32[]{:S(2)}) collective-permute-start(bf16[4,32,1920]{2,1,0:T(8,128)(2,1)S(1)} %shard_map.274.rest_0_), channel_id=1, source_target_pairs={{0,1},{1,0},{2,3},{3,2},{4,5},{5,4},{6,7},{7,6},{8,9},{9,8},{10,11... | collective-permute-start | bytes 1474568 | tf_op jit(solution)/shard_map/ppermute | solution.py:98
  29.9 3.1 %collective-permute-done.4.h2 = bf16[128,1024]{1,0:T(8,128)(2,1)S(1)} collective-permute-done((bf16[128,1024]{1,0:T(8,128)(2,1)}, bf16[128,1024]{1,0:T(8,128)(2,1)S(1)}, u32[]{:S(2)}, u32[]{:S(2)}) %collective-permute-start.4) | collective-permute-done | bytes 262176 | tf_op jit(solution)/shard_map/ppermute | solution.py:95
  33.0 3.3 %collective-permute-start.3 = (bf16[128,1024]{1,0:T(8,128)(2,1)}, bf16[128,1024]{1,0:T(8,128)(2,1)S(1)}, u32[]{:S(2)}, u32[]{:S(2)}) collective-permute-start(bf16[128,1024]{1,0:T(8,128)(2,1)} %x.3), channel_id=1, source_target_pairs={{0,8},{1,9},{2,10},{3,11},{4,12},{5,13},{6,14},{7,15},{8,0},{9,1},... | collective-permute-start | bytes 786440 | tf_op jit(solution)/shard_map/ppermute | solution.py:95
  36.3 2.4 %collective-permute-start.20 = (bf16[160,1024]{1,0:T(8,128)(2,1)S(1)}, bf16[160,1024]{1,0:T(8,128)(2,1)S(1)}, u32[]{:S(2)}, u32[]{:S(2)}) collective-permute-start(bf16[160,1024]{1,0:T(8,128)(2,1)S(1)} %collective-permute-done.16.rest_12_), channel_id=1, source_target_pairs={{0,1},{1,0},{2,3},{3,2},{4,5},{5,4},{6,7},{7,6},{8,9},{9,8},{10,11... | collective-permute-start | bytes 983048 | tf_op jit(solution)/shard_map/ppermute | solution.py:98
  43.0 4.4 %collective-permute-start.11 = (bf16[4,32,1920]{2,1,0:T(8,128)(2,1)S(1)}, bf16[4,32,1920]{2,1,0:T(8,128)(2,1)S(1)}, u32[]{:S(2)}, u32[]{:S(2)}) collective-permute-start(bf16[4,32,1920]{2,1,0:T(8,128)(2,1)S(1)} %collective-permute-done.6.x.rest_1_), channel_id=1, source_target_pairs={{0,1},{1,0},{2,3},{3,2},{4,5},{5,4},{6,7},{7,6},{8,9},{9,8},{10,11... | collective-permute-start | bytes 1474568 | tf_op jit(solution)/shard_map/ppermute | solution.py:98
  53.1 5.3 %collective-permute-done.9.rest_4_ = bf16[2,32,1920]{2,1,0:T(8,128)(2,1)} collective-permute-done((bf16[2,32,1920]{2,1,0:T(8,128)(2,1)S(1)}, bf16[2,32,1920]{2,1,0:T(8,128)(2,1)}, u32[]{:S(2)}, u32[]{:S(2)}) %collective-permute-start.9) | collective-permute-done | bytes 245792 | tf_op jit(solution)/shard_map/ppermute | solution.py:98
  71.6 11.6 %shard_map.276 = (bf16[512,1024]{1,0:T(8,128)(2,1)S(1)}, bf16[512,1024]{1,0:T(8,128)(2,1)S(1)}, bf16[512,256]{1,0:T(8,128)(2,1)S(1)}, bf16[512,256]{1,0:T(8,128)...) custom-call(s32[2]{0:T(128)S(1)} %pad_add_fusion.br, ...), custom_call_target="tpu_custom_call" | custom-call | flops 3355443200 | bytes 25702408 | tf_op jit(solution)/shard_map/pallas_call | solution.py:44
  83.3 3.9 %collective-permute-done.26.g3 = bf16[128,1024]{1,0:T(8,128)(2,1)S(1)} collective-permute-done((bf16[128,1024]{1,0:T(8,128)(2,1)}, bf16[128,1024]{1,0:T(8,128)(2,1)S(1)}, u32[]{:S(2)}, u32[]{:S(2)}) %collective-permute-start.26) | collective-permute-done | bytes 262176 | tf_op jit(solution)/shard_map/ppermute | solution.py:95
  87.2 7.7 %shard_map.279 = (bf16[512,1024]{1,0:T(8,128)(2,1)S(1)}, bf16[512,768]{1,0:T(8,128)(2,1)S(1)}, bf16[512,1024]{1,0:T(8,128)(2,1)S(1)}, f32[4,128,1792]{2,1,0:T(8,...) custom-call(s32[2]{0:T(128)S(1)} %pad_add_fusion.br, ...), custom_call_target="tpu_custom_call" | custom-call | flops 3489660928 | bytes 18621448 | tf_op jit(solution)/shard_map/pallas_call | solution.py:44
  96.0 2.4 %shard_map.286 = (f32[4,160,1024]{2,1,0:T(8,128)S(1)}, bf16[4,160,1024]{2,1,0:T(8,128)(2,1)S(1)}) custom-call(s32[2]{0:T(128)S(1)} %pad_add_fusion.br, bf16[512,1024]{1,0:T(8,128)(2,1)S(1)} %get-tuple-element.110.grad, bf16[512,1024]{1,0:T(8,128)(2,1)S(1)} %get-tuple-element.136.hidden, bf16[512,256]{1,0:T(8,128)(2,1)S(1)} %get-tuple-element.137.mixed), custom_call_target="tpu_custom_call" | custom-call | flops 1342177280 | bytes 6291464 | tf_op jit(solution)/shard_map/pallas_call | solution.py:44
  98.6 4.0 %shard_map.280 = (f32[128,1024]{1,0:T(8,128)S(1)}, f32[4,8,384]{2,1,0:T(8,128)S(1)}, bf16[4,8,384]{2,1,0:T(8,128)(2,1)S(1)}, bf16[256,1024]{1,0:T(8,128)(2,1)S(1)}, f32[128,1024]{1,0:T(8,128)S(1)}) custom-call(s32[2]{0:T(128)S(1)} %pad_add_fusion.br, f32[512,1024]{1,0:T(8,128)S(1)} %get-tuple-element.111.xhat, ...), custom_call_target="tpu_custom_call" | custom-call | flops 1879048192 | bytes 10312712 | tf_op jit(solution)/shard_map/pallas_call | solution.py:44
  109.3 2.4 %collective-permute-done.22.got.p1 = bf16[256,1024]{1,0:T(8,128)(2,1)S(1)} collective-permute-done((bf16[256,1024]{1,0:T(8,128)(2,1)S(1)}, bf16[256,1024]{1,0:T(8,128)(2,1)S(1)}, u32[]{:S(2)}, u32[]{:S(2)}) %collective-permute-start.22) | collective-permute-done | bytes 524320 | tf_op jit(solution)/shard_map/ppermute | solution.py:95
  113.1 9.8 %collective-permute-done.27.got.rest_0_ = bf16[256,1024]{1,0:T(8,128)(2,1)S(1)} collective-permute-done((bf16[256,1024]{1,0:T(8,128)(2,1)S(1)}, bf16[256,1024]{1,0:T(8,128)(2,1)S(1)}, u32[]{:S(2)}, u32[]{:S(2)}) %collective-permute-start.27) | collective-permute-done | bytes 524320 | tf_op jit(solution)/shard_map/ppermute | solution.py:95
  125.4 4.2 %collective-permute-done.32.rest_2_ = bf16[136,1792]{1,0:T(8,128)(2,1)S(1)} collective-permute-done((bf16[136,1792]{1,0:T(8,128)(2,1)S(1)}, bf16[136,1792]{1,0:T(8,128)(2,1)S(1)}, u32[]{:S(2)}, u32[]{:S(2)}) %collective-permute-start.32) | collective-permute-done | bytes 487456 | tf_op jit(solution)/shard_map/ppermute | solution.py:98
  132.4 7.1 %collective-permute-done.23.p2 = bf16[128,1024]{1,0:T(8,128)(2,1)S(1)} collective-permute-done((bf16[128,1024]{1,0:T(8,128)(2,1)S(1)}, bf16[128,1024]{1,0:T(8,128)(2,1)S(1)}, u32[]{:S(2)}, u32[]{:S(2)}) %collective-permute-start.23) | collective-permute-done | bytes 262176 | tf_op jit(solution)/shard_map/ppermute | solution.py:95
  139.5 3.2 %collective-permute-start.34 = (bf16[40,1792]{1,0:T(8,128)(2,1)S(1)}, bf16[40,1792]{1,0:T(8,128)(2,1)S(1)}, u32[]{:S(2)}, u32[]{:S(2)}) collective-permute-start(bf16[40,1792]{1,0:T(8,128)(2,1)S(1)} %get-tuple-element.131), channel_id=1, source_target_pairs={{0,8},{1,9},{2,10},{3,11},{4,12},{5,13},{6,14},{7,15},{8,0},{9,1},... | collective-permute-start | bytes 430088 | tf_op jit(solution)/shard_map/ppermute | solution.py:95
  142.7 2.5 %collective-permute-done.28.rest_1_ = bf16[128,1024]{1,0:T(8,128)(2,1)S(1)} collective-permute-done((bf16[128,1024]{1,0:T(8,128)(2,1)S(1)}, bf16[128,1024]{1,0:T(8,128)(2,1)S(1)}, u32[]{:S(2)}, u32[]{:S(2)}) %collective-permute-start.28) | collective-permute-done | bytes 262176 | tf_op jit(solution)/shard_map/ppermute | solution.py:95
  145.2 3.1 %collective-permute-start.35 = (bf16[40,1792]{1,0:T(8,128)(2,1)S(1)}, bf16[40,1792]{1,0:T(8,128)(2,1)S(1)}, u32[]{:S(2)}, u32[]{:S(2)}) collective-permute-start(bf16[40,1792]{1,0:T(8,128)(2,1)S(1)} %get-tuple-element.132), channel_id=1, source_target_pairs={{0,16},{1,17},{2,18},{3,19},{4,20},{5,21},{6,22},{7,23},{8,24},{9,... | collective-permute-start | bytes 430088 | tf_op jit(solution)/shard_map/ppermute | solution.py:95
  152.5 5.2 %collective-permute-done.35.rest_2_ = bf16[40,1792]{1,0:T(8,128)(2,1)S(1)} collective-permute-done((bf16[40,1792]{1,0:T(8,128)(2,1)S(1)}, bf16[40,1792]{1,0:T(8,128)(2,1)S(1)}, u32[]{:S(2)}, u32[]{:S(2)}) %collective-permute-start.35) | collective-permute-done | bytes 143392 | tf_op jit(solution)/shard_map/ppermute | solution.py:95
  157.7 4.0 %collective-permute-done.36.rest_3_ = bf16[40,1792]{1,0:T(8,128)(2,1)S(1)} collective-permute-done((bf16[40,1792]{1,0:T(8,128)(2,1)S(1)}, bf16[40,1792]{1,0:T(8,128)(2,1)S(1)}, u32[]{:S(2)}, u32[]{:S(2)}) %collective-permute-start.36) | collective-permute-done | bytes 143392 | tf_op jit(solution)/shard_map/ppermute | solution.py:95
  (118 shorter events, 53.0 us)
Async XLA Ops:
  2.9 16.2 %collective-permute-start.15 = (bf16[160,1024]{1,0:T(8,128)(2,1)}, bf16[160,1024]{1,0:T(8,128)(2,1)S(1)}, u32[]{:S(2)}, u32[]{:S(2)}) collective-permute-start(bf16[160,1024]{1,0:T(8,128)(2,1)} %get-tuple-element.95.rest_10_), channel_id=1, source_target_pairs={{0,2},{1,3},{2,0},{3,1},{4,6},{5,7},{6,4},{7,5},{8,10},{9,11},{10,... | collective-permute-start | bytes 983048 | tf_op jit(solution)/shard_map/ppermute | solution.py:98
  6.7 14.7 %collective-permute-start.16 = (bf16[160,1024]{1,0:T(8,128)(2,1)}, bf16[160,1024]{1,0:T(8,128)(2,1)S(1)}, u32[]{:S(2)}, u32[]{:S(2)}) collective-permute-start(bf16[160,1024]{1,0:T(8,128)(2,1)} %get-tuple-element.95.rest_10_), channel_id=1, source_target_pairs={{0,4},{1,5},{2,6},{3,7},{4,0},{5,1},{6,2},{7,3},{8,12},{9,13},{10,... | collective-permute-start | bytes 983048 | tf_op jit(solution)/shard_map/ppermute | solution.py:98
  8.3 15.9 %collective-permute-start.17 = (bf16[160,1024]{1,0:T(8,128)(2,1)}, bf16[160,1024]{1,0:T(8,128)(2,1)}, u32[]{:S(2)}, u32[]{:S(2)}) collective-permute-start(bf16[160,1024]{1,0:T(8,128)(2,1)} %get-tuple-element.95.rest_10_), channel_id=1, source_target_pairs={{0,6},{1,7},{2,4},{3,5},{4,2},{5,3},{6,0},{7,1},{8,14},{9,15},{10,... | collective-permute-start | bytes 983048 | tf_op jit(solution)/shard_map/ppermute | solution.py:98
  18.5 17.8 %collective-permute-start.6 = (bf16[4,32,1920]{2,1,0:T(8,128)(2,1)S(1)}, bf16[4,32,1920]{2,1,0:T(8,128)(2,1)S(1)}, u32[]{:S(2)}, u32[]{:S(2)}) collective-permute-start(bf16[4,32,1920]{2,1,0:T(8,128)(2,1)S(1)} %shard_map.274.rest_0_), channel_id=1, source_target_pairs={{0,2},{1,3},{2,0},{3,1},{4,6},{5,7},{6,4},{7,5},{8,10},{9,11},{10,... | collective-permute-start | bytes 1474568 | tf_op jit(solution)/shard_map/ppermute | solution.py:98
  18.8 17.5 %collective-permute-start.7 = (bf16[4,32,1920]{2,1,0:T(8,128)(2,1)S(1)}, bf16[4,32,1920]{2,1,0:T(8,128)(2,1)S(1)}, u32[]{:S(2)}, u32[]{:S(2)}) collective-permute-start(bf16[4,32,1920]{2,1,0:T(8,128)(2,1)S(1)} %shard_map.274.rest_0_), channel_id=1, source_target_pairs={{0,4},{1,5},{2,6},{3,7},{4,0},{5,1},{6,2},{7,3},{8,12},{9,13},{10,... | collective-permute-start | bytes 1474568 | tf_op jit(solution)/shard_map/ppermute | solution.py:98
  24.3 18.7 %collective-permute-start.10 = (bf16[4,32,1920]{2,1,0:T(8,128)(2,1)S(1)}, bf16[4,32,1920]{2,1,0:T(8,128)(2,1)S(1)}, u32[]{:S(2)}, u32[]{:S(2)}) collective-permute-start(bf16[4,32,1920]{2,1,0:T(8,128)(2,1)S(1)} %shard_map.274.rest_0_), channel_id=1, source_target_pairs={{0,1},{1,0},{2,3},{3,2},{4,5},{5,4},{6,7},{7,6},{8,9},{9,8},{10,11... | collective-permute-start | bytes 1474568 | tf_op jit(solution)/shard_map/ppermute | solution.py:98
  29.8 20.2 %collective-permute-start.19 = (bf16[160,1024]{1,0:T(8,128)(2,1)S(1)}, bf16[160,1024]{1,0:T(8,128)(2,1)S(1)}, u32[]{:S(2)}, u32[]{:S(2)}) collective-permute-start(bf16[160,1024]{1,0:T(8,128)(2,1)S(1)} %collective-permute-done.15.rest_11_), channel_id=1, source_target_pairs={{0,1},{1,0},{2,3},{3,2},{4,5},{5,4},{6,7},{7,6},{8,9},{9,8},{10,11... | collective-permute-start | bytes 983048 | tf_op jit(solution)/shard_map/ppermute | solution.py:98
  36.3 14.4 %collective-permute-start.20 = (bf16[160,1024]{1,0:T(8,128)(2,1)S(1)}, bf16[160,1024]{1,0:T(8,128)(2,1)S(1)}, u32[]{:S(2)}, u32[]{:S(2)}) collective-permute-start(bf16[160,1024]{1,0:T(8,128)(2,1)S(1)} %collective-permute-done.16.rest_12_), channel_id=1, source_target_pairs={{0,1},{1,0},{2,3},{3,2},{4,5},{5,4},{6,7},{7,6},{8,9},{9,8},{10,11... | collective-permute-start | bytes 983048 | tf_op jit(solution)/shard_map/ppermute | solution.py:98
  43.0 19.6 %collective-permute-start.11 = (bf16[4,32,1920]{2,1,0:T(8,128)(2,1)S(1)}, bf16[4,32,1920]{2,1,0:T(8,128)(2,1)S(1)}, u32[]{:S(2)}, u32[]{:S(2)}) collective-permute-start(bf16[4,32,1920]{2,1,0:T(8,128)(2,1)S(1)} %collective-permute-done.6.x.rest_1_), channel_id=1, source_target_pairs={{0,1},{1,0},{2,3},{3,2},{4,5},{5,4},{6,7},{7,6},{8,9},{9,8},{10,11... | collective-permute-start | bytes 1474568 | tf_op jit(solution)/shard_map/ppermute | solution.py:98
  48.1 14.6 %collective-permute-start.12 = (bf16[4,32,1920]{2,1,0:T(8,128)(2,1)S(1)}, bf16[4,32,1920]{2,1,0:T(8,128)(2,1)S(1)}, u32[]{:S(2)}, u32[]{:S(2)}) collective-permute-start(bf16[4,32,1920]{2,1,0:T(8,128)(2,1)S(1)} %collective-permute-done.7.y.rest_2_), channel_id=1, source_target_pairs={{0,1},{1,0},{2,3},{3,2},{4,5},{5,4},{6,7},{7,6},{8,9},{9,8},{10,11... | collective-permute-start | bytes 1474568 | tf_op jit(solution)/shard_map/ppermute | solution.py:98
  61.1 22.2 %collective-permute-start.24 = (bf16[128,1024]{1,0:T(8,128)(2,1)}, bf16[128,1024]{1,0:T(8,128)(2,1)S(1)}, u32[]{:S(2)}, u32[]{:S(2)}) collective-permute-start(bf16[128,1024]{1,0:T(8,128)(2,1)} %g0.1), channel_id=1, source_target_pairs={{0,8},{1,9},{2,10},{3,11},{4,12},{5,13},{6,14},{7,15},{8,0},{9,1},... | collective-permute-start | bytes 786440 | tf_op jit(solution)/shard_map/ppermute | solution.py:95
  62.6 20.7 %collective-permute-start.25 = (bf16[128,1024]{1,0:T(8,128)(2,1)}, bf16[128,1024]{1,0:T(8,128)(2,1)S(1)}, u32[]{:S(2)}, u32[]{:S(2)}) collective-permute-start(bf16[128,1024]{1,0:T(8,128)(2,1)} %g0.1), channel_id=1, source_target_pairs={{0,16},{1,17},{2,18},{3,19},{4,20},{5,21},{6,22},{7,23},{8,24},{9,... | collective-permute-start | bytes 786440 | tf_op jit(solution)/shard_map/ppermute | solution.py:95
  62.6 24.6 %collective-permute-start.26 = (bf16[128,1024]{1,0:T(8,128)(2,1)}, bf16[128,1024]{1,0:T(8,128)(2,1)S(1)}, u32[]{:S(2)}, u32[]{:S(2)}) collective-permute-start(bf16[128,1024]{1,0:T(8,128)(2,1)} %g0.1), channel_id=1, source_target_pairs={{0,24},{1,25},{2,26},{3,27},{4,28},{5,29},{6,30},{7,31},{8,16},{9,... | collective-permute-start | bytes 786440 | tf_op jit(solution)/shard_map/ppermute | solution.py:95
  98.6 13.1 %collective-permute-start.22 = (bf16[256,1024]{1,0:T(8,128)(2,1)S(1)}, bf16[256,1024]{1,0:T(8,128)(2,1)S(1)}, u32[]{:S(2)}, u32[]{:S(2)}) collective-permute-start(bf16[256,1024]{1,0:T(8,128)(2,1)S(1)} %get-tuple-element.98), channel_id=1, source_target_pairs={{0,8},{1,9},{2,10},{3,11},{4,12},{5,13},{6,14},{7,15},{8,0},{9,1},... | collective-permute-start | bytes 1572872 | tf_op jit(solution)/shard_map/ppermute | solution.py:95
  102.7 20.2 %collective-permute-start.27 = (bf16[256,1024]{1,0:T(8,128)(2,1)S(1)}, bf16[256,1024]{1,0:T(8,128)(2,1)S(1)}, u32[]{:S(2)}, u32[]{:S(2)}) collective-permute-start(bf16[256,1024]{1,0:T(8,128)(2,1)S(1)} %get-tuple-element.120), channel_id=1, source_target_pairs={{0,8},{1,9},{2,10},{3,11},{4,12},{5,13},{6,14},{7,15},{8,0},{9,1},... | collective-permute-start | bytes 1572872 | tf_op jit(solution)/shard_map/ppermute | solution.py:95
  106.3 16.9 %collective-permute-start.31 = (bf16[136,1792]{1,0:T(8,128)(2,1)S(1)}, bf16[136,1792]{1,0:T(8,128)(2,1)S(1)}, u32[]{:S(2)}, u32[]{:S(2)}) collective-permute-start(bf16[136,1792]{1,0:T(8,128)(2,1)S(1)} %get-tuple-element.127), channel_id=1, source_target_pairs={{0,2},{1,3},{2,0},{3,1},{4,6},{5,7},{6,4},{7,5},{8,10},{9,11},{10,... | collective-permute-start | bytes 1462280 | tf_op jit(solution)/shard_map/ppermute | solution.py:98
  107.8 21.8 %collective-permute-start.32 = (bf16[136,1792]{1,0:T(8,128)(2,1)S(1)}, bf16[136,1792]{1,0:T(8,128)(2,1)S(1)}, u32[]{:S(2)}, u32[]{:S(2)}) collective-permute-start(bf16[136,1792]{1,0:T(8,128)(2,1)S(1)} %get-tuple-element.128), channel_id=1, source_target_pairs={{0,4},{1,5},{2,6},{3,7},{4,0},{5,1},{6,2},{7,3},{8,12},{9,13},{10,... | collective-permute-start | bytes 1462280 | tf_op jit(solution)/shard_map/ppermute | solution.py:98
  107.8 21.8 %collective-permute-start.33 = (bf16[136,1792]{1,0:T(8,128)(2,1)S(1)}, bf16[136,1792]{1,0:T(8,128)(2,1)S(1)}, u32[]{:S(2)}, u32[]{:S(2)}) collective-permute-start(bf16[136,1792]{1,0:T(8,128)(2,1)S(1)} %get-tuple-element.129), channel_id=1, source_target_pairs={{0,6},{1,7},{2,4},{3,5},{4,2},{5,3},{6,0},{7,1},{8,14},{9,15},{10,... | collective-permute-start | bytes 1462280 | tf_op jit(solution)/shard_map/ppermute | solution.py:98
  111.7 36.6 %collective-permute-start.38 = (bf16[160,1024]{1,0:T(8,128)(2,1)S(1)}, bf16[160,1024]{1,0:T(8,128)(2,1)S(1)}, u32[]{:S(2)}, u32[]{:S(2)}) collective-permute-start(bf16[160,1024]{1,0:T(8,128)(2,1)S(1)} %get-tuple-element.141), channel_id=1, source_target_pairs={{0,2},{1,3},{2,0},{3,1},{4,6},{5,7},{6,4},{7,5},{8,10},{9,11},{10,... | collective-permute-start | bytes 983048 | tf_op jit(solution)/shard_map/ppermute | solution.py:98
  122.9 16.6 %collective-permute-start.23 = (bf16[128,1024]{1,0:T(8,128)(2,1)S(1)}, bf16[128,1024]{1,0:T(8,128)(2,1)S(1)}, u32[]{:S(2)}, u32[]{:S(2)}) collective-permute-start(bf16[128,1024]{1,0:T(8,128)(2,1)S(1)} %shard_map.277), channel_id=1, source_target_pairs={{0,16},{1,17},{2,18},{3,19},{4,20},{5,21},{6,22},{7,23},{8,24},{9,... | collective-permute-start | bytes 786440 | tf_op jit(solution)/shard_map/ppermute | solution.py:95
  123.2 21.9 %collective-permute-start.28 = (bf16[128,1024]{1,0:T(8,128)(2,1)S(1)}, bf16[128,1024]{1,0:T(8,128)(2,1)S(1)}, u32[]{:S(2)}, u32[]{:S(2)}) collective-permute-start(bf16[128,1024]{1,0:T(8,128)(2,1)S(1)} %shard_map.281), channel_id=1, source_target_pairs={{0,16},{1,17},{2,18},{3,19},{4,20},{5,21},{6,22},{7,23},{8,24},{9,... | collective-permute-start | bytes 786440 | tf_op jit(solution)/shard_map/ppermute | solution.py:95
  129.6 21.9 %collective-permute-start.39 = (bf16[160,1024]{1,0:T(8,128)(2,1)S(1)}, bf16[160,1024]{1,0:T(8,128)(2,1)S(1)}, u32[]{:S(2)}, u32[]{:S(2)}) collective-permute-start(bf16[160,1024]{1,0:T(8,128)(2,1)S(1)} %get-tuple-element.142), channel_id=1, source_target_pairs={{0,4},{1,5},{2,6},{3,7},{4,0},{5,1},{6,2},{7,3},{8,12},{9,13},{10,... | collective-permute-start | bytes 983048 | tf_op jit(solution)/shard_map/ppermute | solution.py:98
  129.6 21.9 %collective-permute-start.40 = (bf16[160,1024]{1,0:T(8,128)(2,1)S(1)}, bf16[160,1024]{1,0:T(8,128)(2,1)S(1)}, u32[]{:S(2)}, u32[]{:S(2)}) collective-permute-start(bf16[160,1024]{1,0:T(8,128)(2,1)S(1)} %get-tuple-element.143), channel_id=1, source_target_pairs={{0,6},{1,7},{2,4},{3,5},{4,2},{5,3},{6,0},{7,1},{8,14},{9,15},{10,... | collective-permute-start | bytes 983048 | tf_op jit(solution)/shard_map/ppermute | solution.py:98
  148.3 13.4 %collective-permute-start.36 = (bf16[40,1792]{1,0:T(8,128)(2,1)S(1)}, bf16[40,1792]{1,0:T(8,128)(2,1)S(1)}, u32[]{:S(2)}, u32[]{:S(2)}) collective-permute-start(bf16[40,1792]{1,0:T(8,128)(2,1)S(1)} %get-tuple-element.133), channel_id=1, source_target_pairs={{0,24},{1,25},{2,26},{3,27},{4,28},{5,29},{6,30},{7,31},{8,16},{9,... | collective-permute-start | bytes 430088 | tf_op jit(solution)/shard_map/ppermute | solution.py:95
  (38 other events, 482.5 us)
